TPU v7x, 32 devices: a whole 2x2x4 slice. The times are simulated.
32 devices in a mesh: ctx: 16 (over z, y, x), tp: 2 (over core).
Axes of the slice: x: 2, y: 2, z: 4, core: 2. Of those that a mesh axis runs over, the one named last changes fastest.
Arguments:
- queries: bfloat16 [3072, 32, 128], P('ctx', 'tp'), may hold values from -6 to 6
- key_vectors: bfloat16 [3072, 4, 128], P('ctx', 'tp'), may hold values from -6 to 6
- value_matrix: bfloat16 [3072, 4, 128], P('ctx', 'tp'), may hold values from -6 to 6
- grad_out: bfloat16 [3072, 32, 128], P('ctx', 'tp'), may hold values from -6 to 6
- doc_lengths: int32 [8], replicated, may hold values from 1 to 1345, 3072 in all
Outputs:
- grad_queries: bfloat16 [3072, 32, 128], P('ctx', 'tp')
- grad_keys: bfloat16 [3072, 4, 128], P('ctx', 'tp')
- grad_values: bfloat16 [3072, 4, 128], P('ctx', 'tp')
Inputs may be any that keep to these rules, and one draw needn't show every extreme that they name: `doc_lengths`: 8 document lengths that sum to 3072; the longest is exactly 1345.
All inputs are finite; a program needn't handle non-finite values.
Results may differ from a plain program's by a relative error of at most 0.0079.
Values may be sent and summed in bfloat16 or wider, within the bound.
No kernel may reach another device: no remote copies, remote signals or barrier semaphores. Data moves between devices by JAX's collectives and lax.ppermute only.
A program may use at most 64 MiB of HBM per device.

v0:
```python
import jax
import jax.numpy as jnp
from jax import lax
from jax.sharding import PartitionSpec as P

SPAN_LOG = 3
WIN = 8
KBLOCK = 512


neg_fill = -1e30


def shifted(array, axis, by):
    length = lax.axis_size(axis)
    pairs = [(i, i + by) for i in range(length) if 0 <= i + by < length]
    return lax.ppermute(array, axis, pairs)


def doc_index(positions, lengths):
    doc_ends = jnp.cumsum(lengths)
    return jnp.sum((positions[:, None] >= doc_ends[None, :]).astype(jnp.int32), axis=1)


def fetch_window(stacked):
    window = stacked[None]
    for section_no in range(SPAN_LOG):
        arrived = shifted(window, "ctx", 2**section_no)
        window = jnp.concatenate([arrived, window], axis=0)
    return window


def return_window(partials):
    by_offset = partials[::-1]
    for section_no in range(SPAN_LOG - 1, -1, -1):
        stride = 2**section_no
        arrived = shifted(by_offset[stride:], "ctx", -stride)
        by_offset = by_offset[:stride] + arrived
    return by_offset[0]


def shards(queries, key_vectors, value_matrix, grad_out, doc_lengths):
    stripe = queries.shape[0]
    local_heads = queries.shape[1]
    head_dim = queries.shape[2]
    softmax_scale = head_dim ** (-0.5)
    stacked = jnp.stack([key_vectors, value_matrix], axis=1)
    window = fetch_window(stacked)
    head_groups = window.shape[3]
    repeat_factor = local_heads // head_groups
    key_span = window.shape[0] * stripe
    block_count = key_span // KBLOCK
    key_blocks = window[:, :, 0].reshape(block_count, KBLOCK, head_groups, head_dim)
    value_blocks = window[:, :, 1].reshape(block_count, KBLOCK, head_groups, head_dim)
    query_rows = queries.reshape(stripe, head_groups, repeat_factor, head_dim)
    grad_rows = grad_out.reshape(stripe, head_groups, repeat_factor, head_dim)
    ctx_index = lax.axis_index("ctx")
    query_pos = ctx_index * stripe + jnp.arange(stripe, dtype=jnp.int32)
    query_doc = doc_index(query_pos, doc_lengths)
    window_start = (ctx_index - (WIN - 1)) * stripe
    numbers = jnp.arange(block_count, dtype=jnp.int32)
    stats_shape = (head_groups, repeat_factor, stripe)

    def live_mask(number):
        key_pos = window_start + number * KBLOCK + jnp.arange(KBLOCK, dtype=jnp.int32)
        key_doc = doc_index(key_pos, doc_lengths)
        causal = (key_pos[None, :] <= query_pos[:, None]) & (key_pos[None, :] >= 0)
        return causal & (key_doc[None, :] == query_doc[:, None])

    def logits_of(key_block, live_pairs):
        raw_scores = (
            jnp.einsum("qgrd,kgd->grqk", query_rows, key_block, preferred_element_type=jnp.float32)
            * softmax_scale
        )
        return jnp.where(live_pairs, raw_scores, neg_fill)

    def max_step(carried, inputs):
        run_max, run_sum = carried
        key_block, number = inputs
        live_pairs = live_mask(number)
        logits = logits_of(key_block, live_pairs)
        new_max = jnp.maximum(run_max, jnp.max(logits, axis=-1))
        weights = jnp.where(live_pairs, jnp.exp(logits - new_max[..., None]), 0.0)
        return ((new_max, run_sum * jnp.exp(run_max - new_max) + jnp.sum(weights, axis=-1)), None)

    start_stats = (
        jnp.full(stats_shape, neg_fill, jnp.float32),
        jnp.zeros(stats_shape, jnp.float32),
    )
    (run_max, run_sum), unused = lax.scan(max_step, start_stats, (key_blocks, numbers))
    log_total = run_max + jnp.log(run_sum)

    def probs_of(key_block, live_pairs):
        return jnp.where(
            live_pairs, jnp.exp(logits_of(key_block, live_pairs) - log_total[..., None]), 0.0
        )

    def delta_step(carried, inputs):
        key_block, value_block, number = inputs
        live_pairs = live_mask(number)
        probs = probs_of(key_block, live_pairs)
        grad_probs = jnp.einsum(
            "qgrd,kgd->grqk", grad_rows, value_block, preferred_element_type=jnp.float32
        )
        return (carried + jnp.sum(probs * grad_probs, axis=-1), None)

    row_dots, unused = lax.scan(
        delta_step, jnp.zeros(stats_shape, jnp.float32), (key_blocks, value_blocks, numbers)
    )

    def grad_step(carried, inputs):
        key_block, value_block, number = inputs
        live_pairs = live_mask(number)
        probs = probs_of(key_block, live_pairs)
        grad_probs = jnp.einsum(
            "qgrd,kgd->grqk", grad_rows, value_block, preferred_element_type=jnp.float32
        )
        grad_scores = (probs * (grad_probs - row_dots[..., None])).astype(jnp.bfloat16)
        probs_low = probs.astype(jnp.bfloat16)
        query_grad = carried + jnp.einsum(
            "grqk,kgd->qgrd", grad_scores, key_block, preferred_element_type=jnp.float32
        )
        key_grad = (
            jnp.einsum(
                "grqk,qgrd->kgd", grad_scores, query_rows, preferred_element_type=jnp.float32
            )
            * softmax_scale
        )
        value_grad = jnp.einsum(
            "grqk,qgrd->kgd", probs_low, grad_rows, preferred_element_type=jnp.float32
        )
        return (query_grad, jnp.stack([key_grad, value_grad], axis=1))

    start_grad = jnp.zeros((stripe, head_groups, repeat_factor, head_dim), jnp.float32)
    query_grad, block_grads = lax.scan(grad_step, start_grad, (key_blocks, value_blocks, numbers))
    kv_partials = block_grads.reshape(window.shape[0], stripe, 2, head_groups, head_dim)
    owned = return_window(kv_partials)
    query_out = (
        (query_grad * softmax_scale).reshape(stripe, local_heads, head_dim).astype(jnp.bfloat16)
    )
    return (query_out, owned[:, 0].astype(jnp.bfloat16), owned[:, 1].astype(jnp.bfloat16))


def solution(mesh):
    in_specs = (
        P("ctx", "tp", None),
        P("ctx", "tp", None),
        P("ctx", "tp", None),
        P("ctx", "tp", None),
        P(),
    )
    out_specs = (P("ctx", "tp", None), P("ctx", "tp", None), P("ctx", "tp", None))
    return jax.shard_map(shards, mesh=mesh, in_specs=in_specs, out_specs=out_specs, check_vma=False)
```

profile of v0, /device:TPU:16, one launch (start us, length us, event | category | flops | bytes accessed | tf_op | source)
XLA Modules:
  0.0 190.4 jit_solution(11996719150093022145)
XLA Ops:
  1.6 3.4 %collective-permute-start = (bf16[1,192,2,2,128]{4,1,0,3,2:T(8,128)(2,1)S(1)}, bf16[1,192,2,2,128]{4,1,0,3,2:T(8,128)(2,1)S(1)}, u32[]{:S(2)}, u32[]{:S(2)}) collective-permute-start(bf16[1,192,2,2,128]{4,1,0,3,2:T(8,128)(2,1)S(1)} %maximum_bitcast_fusion.1), channel_id=1, source_target_pairs={{0,2},{2,4},{4,6},{6,8},{8,10},{10,12},{12,14},{14,16},{16,18},{18... | collective-permute-start | bytes 589832 | tf_op jit(solution)/shard_map/ppermute | solution.py:17
  5.0 6.9 %collective-permute-done = bf16[1,192,2,2,128]{4,1,0,3,2:T(8,128)(2,1)S(1)} collective-permute-done((bf16[1,192,2,2,128]{4,1,0,3,2:T(8,128)(2,1)S(1)}, bf16[1,192,2,2,128]{4,1,0,3,2:T(8,128)(2,1)S(1)}, u32[]{:S(2)}, u32[]{:S(2)}) %collective-permute-start) | collective-permute-done | bytes 196640 | tf_op jit(solution)/shard_map/ppermute | solution.py:17
  12.0 2.5 %collective-permute-start.1 = (bf16[2,192,2,2,128]{4,1,0,3,2:T(8,128)(2,1)S(1)}, bf16[2,192,2,2,128]{4,1,0,3,2:T(8,128)(2,1)S(1)}, u32[]{:S(2)}, u32[]{:S(2)}) collective-permute-start(bf16[2,192,2,2,128]{4,1,0,3,2:T(8,128)(2,1)S(1)} %pad_maximum_fusion.2), channel_id=1, source_target_pairs={{0,4},{2,6},{4,8},{6,10},{8,12},{10,14},{12,16},{14,18},{16,20},{1... | collective-permute-start | bytes 1179656 | tf_op jit(solution)/shard_map/ppermute | solution.py:17
  14.5 10.3 %collective-permute-done.1 = bf16[2,192,2,2,128]{4,1,0,3,2:T(8,128)(2,1)S(1)} collective-permute-done((bf16[2,192,2,2,128]{4,1,0,3,2:T(8,128)(2,1)S(1)}, bf16[2,192,2,2,128]{4,1,0,3,2:T(8,128)(2,1)S(1)}, u32[]{:S(2)}, u32[]{:S(2)}) %collective-permute-start.1) | collective-permute-done | bytes 393248 | tf_op jit(solution)/shard_map/ppermute | solution.py:17
  25.8 3.5 %collective-permute-start.2 = (bf16[4,192,2,2,128]{4,1,0,3,2:T(8,128)(2,1)}, bf16[4,192,2,2,128]{4,1,0,3,2:T(8,128)(2,1)}, u32[]{:S(2)}, u32[]{:S(2)}) collective-permute-start(bf16[4,192,2,2,128]{4,1,0,3,2:T(8,128)(2,1)} %pad_maximum_fusion.1), channel_id=1, source_target_pairs={{0,8},{2,10},{4,12},{6,14},{8,16},{10,18},{12,20},{14,22},{16,24},... | collective-permute-start | bytes 2359304 | tf_op jit(solution)/shard_map/ppermute | solution.py:17
  30.1 1.3 copy.26
  31.5 2.2 %copy.28 = bf16[192,16,128]{2,0,1:T(8,128)(2,1)} copy(bf16[192,16,128]{2,1,0:T(8,128)(2,1)} %param.14) | data formatting | bytes 1572864 | tf_op args[3]
  33.8 11.7 %collective-permute-done.2 = bf16[4,192,2,2,128]{4,1,0,3,2:T(8,128)(2,1)} collective-permute-done((bf16[4,192,2,2,128]{4,1,0,3,2:T(8,128)(2,1)}, bf16[4,192,2,2,128]{4,1,0,3,2:T(8,128)(2,1)}, u32[]{:S(2)}, u32[]{:S(2)}) %collective-permute-start.2) | collective-permute-done | bytes 786464 | tf_op jit(solution)/shard_map/ppermute | solution.py:17
  45.5 1.4 pad_maximum_fusion
  48.0 14.7 %while.43 = (s32[]{:T(128)}, f32[2,8,192]{2,1,0:T(8,128)S(1)}, f32[2,8,192]{2,1,0:T(8,128)S(1)}, s32[3]{0:T(128)S(1)}, s32[]{:T(128)}, /*index=5*/s32[1,8]{1,0:T...) while((s32[]{:T(128)}, f32[2,8,192]{2,1,0:T(8,128)S(1)}, ...), condition=%wide.region_6.7_spmd.clone, body=%wide.region_2.6_spmd.clone.sunk | while | flops 415658176 | bytes 14099940 | solution.py:90
  49.6 1.2 fusion.89
  50.8 2.1 %select_reduce_fusion.2 = f32[2,8,192]{2,1,0:T(8,128)S(1)} fusion(f32[2,512,192,8]{1,2,3,0:T(8,128)S(1)} %get-tuple-element.906, f32[2,8,192]{2,1,0:T(8,128)S(1)} %select_maximum_fusion.2, pred[192,512]{1,0:T(8,128)(4,1)S(1)} %compare_and_fusion.6), kind=kLoop, calls=%fused_computation.4.clone.1 | loop fusion | flops 7861248 | bytes 6414336 | tf_op jit(solution)/shard_map/while/body/eval_jaxpr/reduce_sum | solution.py:84
  54.5 1.2 fusion.89
  55.7 2.1 %select_reduce_fusion.2 = f32[2,8,192]{2,1,0:T(8,128)S(1)} fusion(f32[2,512,192,8]{1,2,3,0:T(8,128)S(1)} %get-tuple-element.906, f32[2,8,192]{2,1,0:T(8,128)S(1)} %select_maximum_fusion.2, pred[192,512]{1,0:T(8,128)(4,1)S(1)} %compare_and_fusion.6), kind=kLoop, calls=%fused_computation.4.clone.1 | loop fusion | flops 7861248 | bytes 6414336 | tf_op jit(solution)/shard_map/while/body/eval_jaxpr/reduce_sum | solution.py:84
  59.4 1.2 fusion.89
  60.6 2.1 %select_reduce_fusion.2 = f32[2,8,192]{2,1,0:T(8,128)S(1)} fusion(f32[2,512,192,8]{1,2,3,0:T(8,128)S(1)} %get-tuple-element.906, f32[2,8,192]{2,1,0:T(8,128)S(1)} %select_maximum_fusion.2, pred[192,512]{1,0:T(8,128)(4,1)S(1)} %compare_and_fusion.6), kind=kLoop, calls=%fused_computation.4.clone.1 | loop fusion | flops 7861248 | bytes 6414336 | tf_op jit(solution)/shard_map/while/body/eval_jaxpr/reduce_sum | solution.py:84
  62.8 18.5 %while.44 = (s32[]{:T(128)}, f32[2,8,192]{2,1,0:T(8,128)S(1)}, s32[3]{0:T(128)S(1)}, s32[]{:T(128)}, s32[1,8]{1,0:T(1,128)S(1)}, /*index=5*/s32[192]{0:T(256)S(1...) while((s32[]{:T(128)}, f32[2,8,192]{2,1,0:T(8,128)S(1)}, ...), condition=%wide.region_10.11_spmd.clone, body=%wide.region_7.10_spmd.clone.sunk | while | flops 815153344 | bytes 18097680 | solution.py:107
  65.3 3.6 %fusion.96 = f32[2,8,192]{2,1,0:T(8,128)S(1)} fusion(f32[2,512,192,8]{1,2,3,0:T(8,128)S(1)} %fusion.95, f32[2,8,192]{2,1,0:T(8,128)S(1)} %get-tuple-element.1010, pred[192,512]{1,0:T(8,128)(4,1)S(1)} %compare_and_fusion.7, bf16[192,2,8,128]{3,0,2,1:T(8,128)(2,1)S(1)} %copy-done, bf16[3,512,2,128]{3,1,2,0:T(8,128)(2,1)} %get-tuple-element.1011, ...), kind=kOutput, calls=%fused_computation.19.clone.1 | convolution fusion | flops 412087296 | bytes 7462916 | tf_op jit(solution)/shard_map/while/body/eval_jaxpr/qgrd,kgd->grqk/dot_general | solution.py:102
  71.5 3.6 %fusion.96 = f32[2,8,192]{2,1,0:T(8,128)S(1)} fusion(f32[2,512,192,8]{1,2,3,0:T(8,128)S(1)} %fusion.95, f32[2,8,192]{2,1,0:T(8,128)S(1)} %get-tuple-element.1010, pred[192,512]{1,0:T(8,128)(4,1)S(1)} %compare_and_fusion.7, bf16[192,2,8,128]{3,0,2,1:T(8,128)(2,1)S(1)} %copy-done, bf16[3,512,2,128]{3,1,2,0:T(8,128)(2,1)} %get-tuple-element.1011, ...), kind=kOutput, calls=%fused_computation.19.clone.1 | convolution fusion | flops 412087296 | bytes 7462916 | tf_op jit(solution)/shard_map/while/body/eval_jaxpr/qgrd,kgd->grqk/dot_general | solution.py:102
  77.7 3.6 %fusion.96 = f32[2,8,192]{2,1,0:T(8,128)S(1)} fusion(f32[2,512,192,8]{1,2,3,0:T(8,128)S(1)} %fusion.95, f32[2,8,192]{2,1,0:T(8,128)S(1)} %get-tuple-element.1010, pred[192,512]{1,0:T(8,128)(4,1)S(1)} %compare_and_fusion.7, bf16[192,2,8,128]{3,0,2,1:T(8,128)(2,1)S(1)} %copy-done, bf16[3,512,2,128]{3,1,2,0:T(8,128)(2,1)} %get-tuple-element.1011, ...), kind=kOutput, calls=%fused_computation.19.clone.1 | convolution fusion | flops 412087296 | bytes 7462916 | tf_op jit(solution)/shard_map/while/body/eval_jaxpr/qgrd,kgd->grqk/dot_general | solution.py:102
  81.3 38.1 %while.45 = (s32[]{:T(128)}, f32[192,2,8,128]{3,0,2,1:T(8,128)S(1)}, f32[3,512,2,2,128]{4,1,0,3,2:T(8,128)}, bf16[3,512,2,128]{3,1,2,0:T(8,128)(2,1)S(1)}, s32[3...) while((s32[]{:T(128)}, ...), condition=%wide.region_13.14_spmd.clone, body=%wide.region_11.13_spmd.clone.sunk | while | flops 2033726720 | bytes 42026536 | solution.py:135
  82.9 1.0 fusion.107
  83.9 2.7 %fusion.109 = f32[512,1,2,128]{3,0,2,1:T(8,128)S(1)} fusion(bf16[192,2,8,128]{3,0,2,1:T(8,128)(2,1)S(1)} %copy-done.1, f32[2,512,192,8]{1,2,3,0:T(8,128)S(1)} %fusion.107, f32[2,8,192]{2,1,0:T(8,128)S(1)} %get-tuple-element.1060, pred[192,512]{1,0:T(8,128)(4,1)S(1)} %compare_and_fusion.8), kind=kOutput, calls=%fused_computation.51.clone.1 | convolution fusion | flops 410517504 | bytes 7712768 | tf_op jit(solution)/shard_map/while/body/eval_jaxpr/grqk,qgrd->kgd/dot_general | solution.py:129
  86.6 3.6 %fusion.108 = bf16[2,8,192,512]{3,2,1,0:T(8,128)(2,1)S(1)} fusion(f32[2,512,192,8]{1,2,3,0:T(8,128)S(1)} %fusion.107, f32[2,8,192]{2,1,0:T(8,128)S(1)} %get-tuple-element.1063, f32[2,8,192]{2,1,0:T(8,128)S(1)} %get-tuple-element.1060, pred[192,512]{1,0:T(8,128)(4,1)S(1)} %compare_and_fusion.8, bf16[192,2,8,128]{3,0,2,1:T(8,128)(2,1)S(1)} %copy-done.1, ...), kind=kOutput, calls=%fused_computation.39.clone.1 | convolution fusion | flops 413663232 | bytes 10608644 | tf_op jit(solution)/shard_map/while/body/eval_jaxpr/qgrd,kgd->grqk/dot_general | solution.py:115
  90.2 1.3 fusion.110
  91.5 1.4 bitcast_add_fusion.2
  92.9 1.1 fusion.111
  95.5 1.0 fusion.107
  96.5 2.7 %fusion.109 = f32[512,1,2,128]{3,0,2,1:T(8,128)S(1)} fusion(bf16[192,2,8,128]{3,0,2,1:T(8,128)(2,1)S(1)} %copy-done.1, f32[2,512,192,8]{1,2,3,0:T(8,128)S(1)} %fusion.107, f32[2,8,192]{2,1,0:T(8,128)S(1)} %get-tuple-element.1060, pred[192,512]{1,0:T(8,128)(4,1)S(1)} %compare_and_fusion.8), kind=kOutput, calls=%fused_computation.51.clone.1 | convolution fusion | flops 410517504 | bytes 7712768 | tf_op jit(solution)/shard_map/while/body/eval_jaxpr/grqk,qgrd->kgd/dot_general | solution.py:129
  99.3 3.6 %fusion.108 = bf16[2,8,192,512]{3,2,1,0:T(8,128)(2,1)S(1)} fusion(f32[2,512,192,8]{1,2,3,0:T(8,128)S(1)} %fusion.107, f32[2,8,192]{2,1,0:T(8,128)S(1)} %get-tuple-element.1063, f32[2,8,192]{2,1,0:T(8,128)S(1)} %get-tuple-element.1060, pred[192,512]{1,0:T(8,128)(4,1)S(1)} %compare_and_fusion.8, bf16[192,2,8,128]{3,0,2,1:T(8,128)(2,1)S(1)} %copy-done.1, ...), kind=kOutput, calls=%fused_computation.39.clone.1 | convolution fusion | flops 413663232 | bytes 10608644 | tf_op jit(solution)/shard_map/while/body/eval_jaxpr/qgrd,kgd->grqk/dot_general | solution.py:115
  102.8 1.3 fusion.110
  104.2 1.4 bitcast_add_fusion.2
  105.5 1.1 fusion.111
  109.2 2.7 %fusion.109 = f32[512,1,2,128]{3,0,2,1:T(8,128)S(1)} fusion(bf16[192,2,8,128]{3,0,2,1:T(8,128)(2,1)S(1)} %copy-done.1, f32[2,512,192,8]{1,2,3,0:T(8,128)S(1)} %fusion.107, f32[2,8,192]{2,1,0:T(8,128)S(1)} %get-tuple-element.1060, pred[192,512]{1,0:T(8,128)(4,1)S(1)} %compare_and_fusion.8), kind=kOutput, calls=%fused_computation.51.clone.1 | convolution fusion | flops 410517504 | bytes 7712768 | tf_op jit(solution)/shard_map/while/body/eval_jaxpr/grqk,qgrd->kgd/dot_general | solution.py:129
  111.9 3.6 %fusion.108 = bf16[2,8,192,512]{3,2,1,0:T(8,128)(2,1)S(1)} fusion(f32[2,512,192,8]{1,2,3,0:T(8,128)S(1)} %fusion.107, f32[2,8,192]{2,1,0:T(8,128)S(1)} %get-tuple-element.1063, f32[2,8,192]{2,1,0:T(8,128)S(1)} %get-tuple-element.1060, pred[192,512]{1,0:T(8,128)(4,1)S(1)} %compare_and_fusion.8, bf16[192,2,8,128]{3,0,2,1:T(8,128)(2,1)S(1)} %copy-done.1, ...), kind=kOutput, calls=%fused_computation.39.clone.1 | convolution fusion | flops 413663232 | bytes 10608644 | tf_op jit(solution)/shard_map/while/body/eval_jaxpr/qgrd,kgd->grqk/dot_general | solution.py:115
  115.5 1.3 fusion.110
  116.9 1.4 bitcast_add_fusion.2
  118.2 1.1 fusion.111
  119.4 3.3 %fusion.53 = (f32[4,192,2,2,128]{4,1,0,3,2:T(8,128)}, f32[4,192,2,2,128]{4,1,0,3,2:T(8,128)S(1)}) fusion(f32[8,192,2,2,128]{4,1,0,3,2:T(8,128)} %bitcast.205), kind=kLoop, calls=%fused_computation.90 | loop fusion | bytes 6291456 | tf_op jit(solution)/shard_map/slice | solution.py:38
  122.7 1.3 slice.43
  123.9 2.3 %collective-permute-start.3 = (f32[4,192,2,2,128]{4,1,0,3,2:T(8,128)}, f32[4,192,2,2,128]{4,1,0,3,2:T(8,128)S(1)}, u32[]{:S(2)}, u32[]{:S(2)}) collective-permute-start(f32[4,192,2,2,128]{4,1,0,3,2:T(8,128)} %slice.43), channel_id=1, source_target_pairs={{8,0},{10,2},{12,4},{14,6},{16,8},{18,10},{20,12},{22,14},{24,16},... | collective-permute-start | bytes 4718600 | tf_op jit(solution)/shard_map/ppermute | solution.py:17
  126.3 33.3 %collective-permute-done.3 = f32[4,192,2,2,128]{4,1,0,3,2:T(8,128)S(1)} collective-permute-done((f32[4,192,2,2,128]{4,1,0,3,2:T(8,128)}, f32[4,192,2,2,128]{4,1,0,3,2:T(8,128)S(1)}, u32[]{:S(2)}, u32[]{:S(2)}) %collective-permute-start.3) | collective-permute-done | bytes 1572896 | tf_op jit(solution)/shard_map/ppermute | solution.py:17
  159.6 1.6 reverse_add_fusion
  161.3 1.9 %collective-permute-start.4 = (f32[2,192,2,2,128]{4,1,0,3,2:T(8,128)S(1)}, f32[2,192,2,2,128]{4,1,0,3,2:T(8,128)S(1)}, u32[]{:S(2)}, u32[]{:S(2)}) collective-permute-start(f32[2,192,2,2,128]{4,1,0,3,2:T(8,128)S(1)} %slice.55), channel_id=1, source_target_pairs={{4,0},{6,2},{8,4},{10,6},{12,8},{14,10},{16,12},{18,14},{20,16},{2... | collective-permute-start | bytes 2359304 | tf_op jit(solution)/shard_map/ppermute | solution.py:17
  163.2 15.8 %collective-permute-done.4 = f32[2,192,2,2,128]{4,1,0,3,2:T(8,128)S(1)} collective-permute-done((f32[2,192,2,2,128]{4,1,0,3,2:T(8,128)S(1)}, f32[2,192,2,2,128]{4,1,0,3,2:T(8,128)S(1)}, u32[]{:S(2)}, u32[]{:S(2)}) %collective-permute-start.4) | collective-permute-done | bytes 786464 | tf_op jit(solution)/shard_map/ppermute | solution.py:17
  179.2 2.4 %collective-permute-start.5 = (f32[1,192,2,2,128]{4,1,0,3,2:T(8,128)S(1)}, f32[1,192,2,2,128]{4,1,0,3,2:T(8,128)S(1)}, u32[]{:S(2)}, u32[]{:S(2)}) collective-permute-start(f32[1,192,2,2,128]{4,1,0,3,2:T(8,128)S(1)} %slice.57), channel_id=1, source_target_pairs={{2,0},{4,2},{6,4},{8,6},{10,8},{12,10},{14,12},{16,14},{18,16},{20... | collective-permute-start | bytes 1179656 | tf_op jit(solution)/shard_map/ppermute | solution.py:17
  181.9 1.4 copy.49
  183.2 5.6 %collective-permute-done.5 = f32[1,192,2,2,128]{4,1,0,3,2:T(8,128)S(1)} collective-permute-done((f32[1,192,2,2,128]{4,1,0,3,2:T(8,128)S(1)}, f32[1,192,2,2,128]{4,1,0,3,2:T(8,128)S(1)}, u32[]{:S(2)}, u32[]{:S(2)}) %collective-permute-start.5) | collective-permute-done | bytes 393248 | tf_op jit(solution)/shard_map/ppermute | solution.py:17
  (109 shorter events, 17.9 us)
Async XLA Ops:
  1.6 10.3 %collective-permute-start = (bf16[1,192,2,2,128]{4,1,0,3,2:T(8,128)(2,1)S(1)}, bf16[1,192,2,2,128]{4,1,0,3,2:T(8,128)(2,1)S(1)}, u32[]{:S(2)}, u32[]{:S(2)}) collective-permute-start(bf16[1,192,2,2,128]{4,1,0,3,2:T(8,128)(2,1)S(1)} %maximum_bitcast_fusion.1), channel_id=1, source_target_pairs={{0,2},{2,4},{4,6},{6,8},{8,10},{10,12},{12,14},{14,16},{16,18},{18... | collective-permute-start | bytes 589832 | tf_op jit(solution)/shard_map/ppermute | solution.py:17
  12.0 12.8 %collective-permute-start.1 = (bf16[2,192,2,2,128]{4,1,0,3,2:T(8,128)(2,1)S(1)}, bf16[2,192,2,2,128]{4,1,0,3,2:T(8,128)(2,1)S(1)}, u32[]{:S(2)}, u32[]{:S(2)}) collective-permute-start(bf16[2,192,2,2,128]{4,1,0,3,2:T(8,128)(2,1)S(1)} %pad_maximum_fusion.2), channel_id=1, source_target_pairs={{0,4},{2,6},{4,8},{6,10},{8,12},{10,14},{12,16},{14,18},{16,20},{1... | collective-permute-start | bytes 1179656 | tf_op jit(solution)/shard_map/ppermute | solution.py:17
  25.8 19.8 %collective-permute-start.2 = (bf16[4,192,2,2,128]{4,1,0,3,2:T(8,128)(2,1)}, bf16[4,192,2,2,128]{4,1,0,3,2:T(8,128)(2,1)}, u32[]{:S(2)}, u32[]{:S(2)}) collective-permute-start(bf16[4,192,2,2,128]{4,1,0,3,2:T(8,128)(2,1)} %pad_maximum_fusion.1), channel_id=1, source_target_pairs={{0,8},{2,10},{4,12},{6,14},{8,16},{10,18},{12,20},{14,22},{16,24},... | collective-permute-start | bytes 2359304 | tf_op jit(solution)/shard_map/ppermute | solution.py:17
  64.0 1.3 copy-start
  70.2 1.3 copy-start
  76.4 1.3 copy-start
  82.5 1.3 copy-start.1
  95.2 1.3 copy-start.1
  107.9 1.3 copy-start.1
  123.9 35.7 %collective-permute-start.3 = (f32[4,192,2,2,128]{4,1,0,3,2:T(8,128)}, f32[4,192,2,2,128]{4,1,0,3,2:T(8,128)S(1)}, u32[]{:S(2)}, u32[]{:S(2)}) collective-permute-start(f32[4,192,2,2,128]{4,1,0,3,2:T(8,128)} %slice.43), channel_id=1, source_target_pairs={{8,0},{10,2},{12,4},{14,6},{16,8},{18,10},{20,12},{22,14},{24,16},... | collective-permute-start | bytes 4718600 | tf_op jit(solution)/shard_map/ppermute | solution.py:17
  161.3 17.8 %collective-permute-start.4 = (f32[2,192,2,2,128]{4,1,0,3,2:T(8,128)S(1)}, f32[2,192,2,2,128]{4,1,0,3,2:T(8,128)S(1)}, u32[]{:S(2)}, u32[]{:S(2)}) collective-permute-start(f32[2,192,2,2,128]{4,1,0,3,2:T(8,128)S(1)} %slice.55), channel_id=1, source_target_pairs={{4,0},{6,2},{8,4},{10,6},{12,8},{14,10},{16,12},{18,14},{20,16},{2... | collective-permute-start | bytes 2359304 | tf_op jit(solution)/shard_map/ppermute | solution.py:17
  179.2 9.7 %collective-permute-start.5 = (f32[1,192,2,2,128]{4,1,0,3,2:T(8,128)S(1)}, f32[1,192,2,2,128]{4,1,0,3,2:T(8,128)S(1)}, u32[]{:S(2)}, u32[]{:S(2)}) collective-permute-start(f32[1,192,2,2,128]{4,1,0,3,2:T(8,128)S(1)} %slice.57), channel_id=1, source_target_pairs={{2,0},{4,2},{6,4},{8,6},{10,8},{12,10},{14,12},{16,14},{18,16},{20... | collective-permute-start | bytes 1179656 | tf_op jit(solution)/shard_map/ppermute | solution.py:17
where the time goes:
time: 193 us; the launch traced here: 190 us
  waiting for transfers between devices  83.7 us (43%)
  matrix products  47.2 us (24%)
  local copies, waits for them, and re-layouts  18.6 us (10%)
  other arithmetic  17.4 us (9%)
  starting transfers between devices  16.1 us (8%)
  loops' own time  6.54 us (3%)
    ppermute x6, waiting for transfers between devices, shifted(): return lax.ppermute(array, axis, pairs)  83.7 us
    ppermute x6, starting transfers between devices, shifted(): return lax.ppermute(array, axis, pairs)  16.1 us
    dot_general x3, matrix products, grad_step(): jnp.einsum('qgrd,kgd->grqk', grad_rows, value_block, preferred_element_ty...  10.7 us
    dot_general x3, matrix products, delta_step(): jnp.einsum('qgrd,kgd->grqk', grad_rows, value_block, preferred_element_ty...  10.7 us
    dot_general x9, matrix products, logits_of(): jnp.einsum('qgrd,kgd->grqk', query_rows, key_block, preferred_element_typ...  9.47 us
    dot_general x3, matrix products, grad_step(): jnp.einsum('grqk,qgrd->kgd', probs_low, grad_rows, preferred_element_type...  8.19 us
    reduce_sum x3, other arithmetic, max_step(): jnp.sum(weights, axis=-1)  6.27 us
    unnamed x6, local copies, waits for them, and re-layouts  6.02 us
  transfers between devices with their start and end apart: 6, of which 6 were waited for; matrix products, arithmetic and copies ran while one was open for 3% of the time, Pallas kernels for 0%

commit v1 on v0

v1 whole, which is shorter than its diff:
```python
import functools
import math

import jax
import jax.numpy as jnp
from jax import lax
from jax.experimental import pallas as pl
from jax.experimental.pallas import tpu as pltpu
from jax.sharding import PartitionSpec as P

MAXDOC = 1345
PLANE = 4
FLIPS = (1, 2, 3)
LOG2E = math.log2(math.e)
NEG_INIT = -1e30
NEG_DEAD = -2e30
CHUNK = 512

NT = (((1,), (1,)), ((), ()))
NN = (((1,), (0,)), ((), ()))
TN = (((0,), (0,)), ((), ()))


def mm(a, b, dims):
    return lax.dot_general(a, b, dims, preferred_element_type=jnp.float32)


def kernel(heads_per, n_docs, *refs):
    (place_ref, lens_ref, q_ref, do_ref, own_ref, up_ref) = refs[:6]
    near_refs, far_refs, upx_refs = refs[6:9], refs[9:12], refs[12:15]
    dq_ref = refs[15]
    part_refs = refs[16:24]
    kv, part, m_ref, l_ref, d_ref, dqt, start_ref, pos_ref, stripe_ref = refs[24:]
    groups, cols, dim = q_ref.shape
    stripe = own_ref.shape[2]
    scale = dim**-0.5
    scale2 = scale * LOG2E
    me = place_ref[0]
    lane = lax.rem(me, PLANE)
    first_pos = me * stripe

    col = lax.broadcasted_iota(jnp.int32, (1, cols), 1)
    pos = first_pos + lax.div(col, heads_per)
    start = jnp.zeros((1, cols), jnp.int32)
    end = jnp.int32(0)
    first_key = jnp.int32(0)
    for n in range(n_docs):
        end = end + lens_ref[n]
        start = jnp.maximum(start, jnp.where(pos >= end, end, 0))
        first_key = jnp.maximum(first_key, jnp.where(first_pos >= end, end, 0))
    start_ref[...] = start
    pos_ref[...] = pos

    kv[0] = own_ref[...]
    kv[1] = up_ref[...]
    stripe_ref[0] = me
    stripe_ref[1] = me - PLANE
    for k, flip in enumerate(FLIPS):
        other = jnp.bitwise_xor(lane, flip)
        is_near = other < lane
        kv[2 + k] = upx_refs[k][...]
        stripe_ref[2 + k] = me - PLANE - lane + other

        @pl.when(is_near)
        def _():
            kv[5 + k] = near_refs[k][...]

        @pl.when(jnp.logical_not(is_near))
        def _():
            kv[5 + k] = far_refs[k][...]

        stripe_ref[5 + k] = jnp.where(is_near, me - lane + other, me - 2 * PLANE - lane + other)

    m_ref[...] = jnp.full_like(m_ref, NEG_INIT)
    l_ref[...] = jnp.zeros_like(l_ref)
    d_ref[...] = jnp.zeros_like(d_ref)
    dqt[...] = jnp.zeros_like(dqt)

    def logits(keys, q_c, base, cs):
        s = mm(keys, q_c, NT) * scale2
        kpos = base + lax.broadcasted_iota(jnp.int32, s.shape, 0)
        live = (kpos >= start_ref[:, cs]) & (kpos <= pos_ref[:, cs])
        return jnp.where(live, s, NEG_DEAD)

    def is_live(slot):
        at = stripe_ref[slot]
        return (at >= 0) & ((at + 1) * stripe > first_key)

    def stats_step(i, carry):
        slot, g = lax.div(i, groups), lax.rem(i, groups)

        @pl.when(is_live(slot))
        def _():
            base = stripe_ref[slot] * stripe
            keys, vals = kv[slot, 0, g], kv[slot, 1, g]
            for c in range(0, cols, CHUNK):
                cs = pl.ds(c, CHUNK)
                s = logits(keys, q_ref[g, cs, :], base, cs)
                gp = mm(vals, do_ref[g, cs, :], NT)
                m_old = m_ref[g, :, cs]
                m_new = jnp.maximum(m_old, jnp.max(s, axis=0, keepdims=True))
                e = jnp.exp2(s - m_new)
                fade = jnp.exp2(m_old - m_new)
                m_ref[g, :, cs] = m_new
                l_ref[g, :, cs] = l_ref[g, :, cs] * fade + jnp.sum(e, axis=0, keepdims=True)
                d_ref[g, :, cs] = d_ref[g, :, cs] * fade + jnp.sum(e * gp, axis=0, keepdims=True)

        return carry

    lax.fori_loop(0, 8 * groups, stats_step, 0)
    d_ref[...] = d_ref[...] / l_ref[...]
    m_ref[...] = m_ref[...] + jnp.log2(l_ref[...])

    def grad_step(i, carry):
        slot, g = lax.div(i, groups), lax.rem(i, groups)
        live = is_live(slot)

        @pl.when(live)
        def _():
            base = stripe_ref[slot] * stripe
            keys, vals = kv[slot, 0, g], kv[slot, 1, g]
            dk = jnp.zeros((stripe, dim), jnp.float32)
            dv = jnp.zeros((stripe, dim), jnp.float32)
            for c in range(0, cols, CHUNK):
                cs = pl.ds(c, CHUNK)
                q_c, do_c = q_ref[g, cs, :], do_ref[g, cs, :]
                s = logits(keys, q_c, base, cs)
                gp = mm(vals, do_c, NT)
                p = jnp.exp2(s - m_ref[g, :, cs])
                ds = (p * (gp - d_ref[g, :, cs])).astype(jnp.bfloat16)
                dv = dv + mm(p.astype(jnp.bfloat16), do_c, NN)
                dk = dk + mm(ds, q_c, NN)
                dqt[g, :, cs] = dqt[g, :, cs] + mm(keys, ds, TN)
            part[slot, 0, g] = (dk * scale).astype(jnp.bfloat16)
            part[slot, 1, g] = dv.astype(jnp.bfloat16)

        @pl.when(jnp.logical_not(live))
        def _():
            part[slot, 0, g] = jnp.zeros((stripe, dim), jnp.bfloat16)
            part[slot, 1, g] = jnp.zeros((stripe, dim), jnp.bfloat16)

        return carry

    lax.fori_loop(0, 8 * groups, grad_step, 0)
    for n in range(8):
        part_refs[n][...] = part[n]
    for g in range(groups):
        dq_ref[g] = (dqt[g] * scale).T.astype(jnp.bfloat16)


def shards(queries, key_vectors, value_matrix, grad_out, doc_lengths):
    stripe, heads, dim = queries.shape
    groups = key_vectors.shape[1]
    heads_per = heads // groups
    cols = stripe * heads_per
    length = lax.axis_size("ctx")
    me = lax.axis_index("ctx").astype(jnp.int32)
    lane = lax.rem(me, PLANE)

    def send(array, to):
        pairs = [(i, to(i)) for i in range(length) if to(i) is not None and 0 <= to(i) < length]
        return lax.ppermute(array, "ctx", pairs)

    def flip_if(flip, test):
        return lambda i: (i ^ flip) if test(i ^ flip, i) else None

    own = jnp.stack([key_vectors, value_matrix]).transpose(0, 2, 1, 3)
    up = send(own, lambda i: i + PLANE)
    near = [send(own, flip_if(f, lambda to, i: to > i)) for f in FLIPS]
    upx = [send(up, lambda i, f=f: i ^ f) for f in FLIPS]
    up2 = send(up, lambda i: i + PLANE)
    far = [send(up2, flip_if(f, lambda to, i: to < i)) for f in FLIPS]

    def columns(array):
        return array.reshape(stripe, groups, heads_per, dim).transpose(1, 0, 2, 3).reshape(groups, cols, dim)

    q, do = columns(queries), columns(grad_out)
    smem = pl.BlockSpec(memory_space=pltpu.SMEM)
    vmem = pl.BlockSpec(memory_space=pltpu.VMEM)
    piece = jax.ShapeDtypeStruct(own.shape, jnp.bfloat16)
    stat = pltpu.VMEM((groups, 1, cols), jnp.float32)
    row = pltpu.VMEM((1, cols), jnp.int32)
    outs = pl.pallas_call(
        functools.partial(kernel, heads_per, doc_lengths.shape[0]),
        out_shape=[jax.ShapeDtypeStruct(q.shape, jnp.bfloat16)] + [piece] * 8,
        in_specs=[smem, smem] + [vmem] * 13,
        out_specs=[vmem] * 9,
        scratch_shapes=[
            pltpu.VMEM((8,) + own.shape, jnp.bfloat16),
            pltpu.VMEM((8,) + own.shape, jnp.bfloat16),
            stat,
            stat,
            stat,
            pltpu.VMEM((groups, dim, cols), jnp.float32),
            row,
            row,
            pltpu.SMEM((8,), jnp.int32),
        ],
        compiler_params=pltpu.CompilerParams(vmem_limit_bytes=40 << 20),
    )(me[None], doc_lengths, q, do, own, up, *near, *far, *upx)
    dq, parts = outs[0], outs[1:]
    mixed = [send(parts[5 + k], lambda i, f=f: i ^ f).astype(jnp.float32) for k, f in enumerate(FLIPS)]
    level = [send(parts[2 + k], lambda i, f=f: i ^ f).astype(jnp.float32) for k, f in enumerate(FLIPS)]
    mine = parts[0].astype(jnp.float32)
    far_sum = jnp.zeros_like(mine)
    for k, flip in enumerate(FLIPS):
        other = jnp.bitwise_xor(lane, flip)
        mine = mine + jnp.where(other > lane, mixed[k], 0.0)
        far_sum = far_sum + jnp.where(other < lane, mixed[k], 0.0)
    down2 = send(far_sum.astype(jnp.bfloat16), lambda i: i - PLANE).astype(jnp.float32)
    level_sum = parts[1].astype(jnp.float32) + sum(level) + down2
    down = send(level_sum.astype(jnp.bfloat16), lambda i: i - PLANE).astype(jnp.float32)
    total = (mine + down).astype(jnp.bfloat16).transpose(0, 2, 1, 3)
    dq = dq.reshape(groups, stripe, heads_per, dim).transpose(1, 0, 2, 3).reshape(stripe, heads, dim)
    return dq, total[0], total[1]


def solution(mesh):
    spec = P("ctx", "tp", None)
    return jax.shard_map(
        shards,
        mesh=mesh,
        in_specs=(spec, spec, spec, spec, P()),
        out_specs=(spec, spec, spec),
        check_vma=False,
    )
```

time: 193 us -> 110 us (0.57); the launches traced: 190 us -> 110 us
  waiting for transfers between devices: 83.7 us -> 27.7 us
  matrix products: 47.2 us -> 0 us
  Pallas kernels: 0 us -> 27.7 us
  starting transfers between devices: 16.1 us -> 41.3 us
  other arithmetic: 17.4 us -> 0.45 us
  local copies, waits for them, and re-layouts: 18.6 us -> 11.7 us
  loops' own time: 6.54 us -> 0 us
    ppermute x6 -> x19, waiting for transfers between devices: 83.7 us -> 27.7 us  [send(): return lax.ppermute(array, 'ctx', pairs)]
    dot_general x24 -> x0, matrix products: 47.2 us -> none  [the longest x3 10.7 us: grad_step(): jnp.einsum('qgrd,kgd->grqk', grad_rows, value_block, preferred_element_ty...]
    pallas_call x0 -> x1, Pallas kernels: none -> 27.7 us  [shards(): pl.pallas_call(functools.partial(kernel, heads_per, doc_lengths.shape[0])...]
    ppermute x6 -> x19, starting transfers between devices: 16.1 us -> 41.3 us  [send(): return lax.ppermute(array, 'ctx', pairs)]
    reduce_sum x13 -> x0, other arithmetic: 7.12 us -> none  [the longest x3 6.27 us: max_step(): jnp.sum(weights, axis=-1)]
    another operation x3 -> x0, loops' own time: 6.54 us -> none  [the longest x1 2.22 us: shards(): lax.scan(grad_step, start_grad, (key_blocks, value_blocks, numbers))]
    dynamic_slice x9 -> x0, local copies, waits for them, and re-layouts: 5.42 us -> none  [shards(): lax.scan(max_step, start_stats, (key_blocks, numbers))]
    slice x5 -> x0, local copies, waits for them, and re-layouts: 4.75 us -> none  [the longest x1 3.3 us: return_window(): by_offset = by_offset[:stride] + arrived]
  transfers between devices with their start and end apart: 6 -> 19, of which waited for: 6 -> 13; matrix products, arithmetic and copies ran while one was open for 3% -> 1% of each run, Pallas kernels for 0% -> 0%
where the time goes in v1:
time: 110 us
  starting transfers between devices  41.3 us (38%)
  waiting for transfers between devices  27.7 us (25%)
  Pallas kernels  27.7 us (25%)
  local copies, waits for them, and re-layouts  11.7 us (11%)
    ppermute x19, starting transfers between devices, send(): return lax.ppermute(array, 'ctx', pairs)  41.3 us
    ppermute x19, waiting for transfers between devices, send(): return lax.ppermute(array, 'ctx', pairs)  27.7 us
    pallas_call x1, Pallas kernels, shards(): pl.pallas_call(functools.partial(kernel, heads_per, doc_lengths.shape[0])...  27.7 us
    unnamed x38, local copies, waits for them, and re-layouts  9.28 us
  transfers between devices with their start and end apart: 19, of which 13 were waited for; matrix products, arithmetic and copies ran while one was open for 1% of the time, Pallas kernels for 0%

profile of v1, /device:TPU:16, one launch (start us, length us, event | category | flops | bytes accessed | tf_op | source)
XLA Modules:
  0.0 109.7 jit_solution(11891911289465194668)
XLA Ops:
  0.7 1.1 copy_bitcast_fusion.3
  1.8 3.5 %collective-permute-start = (bf16[2,2,192,128]{3,2,1,0:T(8,128)(2,1)S(1)}, bf16[2,2,192,128]{3,2,1,0:T(8,128)(2,1)S(1)}, u32[]{:S(2)}, u32[]{:S(2)}) collective-permute-start(bf16[2,2,192,128]{3,2,1,0:T(8,128)(2,1)S(1)} %maximum_bitcast_fusion.refs_4_), channel_id=1, source_target_pairs={{0,8},{2,10},{4,12},{6,14},{8,16},{10,18},{12,20},{14,22},{16,24},... | collective-permute-start | bytes 589832 | tf_op jit(solution)/shard_map/ppermute | solution.py:162
  5.3 3.4 %collective-permute-start.1 = (bf16[2,2,192,128]{3,2,1,0:T(8,128)(2,1)S(1)}, bf16[2,2,192,128]{3,2,1,0:T(8,128)(2,1)S(1)}, u32[]{:S(2)}, u32[]{:S(2)}) collective-permute-start(bf16[2,2,192,128]{3,2,1,0:T(8,128)(2,1)S(1)} %maximum_bitcast_fusion.refs_4_), channel_id=1, source_target_pairs={{0,2},{4,6},{8,10},{12,14},{16,18},{20,22},{24,26},{28,30},{1,3},{... | collective-permute-start | bytes 589832 | tf_op jit(solution)/shard_map/ppermute | solution.py:162
  8.7 3.4 %collective-permute-start.2 = (bf16[2,2,192,128]{3,2,1,0:T(8,128)(2,1)S(1)}, bf16[2,2,192,128]{3,2,1,0:T(8,128)(2,1)S(1)}, u32[]{:S(2)}, u32[]{:S(2)}) collective-permute-start(bf16[2,2,192,128]{3,2,1,0:T(8,128)(2,1)S(1)} %maximum_bitcast_fusion.refs_4_), channel_id=1, source_target_pairs={{0,4},{2,6},{8,12},{10,14},{16,20},{18,22},{24,28},{26,30},{1,5},{... | collective-permute-start | bytes 589832 | tf_op jit(solution)/shard_map/ppermute | solution.py:162
  12.1 1.9 %collective-permute-start.4 = (bf16[2,2,192,128]{3,2,1,0:T(8,128)(2,1)S(1)}, bf16[2,2,192,128]{3,2,1,0:T(8,128)(2,1)}, u32[]{:S(2)}, u32[]{:S(2)}) collective-permute-start(bf16[2,2,192,128]{3,2,1,0:T(8,128)(2,1)S(1)} %collective-permute-done.refs_5_), channel_id=1, source_target_pairs={{0,8},{2,10},{4,12},{6,14},{8,16},{10,18},{12,20},{14,22},{16,24},... | collective-permute-start | bytes 589832 | tf_op jit(solution)/shard_map/ppermute | solution.py:162
  14.1 4.1 %collective-permute-start.3 = (bf16[2,2,192,128]{3,2,1,0:T(8,128)(2,1)S(1)}, bf16[2,2,192,128]{3,2,1,0:T(8,128)(2,1)S(1)}, u32[]{:S(2)}, u32[]{:S(2)}) collective-permute-start(bf16[2,2,192,128]{3,2,1,0:T(8,128)(2,1)S(1)} %maximum_bitcast_fusion.refs_4_), channel_id=1, source_target_pairs={{0,6},{2,4},{8,14},{10,12},{16,22},{18,20},{24,30},{26,28},{1,7},{... | collective-permute-start | bytes 589832 | tf_op jit(solution)/shard_map/ppermute | solution.py:162
  18.3 0.6 collective-permute-start.8
  18.9 2.9 %collective-permute-start.9 = (bf16[2,2,192,128]{3,2,1,0:T(8,128)(2,1)S(1)}, bf16[2,2,192,128]{3,2,1,0:T(8,128)(2,1)}, u32[]{:S(2)}, u32[]{:S(2)}) collective-permute-start(bf16[2,2,192,128]{3,2,1,0:T(8,128)(2,1)S(1)} %collective-permute-done.refs_5_), channel_id=1, source_target_pairs={{0,4},{2,6},{4,0},{6,2},{8,12},{10,14},{12,8},{14,10},{16,20},{18,... | collective-permute-start | bytes 589832 | tf_op jit(solution)/shard_map/ppermute | solution.py:162
  21.7 1.3 %collective-permute-start.5 = (bf16[2,2,192,128]{3,2,1,0:T(8,128)(2,1)}, bf16[2,2,192,128]{3,2,1,0:T(8,128)(2,1)}, u32[]{:S(2)}, u32[]{:S(2)}) collective-permute-start(bf16[2,2,192,128]{3,2,1,0:T(8,128)(2,1)} %collective-permute-done.4), channel_id=1, source_target_pairs={{2,0},{6,4},{10,8},{14,12},{18,16},{22,20},{26,24},{30,28},{3,1},{... | collective-permute-start | bytes 589832 | tf_op jit(solution)/shard_map/ppermute | solution.py:162
  23.0 0.4 collective-permute-done.3.refs_8_
  23.5 1.3 %collective-permute-start.6 = (bf16[2,2,192,128]{3,2,1,0:T(8,128)(2,1)}, bf16[2,2,192,128]{3,2,1,0:T(8,128)(2,1)}, u32[]{:S(2)}, u32[]{:S(2)}) collective-permute-start(bf16[2,2,192,128]{3,2,1,0:T(8,128)(2,1)} %collective-permute-done.4), channel_id=1, source_target_pairs={{4,0},{6,2},{12,8},{14,10},{20,16},{22,18},{28,24},{30,26},{5,1},{... | collective-permute-start | bytes 589832 | tf_op jit(solution)/shard_map/ppermute | solution.py:162
  24.8 2.8 %collective-permute-done.10.refs_14_ = bf16[2,2,192,128]{3,2,1,0:T(8,128)(2,1)S(1)} collective-permute-done((bf16[2,2,192,128]{3,2,1,0:T(8,128)(2,1)S(1)}, bf16[2,2,192,128]{3,2,1,0:T(8,128)(2,1)S(1)}, u32[]{:S(2)}, u32[]{:S(2)}) %collective-permute-start.10) | collective-permute-done | bytes 196640 | tf_op jit(solution)/shard_map/ppermute | solution.py:162
  27.5 1.3 %collective-permute-start.7 = (bf16[2,2,192,128]{3,2,1,0:T(8,128)(2,1)}, bf16[2,2,192,128]{3,2,1,0:T(8,128)(2,1)}, u32[]{:S(2)}, u32[]{:S(2)}) collective-permute-start(bf16[2,2,192,128]{3,2,1,0:T(8,128)(2,1)} %collective-permute-done.4), channel_id=1, source_target_pairs={{4,2},{6,0},{12,10},{14,8},{20,18},{22,16},{28,26},{30,24},{5,3},{... | collective-permute-start | bytes 589832 | tf_op jit(solution)/shard_map/ppermute | solution.py:162
  28.8 0.3 copy_bitcast_fusion.1
  29.2 3.7 %collective-permute-done.8.refs_12_ = bf16[2,2,192,128]{3,2,1,0:T(8,128)(2,1)} collective-permute-done((bf16[2,2,192,128]{3,2,1,0:T(8,128)(2,1)S(1)}, bf16[2,2,192,128]{3,2,1,0:T(8,128)(2,1)}, u32[]{:S(2)}, u32[]{:S(2)}) %collective-permute-start.8) | collective-permute-done | bytes 196640 | tf_op jit(solution)/shard_map/ppermute | solution.py:162
  32.8 2.1 %collective-permute-done.5.refs_9_ = bf16[2,2,192,128]{3,2,1,0:T(8,128)(2,1)} collective-permute-done((bf16[2,2,192,128]{3,2,1,0:T(8,128)(2,1)}, bf16[2,2,192,128]{3,2,1,0:T(8,128)(2,1)}, u32[]{:S(2)}, u32[]{:S(2)}) %collective-permute-start.5) | collective-permute-done | bytes 196640 | tf_op jit(solution)/shard_map/ppermute | solution.py:162
  35.0 2.1 %collective-permute-done.7.refs_11_ = bf16[2,2,192,128]{3,2,1,0:T(8,128)(2,1)} collective-permute-done((bf16[2,2,192,128]{3,2,1,0:T(8,128)(2,1)}, bf16[2,2,192,128]{3,2,1,0:T(8,128)(2,1)}, u32[]{:S(2)}, u32[]{:S(2)}) %collective-permute-start.7) | collective-permute-done | bytes 196640 | tf_op jit(solution)/shard_map/ppermute | solution.py:162
  37.1 0.7 copy-done.13
  37.8 0.9 copy-done.2
  38.7 0.9 copy-done.4
  39.6 0.9 copy-done.6
  40.6 0.9 copy-done.8
  41.5 27.7 %shard_map.76 = (bf16[2,1536,128]{2,1,0:T(8,128)(2,1)S(1)}, bf16[2,2,192,128]{3,2,1,0:T(8,128)(2,1)S(1)}, bf16[2,2,192,128]{3,2,1,0:T(8,128)(2,1)S(1)}, bf16[2,2...) custom-call(s32[1]{0:T(128)} %bitcast.refs_0_, ...), custom_call_target="tpu_custom_call" | custom-call | tf_op jit(solution)/shard_map/pallas_call | solution.py:183
  69.2 0.7 copy-done.9
  69.9 0.7 copy-done.11
  70.5 0.7 copy-done.14
  71.2 0.7 copy-done.15
  71.9 0.7 copy-done.16
  72.6 4.5 %collective-permute-start.11 = (bf16[2,2,192,128]{3,2,1,0:T(8,128)(2,1)}, bf16[2,2,192,128]{3,2,1,0:T(8,128)(2,1)S(1)}, u32[]{:S(2)}, u32[]{:S(2)}) collective-permute-start(bf16[2,2,192,128]{3,2,1,0:T(8,128)(2,1)} %get-tuple-element.14), channel_id=1, source_target_pairs={{0,2},{2,0},{4,6},{6,4},{8,10},{10,8},{12,14},{14,12},{16,18},{18,... | collective-permute-start | bytes 589832 | tf_op jit(solution)/shard_map/ppermute | solution.py:162
  77.1 2.0 %collective-permute-start.12 = (bf16[2,2,192,128]{3,2,1,0:T(8,128)(2,1)}, bf16[2,2,192,128]{3,2,1,0:T(8,128)(2,1)S(1)}, u32[]{:S(2)}, u32[]{:S(2)}) collective-permute-start(bf16[2,2,192,128]{3,2,1,0:T(8,128)(2,1)} %get-tuple-element.15), channel_id=1, source_target_pairs={{0,4},{2,6},{4,0},{6,2},{8,12},{10,14},{12,8},{14,10},{16,20},{18,... | collective-permute-start | bytes 589832 | tf_op jit(solution)/shard_map/ppermute | solution.py:162
  79.2 1.5 %collective-permute-start.13 = (bf16[2,2,192,128]{3,2,1,0:T(8,128)(2,1)}, bf16[2,2,192,128]{3,2,1,0:T(8,128)(2,1)S(1)}, u32[]{:S(2)}, u32[]{:S(2)}) collective-permute-start(bf16[2,2,192,128]{3,2,1,0:T(8,128)(2,1)} %get-tuple-element.16), channel_id=1, source_target_pairs={{0,6},{2,4},{4,2},{6,0},{8,14},{10,12},{12,10},{14,8},{16,22},{18,... | collective-permute-start | bytes 589832 | tf_op jit(solution)/shard_map/ppermute | solution.py:162
  80.6 0.6 collective-permute-start.14
  81.2 1.5 %collective-permute-start.15 = (bf16[2,2,192,128]{3,2,1,0:T(8,128)(2,1)}, bf16[2,2,192,128]{3,2,1,0:T(8,128)(2,1)S(1)}, u32[]{:S(2)}, u32[]{:S(2)}) collective-permute-start(bf16[2,2,192,128]{3,2,1,0:T(8,128)(2,1)} %copy-done.15), channel_id=1, source_target_pairs={{0,4},{2,6},{4,0},{6,2},{8,12},{10,14},{12,8},{14,10},{16,20},{18,... | collective-permute-start | bytes 589832 | tf_op jit(solution)/shard_map/ppermute | solution.py:162
  82.6 0.2 collective-permute-done.11
  82.8 3.7 %collective-permute-start.16 = (bf16[2,2,192,128]{3,2,1,0:T(8,128)(2,1)}, bf16[2,2,192,128]{3,2,1,0:T(8,128)(2,1)S(1)}, u32[]{:S(2)}, u32[]{:S(2)}) collective-permute-start(bf16[2,2,192,128]{3,2,1,0:T(8,128)(2,1)} %copy-done.14), channel_id=1, source_target_pairs={{0,6},{2,4},{4,2},{6,0},{8,14},{10,12},{12,10},{14,8},{16,22},{18,... | collective-permute-start | bytes 589832 | tf_op jit(solution)/shard_map/ppermute | solution.py:162
  86.6 1.9 %collective-permute-done.12 = bf16[2,2,192,128]{3,2,1,0:T(8,128)(2,1)S(1)} collective-permute-done((bf16[2,2,192,128]{3,2,1,0:T(8,128)(2,1)}, bf16[2,2,192,128]{3,2,1,0:T(8,128)(2,1)S(1)}, u32[]{:S(2)}, u32[]{:S(2)}) %collective-permute-start.12) | collective-permute-done | bytes 196640 | tf_op jit(solution)/shard_map/ppermute | solution.py:162
  88.4 2.4 %collective-permute-done.13 = bf16[2,2,192,128]{3,2,1,0:T(8,128)(2,1)S(1)} collective-permute-done((bf16[2,2,192,128]{3,2,1,0:T(8,128)(2,1)}, bf16[2,2,192,128]{3,2,1,0:T(8,128)(2,1)S(1)}, u32[]{:S(2)}, u32[]{:S(2)}) %collective-permute-start.13) | collective-permute-done | bytes 196640 | tf_op jit(solution)/shard_map/ppermute | solution.py:162
  91.0 1.9 %collective-permute-start.17 = (bf16[2,2,192,128]{3,2,1,0:T(8,128)(2,1)S(1)}, bf16[2,2,192,128]{3,2,1,0:T(8,128)(2,1)S(1)}, u32[]{:S(2)}, u32[]{:S(2)}) collective-permute-start(bf16[2,2,192,128]{3,2,1,0:T(8,128)(2,1)S(1)} %fusion.7), channel_id=1, source_target_pairs={{8,0},{10,2},{12,4},{14,6},{16,8},{18,10},{20,12},{22,14},{24,16},... | collective-permute-start | bytes 589832 | tf_op jit(solution)/shard_map/ppermute | solution.py:162
  93.0 0.9 collective-permute-done.15
  93.9 1.9 %collective-permute-done.16 = bf16[2,2,192,128]{3,2,1,0:T(8,128)(2,1)S(1)} collective-permute-done((bf16[2,2,192,128]{3,2,1,0:T(8,128)(2,1)}, bf16[2,2,192,128]{3,2,1,0:T(8,128)(2,1)S(1)}, u32[]{:S(2)}, u32[]{:S(2)}) %collective-permute-start.16) | collective-permute-done | bytes 196640 | tf_op jit(solution)/shard_map/ppermute | solution.py:162
  95.8 4.5 %collective-permute-done.17 = bf16[2,2,192,128]{3,2,1,0:T(8,128)(2,1)S(1)} collective-permute-done((bf16[2,2,192,128]{3,2,1,0:T(8,128)(2,1)S(1)}, bf16[2,2,192,128]{3,2,1,0:T(8,128)(2,1)S(1)}, u32[]{:S(2)}, u32[]{:S(2)}) %collective-permute-start.17) | collective-permute-done | bytes 196640 | tf_op jit(solution)/shard_map/ppermute | solution.py:162
  100.3 0.1 add_convert_fusion
  100.5 1.9 %collective-permute-start.18 = (bf16[2,2,192,128]{3,2,1,0:T(8,128)(2,1)S(1)}, bf16[2,2,192,128]{3,2,1,0:T(8,128)(2,1)S(1)}, u32[]{:S(2)}, u32[]{:S(2)}) collective-permute-start(bf16[2,2,192,128]{3,2,1,0:T(8,128)(2,1)S(1)} %add_convert_fusion), channel_id=1, source_target_pairs={{8,0},{10,2},{12,4},{14,6},{16,8},{18,10},{20,12},{22,14},{24,16},... | collective-permute-start | bytes 589832 | tf_op jit(solution)/shard_map/ppermute | solution.py:162
  102.4 1.0 copy_bitcast_fusion
  103.4 4.6 %collective-permute-done.18 = bf16[2,2,192,128]{3,2,1,0:T(8,128)(2,1)S(1)} collective-permute-done((bf16[2,2,192,128]{3,2,1,0:T(8,128)(2,1)S(1)}, bf16[2,2,192,128]{3,2,1,0:T(8,128)(2,1)S(1)}, u32[]{:S(2)}, u32[]{:S(2)}) %collective-permute-start.18) | collective-permute-done | bytes 196640 | tf_op jit(solution)/shard_map/ppermute | solution.py:162
  108.1 0.2 fusion.8
  108.3 0.7 copy.13
  109.0 0.7 copy.14
  (37 shorter events, 0.4 us)
Async XLA Ops:
  0.6 28.2 %copy-start = (bf16[192,16,128]{2,1,0:T(8,128)(2,1)S(1)}, bf16[192,16,128]{2,1,0:T(8,128)(2,1)}, u32[]{:S(2)}) copy-start(bf16[192,16,128]{2,1,0:T(8,128)(2,1)} %param.5) | copy-start | bytes 2359300
  0.6 28.2 %copy-start.17 = (bf16[192,16,128]{2,1,0:T(8,128)(2,1)S(1)}, bf16[192,16,128]{2,1,0:T(8,128)(2,1)}, u32[]{:S(2)}) copy-start(bf16[192,16,128]{2,1,0:T(8,128)(2,1)} %param.8) | copy-start | bytes 2359300
  1.8 10.4 %collective-permute-start = (bf16[2,2,192,128]{3,2,1,0:T(8,128)(2,1)S(1)}, bf16[2,2,192,128]{3,2,1,0:T(8,128)(2,1)S(1)}, u32[]{:S(2)}, u32[]{:S(2)}) collective-permute-start(bf16[2,2,192,128]{3,2,1,0:T(8,128)(2,1)S(1)} %maximum_bitcast_fusion.refs_4_), channel_id=1, source_target_pairs={{0,8},{2,10},{4,12},{6,14},{8,16},{10,18},{12,20},{14,22},{16,24},... | collective-permute-start | bytes 589832 | tf_op jit(solution)/shard_map/ppermute | solution.py:162
  5.3 13.0 %collective-permute-start.1 = (bf16[2,2,192,128]{3,2,1,0:T(8,128)(2,1)S(1)}, bf16[2,2,192,128]{3,2,1,0:T(8,128)(2,1)S(1)}, u32[]{:S(2)}, u32[]{:S(2)}) collective-permute-start(bf16[2,2,192,128]{3,2,1,0:T(8,128)(2,1)S(1)} %maximum_bitcast_fusion.refs_4_), channel_id=1, source_target_pairs={{0,2},{4,6},{8,10},{12,14},{16,18},{20,22},{24,26},{28,30},{1,3},{... | collective-permute-start | bytes 589832 | tf_op jit(solution)/shard_map/ppermute | solution.py:162
  8.7 10.2 %collective-permute-start.2 = (bf16[2,2,192,128]{3,2,1,0:T(8,128)(2,1)S(1)}, bf16[2,2,192,128]{3,2,1,0:T(8,128)(2,1)S(1)}, u32[]{:S(2)}, u32[]{:S(2)}) collective-permute-start(bf16[2,2,192,128]{3,2,1,0:T(8,128)(2,1)S(1)} %maximum_bitcast_fusion.refs_4_), channel_id=1, source_target_pairs={{0,4},{2,6},{8,12},{10,14},{16,20},{18,22},{24,28},{26,30},{1,5},{... | collective-permute-start | bytes 589832 | tf_op jit(solution)/shard_map/ppermute | solution.py:162
  12.1 9.6 %collective-permute-start.4 = (bf16[2,2,192,128]{3,2,1,0:T(8,128)(2,1)S(1)}, bf16[2,2,192,128]{3,2,1,0:T(8,128)(2,1)}, u32[]{:S(2)}, u32[]{:S(2)}) collective-permute-start(bf16[2,2,192,128]{3,2,1,0:T(8,128)(2,1)S(1)} %collective-permute-done.refs_5_), channel_id=1, source_target_pairs={{0,8},{2,10},{4,12},{6,14},{8,16},{10,18},{12,20},{14,22},{16,24},... | collective-permute-start | bytes 589832 | tf_op jit(solution)/shard_map/ppermute | solution.py:162
  14.1 9.4 %collective-permute-start.3 = (bf16[2,2,192,128]{3,2,1,0:T(8,128)(2,1)S(1)}, bf16[2,2,192,128]{3,2,1,0:T(8,128)(2,1)S(1)}, u32[]{:S(2)}, u32[]{:S(2)}) collective-permute-start(bf16[2,2,192,128]{3,2,1,0:T(8,128)(2,1)S(1)} %maximum_bitcast_fusion.refs_4_), channel_id=1, source_target_pairs={{0,6},{2,4},{8,14},{10,12},{16,22},{18,20},{24,30},{26,28},{1,7},{... | collective-permute-start | bytes 589832 | tf_op jit(solution)/shard_map/ppermute | solution.py:162
  18.2 9.4 %collective-permute-start.10 = (bf16[2,2,192,128]{3,2,1,0:T(8,128)(2,1)S(1)}, bf16[2,2,192,128]{3,2,1,0:T(8,128)(2,1)S(1)}, u32[]{:S(2)}, u32[]{:S(2)}) collective-permute-start(bf16[2,2,192,128]{3,2,1,0:T(8,128)(2,1)S(1)} %collective-permute-done.refs_5_), channel_id=1, source_target_pairs={{0,6},{2,4},{4,2},{6,0},{8,14},{10,12},{12,10},{14,8},{16,22},{18,... | collective-permute-start | bytes 589832 | tf_op jit(solution)/shard_map/ppermute | solution.py:162
  18.3 10.9 %copy-start.1 = (bf16[2,2,192,128]{3,2,1,0:T(8,128)(2,1)}, bf16[2,2,192,128]{3,2,1,0:T(8,128)(2,1)S(1)}, u32[]{:S(2)}) copy-start(bf16[2,2,192,128]{3,2,1,0:T(8,128)(2,1)S(1)} %collective-permute-done.1.refs_6_) | copy-start | bytes 589828
  18.3 14.6 %collective-permute-start.8 = (bf16[2,2,192,128]{3,2,1,0:T(8,128)(2,1)S(1)}, bf16[2,2,192,128]{3,2,1,0:T(8,128)(2,1)}, u32[]{:S(2)}, u32[]{:S(2)}) collective-permute-start(bf16[2,2,192,128]{3,2,1,0:T(8,128)(2,1)S(1)} %collective-permute-done.refs_5_), channel_id=1, source_target_pairs={{0,2},{2,0},{4,6},{6,4},{8,10},{10,8},{12,14},{14,12},{16,18},{18,... | collective-permute-start | bytes 589832 | tf_op jit(solution)/shard_map/ppermute | solution.py:162
  18.9 10.3 %copy-start.3 = (bf16[2,2,192,128]{3,2,1,0:T(8,128)(2,1)}, bf16[2,2,192,128]{3,2,1,0:T(8,128)(2,1)S(1)}, u32[]{:S(2)}) copy-start(bf16[2,2,192,128]{3,2,1,0:T(8,128)(2,1)S(1)} %collective-permute-done.2.refs_7_) | copy-start | bytes 589828
  18.9 14.0 %collective-permute-start.9 = (bf16[2,2,192,128]{3,2,1,0:T(8,128)(2,1)S(1)}, bf16[2,2,192,128]{3,2,1,0:T(8,128)(2,1)}, u32[]{:S(2)}, u32[]{:S(2)}) collective-permute-start(bf16[2,2,192,128]{3,2,1,0:T(8,128)(2,1)S(1)} %collective-permute-done.refs_5_), channel_id=1, source_target_pairs={{0,4},{2,6},{4,0},{6,2},{8,12},{10,14},{12,8},{14,10},{16,20},{18,... | collective-permute-start | bytes 589832 | tf_op jit(solution)/shard_map/ppermute | solution.py:162
  21.7 13.2 %collective-permute-start.5 = (bf16[2,2,192,128]{3,2,1,0:T(8,128)(2,1)}, bf16[2,2,192,128]{3,2,1,0:T(8,128)(2,1)}, u32[]{:S(2)}, u32[]{:S(2)}) collective-permute-start(bf16[2,2,192,128]{3,2,1,0:T(8,128)(2,1)} %collective-permute-done.4), channel_id=1, source_target_pairs={{2,0},{6,4},{10,8},{14,12},{18,16},{22,20},{26,24},{30,28},{3,1},{... | collective-permute-start | bytes 589832 | tf_op jit(solution)/shard_map/ppermute | solution.py:162
  23.5 5.7 %copy-start.5 = (bf16[2,2,192,128]{3,2,1,0:T(8,128)(2,1)}, bf16[2,2,192,128]{3,2,1,0:T(8,128)(2,1)S(1)}, u32[]{:S(2)}) copy-start(bf16[2,2,192,128]{3,2,1,0:T(8,128)(2,1)S(1)} %collective-permute-done.3.refs_8_) | copy-start | bytes 589828
  23.5 11.5 %collective-permute-start.6 = (bf16[2,2,192,128]{3,2,1,0:T(8,128)(2,1)}, bf16[2,2,192,128]{3,2,1,0:T(8,128)(2,1)}, u32[]{:S(2)}, u32[]{:S(2)}) collective-permute-start(bf16[2,2,192,128]{3,2,1,0:T(8,128)(2,1)} %collective-permute-done.4), channel_id=1, source_target_pairs={{4,0},{6,2},{12,8},{14,10},{20,16},{22,18},{28,24},{30,26},{5,1},{... | collective-permute-start | bytes 589832 | tf_op jit(solution)/shard_map/ppermute | solution.py:162
  27.5 1.6 %copy-start.7 = (bf16[2,2,192,128]{3,2,1,0:T(8,128)(2,1)}, bf16[2,2,192,128]{3,2,1,0:T(8,128)(2,1)S(1)}, u32[]{:S(2)}) copy-start(bf16[2,2,192,128]{3,2,1,0:T(8,128)(2,1)S(1)} %collective-permute-done.10.refs_14_) | copy-start | bytes 589828
  27.5 9.6 %collective-permute-start.7 = (bf16[2,2,192,128]{3,2,1,0:T(8,128)(2,1)}, bf16[2,2,192,128]{3,2,1,0:T(8,128)(2,1)}, u32[]{:S(2)}, u32[]{:S(2)}) collective-permute-start(bf16[2,2,192,128]{3,2,1,0:T(8,128)(2,1)} %collective-permute-done.4), channel_id=1, source_target_pairs={{4,2},{6,0},{12,10},{14,8},{20,18},{22,16},{28,26},{30,24},{5,3},{... | collective-permute-start | bytes 589832 | tf_op jit(solution)/shard_map/ppermute | solution.py:162
  37.1 0.7 copy-start.13
  37.8 0.9 copy-start.2
  38.7 0.9 copy-start.4
  39.6 0.9 copy-start.6
  40.6 0.9 copy-start.8
  69.2 0.7 copy-start.9
  69.9 0.7 copy-start.11
  70.5 0.7 copy-start.14
  71.2 0.7 copy-start.15
  71.9 0.7 copy-start.16
  72.6 10.2 %collective-permute-start.11 = (bf16[2,2,192,128]{3,2,1,0:T(8,128)(2,1)}, bf16[2,2,192,128]{3,2,1,0:T(8,128)(2,1)S(1)}, u32[]{:S(2)}, u32[]{:S(2)}) collective-permute-start(bf16[2,2,192,128]{3,2,1,0:T(8,128)(2,1)} %get-tuple-element.14), channel_id=1, source_target_pairs={{0,2},{2,0},{4,6},{6,4},{8,10},{10,8},{12,14},{14,12},{16,18},{18,... | collective-permute-start | bytes 589832 | tf_op jit(solution)/shard_map/ppermute | solution.py:162
  77.1 11.3 %collective-permute-start.12 = (bf16[2,2,192,128]{3,2,1,0:T(8,128)(2,1)}, bf16[2,2,192,128]{3,2,1,0:T(8,128)(2,1)S(1)}, u32[]{:S(2)}, u32[]{:S(2)}) collective-permute-start(bf16[2,2,192,128]{3,2,1,0:T(8,128)(2,1)} %get-tuple-element.15), channel_id=1, source_target_pairs={{0,4},{2,6},{4,0},{6,2},{8,12},{10,14},{12,8},{14,10},{16,20},{18,... | collective-permute-start | bytes 589832 | tf_op jit(solution)/shard_map/ppermute | solution.py:162
  79.2 11.7 %collective-permute-start.13 = (bf16[2,2,192,128]{3,2,1,0:T(8,128)(2,1)}, bf16[2,2,192,128]{3,2,1,0:T(8,128)(2,1)S(1)}, u32[]{:S(2)}, u32[]{:S(2)}) collective-permute-start(bf16[2,2,192,128]{3,2,1,0:T(8,128)(2,1)} %get-tuple-element.16), channel_id=1, source_target_pairs={{0,6},{2,4},{4,2},{6,0},{8,14},{10,12},{12,10},{14,8},{16,22},{18,... | collective-permute-start | bytes 589832 | tf_op jit(solution)/shard_map/ppermute | solution.py:162
  80.6 12.3 %collective-permute-start.14 = (bf16[2,2,192,128]{3,2,1,0:T(8,128)(2,1)}, bf16[2,2,192,128]{3,2,1,0:T(8,128)(2,1)S(1)}, u32[]{:S(2)}, u32[]{:S(2)}) collective-permute-start(bf16[2,2,192,128]{3,2,1,0:T(8,128)(2,1)} %copy-done.16), channel_id=1, source_target_pairs={{0,2},{2,0},{4,6},{6,4},{8,10},{10,8},{12,14},{14,12},{16,18},{18,... | collective-permute-start | bytes 589832 | tf_op jit(solution)/shard_map/ppermute | solution.py:162
  81.2 12.7 %collective-permute-start.15 = (bf16[2,2,192,128]{3,2,1,0:T(8,128)(2,1)}, bf16[2,2,192,128]{3,2,1,0:T(8,128)(2,1)S(1)}, u32[]{:S(2)}, u32[]{:S(2)}) collective-permute-start(bf16[2,2,192,128]{3,2,1,0:T(8,128)(2,1)} %copy-done.15), channel_id=1, source_target_pairs={{0,4},{2,6},{4,0},{6,2},{8,12},{10,14},{12,8},{14,10},{16,20},{18,... | collective-permute-start | bytes 589832 | tf_op jit(solution)/shard_map/ppermute | solution.py:162
  82.8 17.5 %copy-start.12 = (bf16[2,2,192,128]{3,2,1,0:T(8,128)(2,1)S(1)}, bf16[2,2,192,128]{3,2,1,0:T(8,128)(2,1)}, u32[]{:S(2)}) copy-start(bf16[2,2,192,128]{3,2,1,0:T(8,128)(2,1)} %copy-done.11) | copy-start | bytes 589828
  82.8 13.0 %collective-permute-start.16 = (bf16[2,2,192,128]{3,2,1,0:T(8,128)(2,1)}, bf16[2,2,192,128]{3,2,1,0:T(8,128)(2,1)S(1)}, u32[]{:S(2)}, u32[]{:S(2)}) collective-permute-start(bf16[2,2,192,128]{3,2,1,0:T(8,128)(2,1)} %copy-done.14), channel_id=1, source_target_pairs={{0,6},{2,4},{4,2},{6,0},{8,14},{10,12},{12,10},{14,8},{16,22},{18,... | collective-permute-start | bytes 589832 | tf_op jit(solution)/shard_map/ppermute | solution.py:162
  91.0 9.3 %collective-permute-start.17 = (bf16[2,2,192,128]{3,2,1,0:T(8,128)(2,1)S(1)}, bf16[2,2,192,128]{3,2,1,0:T(8,128)(2,1)S(1)}, u32[]{:S(2)}, u32[]{:S(2)}) collective-permute-start(bf16[2,2,192,128]{3,2,1,0:T(8,128)(2,1)S(1)} %fusion.7), channel_id=1, source_target_pairs={{8,0},{10,2},{12,4},{14,6},{16,8},{18,10},{20,12},{22,14},{24,16},... | collective-permute-start | bytes 589832 | tf_op jit(solution)/shard_map/ppermute | solution.py:162
  100.5 7.6 %collective-permute-start.18 = (bf16[2,2,192,128]{3,2,1,0:T(8,128)(2,1)S(1)}, bf16[2,2,192,128]{3,2,1,0:T(8,128)(2,1)S(1)}, u32[]{:S(2)}, u32[]{:S(2)}) collective-permute-start(bf16[2,2,192,128]{3,2,1,0:T(8,128)(2,1)S(1)} %add_convert_fusion), channel_id=1, source_target_pairs={{8,0},{10,2},{12,4},{14,6},{16,8},{18,10},{20,12},{22,14},{24,16},... | collective-permute-start | bytes 589832 | tf_op jit(solution)/shard_map/ppermute | solution.py:162
  102.4 5.6 %copy-start.10 = (bf16[2,2,192,128]{3,2,1,0:T(8,128)(2,1)S(1)}, bf16[2,2,192,128]{3,2,1,0:T(8,128)(2,1)}, u32[]{:S(2)}) copy-start(bf16[2,2,192,128]{3,2,1,0:T(8,128)(2,1)} %copy-done.9) | copy-start | bytes 589828

commit v2 on v1

v2 whole, which is shorter than its diff:
```python
import functools
import math

import jax
import jax.numpy as jnp
from jax import lax
from jax.experimental import pallas as pl
from jax.experimental.pallas import tpu as pltpu
from jax.sharding import PartitionSpec as P

PLANE = 4
FLIPS = (1, 2, 3)
LOG2E = math.log2(math.e)
NEG_INIT = -1e30
NEG_DEAD = -2e30
CHUNK = 512

NT = (((1,), (1,)), ((), ()))
NN = (((1,), (0,)), ((), ()))
TN = (((0,), (0,)), ((), ()))
SMEM = pl.BlockSpec(memory_space=pltpu.SMEM)
VMEM = pl.BlockSpec(memory_space=pltpu.VMEM)


def mm(a, b, dims):
    return lax.dot_general(a, b, dims, preferred_element_type=jnp.float32)


def own_slot(me, lane):
    return me


def up_slot(me, lane):
    return me - PLANE


def upx_slot(flip, me, lane):
    return me - PLANE - lane + jnp.bitwise_xor(lane, flip)


def mix_slot(flip, me, lane):
    other = jnp.bitwise_xor(lane, flip)
    return me - lane + other - jnp.where(other < lane, 0, 2 * PLANE)


def mark_rows(place_ref, lens_ref, n_docs, stripe, heads_per, start_ref, pos_ref):
    me = place_ref[0]
    first_pos = me * stripe
    col = lax.broadcasted_iota(jnp.int32, start_ref.shape, 1)
    pos = first_pos + lax.div(col, heads_per)
    start = jnp.zeros(start_ref.shape, jnp.int32)
    end = jnp.int32(0)
    first_key = jnp.int32(0)
    for n in range(n_docs):
        end = end + lens_ref[n]
        start = jnp.maximum(start, jnp.where(pos >= end, end, 0))
        first_key = jnp.maximum(first_key, jnp.where(first_pos >= end, end, 0))
    start_ref[...] = start
    pos_ref[...] = pos
    return me, lax.rem(me, PLANE), first_key


def logits(keys, q_c, base, cs, start_ref, pos_ref, scale2):
    s = mm(keys, q_c, NT) * scale2
    kpos = base + lax.broadcasted_iota(jnp.int32, s.shape, 0)
    live = (kpos >= start_ref[:, cs]) & (kpos <= pos_ref[:, cs])
    return jnp.where(live, s, NEG_DEAD)


def stats_kernel(slots, heads_per, n_docs, first, last, *refs):
    n = len(slots)
    place_ref, lens_ref, q_ref, do_ref = refs[:4]
    kv_refs = refs[4 : 4 + n]
    refs = refs[4 + n :]
    if not first:
        m_in, l_in, d_in = refs[:3]
        refs = refs[3:]
    m_ref, l_ref, d_ref, start_ref, pos_ref = refs
    groups, cols, dim = q_ref.shape
    stripe = kv_refs[0].shape[2]
    scale2 = dim**-0.5 * LOG2E
    me, lane, first_key = mark_rows(place_ref, lens_ref, n_docs, stripe, heads_per, start_ref, pos_ref)
    if first:
        m_ref[...] = jnp.full_like(m_ref, NEG_INIT)
        l_ref[...] = jnp.zeros_like(l_ref)
        d_ref[...] = jnp.zeros_like(d_ref)
    else:
        m_ref[...] = m_in[...]
        l_ref[...] = l_in[...]
        d_ref[...] = d_in[...]
    for kv_ref, slot in zip(kv_refs, slots):
        at = slot(me, lane)

        @pl.when((at >= 0) & ((at + 1) * stripe > first_key))
        def _():
            base = at * stripe

            @pl.loop(0, groups)
            def _(g):
                keys, vals = kv_ref[0, g], kv_ref[1, g]
                for c in range(0, cols, CHUNK):
                    cs = pl.ds(c, CHUNK)
                    s = logits(keys, q_ref[g, cs, :], base, cs, start_ref, pos_ref, scale2)
                    gp = mm(vals, do_ref[g, cs, :], NT)
                    m_old = m_ref[g, :, cs]
                    m_new = jnp.maximum(m_old, jnp.max(s, axis=0, keepdims=True))
                    e = jnp.exp2(s - m_new)
                    fade = jnp.exp2(m_old - m_new)
                    m_ref[g, :, cs] = m_new
                    l_ref[g, :, cs] = l_ref[g, :, cs] * fade + jnp.sum(e, axis=0, keepdims=True)
                    d_ref[g, :, cs] = d_ref[g, :, cs] * fade + jnp.sum(e * gp, axis=0, keepdims=True)

    if last:
        d_ref[...] = d_ref[...] / l_ref[...]
        m_ref[...] = m_ref[...] + jnp.log2(l_ref[...])


def grad_kernel(slots, heads_per, n_docs, first, last, *refs):
    n = len(slots)
    place_ref, lens_ref, q_ref, do_ref, m_ref, d_ref = refs[:6]
    kv_refs = refs[6 : 6 + n]
    refs = refs[6 + n :]
    if not first:
        dq_in = refs[0]
        refs = refs[1:]
    part_refs = refs[:n]
    dq_out = refs[n]
    start_ref, pos_ref = refs[n + 1 : n + 3]
    groups, cols, dim = q_ref.shape
    stripe = kv_refs[0].shape[2]
    scale = dim**-0.5
    scale2 = scale * LOG2E
    me, lane, first_key = mark_rows(place_ref, lens_ref, n_docs, stripe, heads_per, start_ref, pos_ref)
    dqt = refs[n + 3] if last else dq_out
    if first:
        dqt[...] = jnp.zeros_like(dqt)
    else:
        dqt[...] = dq_in[...]
    for kv_ref, part_ref, slot in zip(kv_refs, part_refs, slots):
        at = slot(me, lane)
        live = (at >= 0) & ((at + 1) * stripe > first_key)

        @pl.when(live)
        def _():
            base = at * stripe

            @pl.loop(0, groups)
            def _(g):
                keys, vals = kv_ref[0, g], kv_ref[1, g]
                dk = jnp.zeros((stripe, dim), jnp.float32)
                dv = jnp.zeros((stripe, dim), jnp.float32)
                for c in range(0, cols, CHUNK):
                    cs = pl.ds(c, CHUNK)
                    q_c, do_c = q_ref[g, cs, :], do_ref[g, cs, :]
                    s = logits(keys, q_c, base, cs, start_ref, pos_ref, scale2)
                    gp = mm(vals, do_c, NT)
                    p = jnp.exp2(s - m_ref[g, :, cs])
                    ds = (p * (gp - d_ref[g, :, cs])).astype(jnp.bfloat16)
                    dv = dv + mm(p.astype(jnp.bfloat16), do_c, NN)
                    dk = dk + mm(ds, q_c, NN)
                    dqt[g, :, cs] = dqt[g, :, cs] + mm(keys, ds, TN)
                part_ref[0, g] = (dk * scale).astype(jnp.bfloat16)
                part_ref[1, g] = dv.astype(jnp.bfloat16)

        @pl.when(jnp.logical_not(live))
        def _():
            part_ref[...] = jnp.zeros_like(part_ref)

    if last:
        for g in range(groups):
            dq_out[g] = (dqt[g] * scale).T.astype(jnp.bfloat16)


def shards(queries, key_vectors, value_matrix, grad_out, doc_lengths):
    stripe, heads, dim = queries.shape
    groups = key_vectors.shape[1]
    heads_per = heads // groups
    cols = stripe * heads_per
    length = lax.axis_size("ctx")
    me = lax.axis_index("ctx").astype(jnp.int32)
    lane = lax.rem(me, PLANE)
    place = me[None]

    def send(array, to):
        pairs = [(i, to(i)) for i in range(length) if 0 <= to(i) < length]
        return lax.ppermute(array, "ctx", pairs)

    def columns(array):
        return array.reshape(stripe, groups, heads_per, dim).transpose(1, 0, 2, 3).reshape(groups, cols, dim)

    own = jnp.stack([key_vectors, value_matrix]).transpose(0, 2, 1, 3)
    q, do = columns(queries), columns(grad_out)
    piece = jax.ShapeDtypeStruct(own.shape, jnp.bfloat16)
    stat = jax.ShapeDtypeStruct((groups, 1, cols), jnp.float32)
    total = jax.ShapeDtypeStruct((groups, dim, cols), jnp.float32)
    row = pltpu.VMEM((1, cols), jnp.int32)
    n_docs = doc_lengths.shape[0]
    pair_flops = groups * stripe * cols * dim * 2

    def params(products, n):
        return dict(
            compiler_params=pltpu.CompilerParams(vmem_limit_bytes=20 << 20),
            cost_estimate=pl.CostEstimate(flops=products * n * pair_flops * 2, bytes_accessed=1 << 20, transcendentals=0),
        )

    def stats(slots, kvs, old=None, last=False):
        return pl.pallas_call(
            functools.partial(stats_kernel, slots, heads_per, n_docs, old is None, last),
            out_shape=[stat] * 3,
            in_specs=[SMEM, SMEM] + [VMEM] * (2 + len(kvs) + (0 if old is None else 3)),
            out_specs=[VMEM] * 3,
            scratch_shapes=[row, row],
            **params(2, len(kvs)),
        )(place, doc_lengths, q, do, *kvs, *(old or ()))

    def grads(slots, kvs, m, d, old=None, last=False):
        n = len(kvs)
        dq_shape = jax.ShapeDtypeStruct(q.shape, jnp.bfloat16) if last else total
        outs = pl.pallas_call(
            functools.partial(grad_kernel, slots, heads_per, n_docs, old is None, last),
            out_shape=[piece] * n + [dq_shape],
            in_specs=[SMEM, SMEM] + [VMEM] * (4 + n + (0 if old is None else 1)),
            out_specs=[VMEM] * (n + 1),
            scratch_shapes=[row, row] + ([pltpu.VMEM(total.shape, jnp.float32)] if last else []),
            **params(5, n),
        )(place, doc_lengths, q, do, m, d, *kvs, *(() if old is None else (old,)))
        return outs[:n], outs[n]

    upx_slots = [functools.partial(upx_slot, f) for f in FLIPS]
    mix_slots = [functools.partial(mix_slot, f) for f in FLIPS]
    other = [jnp.bitwise_xor(lane, f) for f in FLIPS]

    up = send(own, lambda i: i + PLANE)
    seen = stats([own_slot], [own])
    up, seen = lax.optimization_barrier((up, seen))
    up2 = send(up, lambda i: i + PLANE)
    upx = [send(up, lambda i, f=f: i ^ f) for f in FLIPS]
    seen = stats([up_slot], [up], seen)
    mix = [send(jnp.where(other[k] > lane, own, up2), lambda i, f=f: i ^ f) for k, f in enumerate(FLIPS)]
    seen = stats(upx_slots, upx, seen)
    m, _, d = stats(mix_slots, mix, seen, last=True)

    mix_parts, dq = grads(mix_slots, mix, m, d)
    mixed = [send(part, lambda i, f=f: i ^ f) for part, f in zip(mix_parts, FLIPS)]
    upx_parts, dq = grads(upx_slots, upx, m, d, dq)
    level = [send(part, lambda i, f=f: i ^ f) for part, f in zip(upx_parts, FLIPS)]
    (up_part, own_part), dq = grads([up_slot, own_slot], [up, own], m, d, dq, last=True)

    wide = [x.astype(jnp.float32) for x in mixed]
    far_sum = sum(jnp.where(other[k] < lane, wide[k], 0.0) for k in range(3))
    down2 = send(far_sum.astype(jnp.bfloat16), lambda i: i - PLANE).astype(jnp.float32)
    level_sum = up_part.astype(jnp.float32) + sum(x.astype(jnp.float32) for x in level) + down2
    down = send(level_sum.astype(jnp.bfloat16), lambda i: i - PLANE).astype(jnp.float32)
    mine = own_part.astype(jnp.float32) + sum(jnp.where(other[k] > lane, wide[k], 0.0) for k in range(3))
    kv_grad = (mine + down).astype(jnp.bfloat16).transpose(0, 2, 1, 3)
    dq = dq.reshape(groups, stripe, heads_per, dim).transpose(1, 0, 2, 3).reshape(stripe, heads, dim)
    return dq, kv_grad[0], kv_grad[1]


def solution(mesh):
    spec = P("ctx", "tp", None)
    return jax.shard_map(
        shards,
        mesh=mesh,
        in_specs=(spec, spec, spec, spec, P()),
        out_specs=(spec, spec, spec),
        check_vma=False,
    )
```

time: 110 us -> 80.9 us (0.74)
  waiting for transfers between devices: 27.7 us -> 10.1 us
  starting transfers between devices: 41.3 us -> 26.1 us
  Pallas kernels: 27.7 us -> 37.8 us
  local copies, waits for them, and re-layouts: 11.7 us -> 4.98 us
    ppermute x19 -> x16, waiting for transfers between devices: 27.7 us -> 10.1 us  [send(): return lax.ppermute(array, 'ctx', pairs)]
    ppermute x19 -> x16, starting transfers between devices: 41.3 us -> 26.1 us  [send(): return lax.ppermute(array, 'ctx', pairs)]
    pallas_call x1 -> x7, Pallas kernels: 27.7 us -> 37.8 us  [the longest x3 22.3 us: grads(): pl.pallas_call(functools.partial(grad_kernel, slots, heads_per, n_docs, o...]
    unnamed x38 -> x6, local copies, waits for them, and re-layouts: 9.28 us -> 1.5 us
    reshape x1, local copies, waits for them, and re-layouts: 0.27 us -> 1.41 us  [columns(): array.reshape(stripe, groups, heads_per, dim).transpose(1, 0, 2, 3)]
  transfers between devices with their start and end apart: 19 -> 16, of which waited for: 13 -> 5; matrix products, arithmetic and copies ran while one was open for 1% -> 3% of each run, Pallas kernels for 0% -> 30%
where the time goes in v2:
time: 80.9 us; the launch traced here: 80.4 us
  Pallas kernels  37.8 us (47%)
  starting transfers between devices  26.1 us (32%)
  waiting for transfers between devices  10.1 us (12%)
  local copies, waits for them, and re-layouts  4.98 us (6%)
  between operations  0.91 us (1%)
    ppermute x16, starting transfers between devices, send(): return lax.ppermute(array, 'ctx', pairs)  26.1 us
    pallas_call x3, Pallas kernels, grads(): pl.pallas_call(functools.partial(grad_kernel, slots, heads_per, n_docs, o...  22.3 us
    pallas_call x4, Pallas kernels, stats(): pl.pallas_call(functools.partial(stats_kernel, slots, heads_per, n_docs,...  15.4 us
    ppermute x16, waiting for transfers between devices, send(): return lax.ppermute(array, 'ctx', pairs)  10.1 us
  transfers between devices with their start and end apart: 16, of which 5 were waited for; matrix products, arithmetic and copies ran while one was open for 3% of the time, Pallas kernels for 30%

profile of v2, /device:TPU:16, one launch (start us, length us, event | category | flops | bytes accessed | tf_op | source)
XLA Modules:
  0.0 80.4 jit_solution(2867496804943406965)
XLA Ops:
  0.6 0.0 copy-start
  0.6 1.0 %copy_bitcast_fusion.3 = (bf16[1,192,2,128]{3,1,2,0:T(8,128)(2,1)S(1)}, bf16[1,192,2,128]{3,1,2,0:T(8,128)(2,1)S(1)}) fusion(bf16[192,2,128]{2,1,0:T(2,128)(2,1)} %param.7, bf16[192,2,128]{2,1,0:T(2,128)(2,1)} %param.6), kind=kLoop, calls=%fused_computation.25 | loop fusion | bytes 393216 | tf_op jit(solution)/shard_map/stack | solution.py:191
  1.7 0.0 copy-start.1
  1.7 3.5 %collective-permute-start = (bf16[2,2,192,128]{3,2,1,0:T(8,128)(2,1)S(1)}, bf16[2,2,192,128]{3,2,1,0:T(8,128)(2,1)S(1)}, u32[]{:S(2)}, u32[]{:S(2)}) collective-permute-start(bf16[2,2,192,128]{3,2,1,0:T(8,128)(2,1)S(1)} %maximum_bitcast_fusion.refs_4_.refs_7_), channel_id=1, source_target_pairs={{0,8},{2,10},{4,12},{6,14},{8,16},{10,18},{12,20},{14,22},{16,24},... | collective-permute-start | bytes 589832 | tf_op jit(solution)/shard_map/ppermute | solution.py:186
  5.2 1.4 %copy_bitcast_fusion.1 = (bf16[2,1536,128]{2,1,0:T(8,128)(2,1)S(1)}, bf16[2,1536,128]{2,1,0:T(8,128)(2,1)S(1)}) fusion(bf16[192,16,128]{2,1,0:T(8,128)(2,1)S(1)} %copy-done, bf16[192,16,128]{2,1,0:T(8,128)(2,1)} %param.8), kind=kLoop, calls=%fused_computation.1 | loop fusion | bytes 3145728 | tf_op jit(solution)/shard_map/reshape | solution.py:189
  6.7 2.1 %shard_map.76 = (f32[2,1,1536]{2,1,0:T(1,128)S(1)}, f32[2,1,1536]{2,1,0:T(1,128)S(1)}, f32[2,1,1536]{2,1,0:T(1,128)S(1)}) custom-call(s32[1]{0:T(128)} %bitcast.refs_0_, s32[8]{0:T(128)S(1)} %copy-done.1, bf16[2,1536,128]{2,1,0:T(8,128)(2,1)S(1)} %get-tuple-element.66.refs_2_, bf16[2,1536,128]{2,1,0:T(8,128)(2,1)S(1)} %get-tuple-element.65.refs_3_, ...), custom_call_target="tpu_custom_call" | custom-call | flops 603979776 | bytes 1048576 | tf_op jit(solution)/shard_map/pallas_call | solution.py:207
  8.8 1.5 %collective-permute-done.refs_4_.refs_6_ = bf16[2,2,192,128]{3,2,1,0:T(8,128)(2,1)S(1)} collective-permute-done((bf16[2,2,192,128]{3,2,1,0:T(8,128)(2,1)S(1)}, bf16[2,2,192,128]{3,2,1,0:T(8,128)(2,1)S(1)}, u32[]{:S(2)}, u32[]{:S(2)}) %collective-permute-start) | collective-permute-done | bytes 196640 | tf_op jit(solution)/shard_map/ppermute | solution.py:186
  10.3 3.5 %collective-permute-start.1 = (bf16[2,2,192,128]{3,2,1,0:T(8,128)(2,1)S(1)}, bf16[2,2,192,128]{3,2,1,0:T(8,128)(2,1)S(1)}, u32[]{:S(2)}, u32[]{:S(2)}) collective-permute-start(bf16[2,2,192,128]{3,2,1,0:T(8,128)(2,1)S(1)} %collective-permute-done.refs_4_.refs_6_), channel_id=1, source_target_pairs={{0,8},{2,10},{4,12},{6,14},{8,16},{10,18},{12,20},{14,22},{16,24},... | collective-permute-start | bytes 589832 | tf_op jit(solution)/shard_map/ppermute | solution.py:186
  13.8 2.5 %collective-permute-start.7 = (bf16[2,2,192,128]{3,2,1,0:T(8,128)(2,1)S(1)}, bf16[2,2,192,128]{3,2,1,0:T(8,128)(2,1)S(1)}, u32[]{:S(2)}, u32[]{:S(2)}) collective-permute-start(bf16[2,2,192,128]{3,2,1,0:T(8,128)(2,1)S(1)} %collective-permute-done.refs_4_.refs_6_), channel_id=1, source_target_pairs={{0,6},{2,4},{4,2},{6,0},{8,14},{10,12},{12,10},{14,8},{16,22},{18,... | collective-permute-start | bytes 589832 | tf_op jit(solution)/shard_map/ppermute | solution.py:186
  16.3 0.5 collective-permute-start.6
  16.8 0.5 collective-permute-start.5
  17.3 0.6 collective-permute-done.1
  18.0 2.5 %collective-permute-start.4 = (bf16[2,2,192,128]{3,2,1,0:T(8,128)(2,1)S(1)}, bf16[2,2,192,128]{3,2,1,0:T(8,128)(2,1)S(1)}, u32[]{:S(2)}, u32[]{:S(2)}) collective-permute-start(bf16[2,2,192,128]{3,2,1,0:T(8,128)(2,1)S(1)} %get-tuple-element.58), channel_id=1, source_target_pairs={{0,6},{2,4},{4,2},{6,0},{8,14},{10,12},{12,10},{14,8},{16,22},{18,... | collective-permute-start | bytes 589832 | tf_op jit(solution)/shard_map/ppermute | solution.py:186
  20.5 0.5 collective-permute-start.3
  21.0 1.3 %collective-permute-done.7.refs_6_.refs_8_ = bf16[2,2,192,128]{3,2,1,0:T(8,128)(2,1)S(1)} collective-permute-done((bf16[2,2,192,128]{3,2,1,0:T(8,128)(2,1)S(1)}, bf16[2,2,192,128]{3,2,1,0:T(8,128)(2,1)S(1)}, u32[]{:S(2)}, u32[]{:S(2)}) %collective-permute-start.7) | collective-permute-done | bytes 196640 | tf_op jit(solution)/shard_map/ppermute | solution.py:186
  22.3 1.7 %collective-permute-start.2 = (bf16[2,2,192,128]{3,2,1,0:T(8,128)(2,1)S(1)}, bf16[2,2,192,128]{3,2,1,0:T(8,128)(2,1)S(1)}, u32[]{:S(2)}, u32[]{:S(2)}) collective-permute-start(bf16[2,2,192,128]{3,2,1,0:T(8,128)(2,1)S(1)} %get-tuple-element.60), channel_id=1, source_target_pairs={{0,2},{2,0},{4,6},{6,4},{8,10},{10,8},{12,14},{14,12},{16,18},{18,... | collective-permute-start | bytes 589832 | tf_op jit(solution)/shard_map/ppermute | solution.py:186
  24.0 2.1 %shard_map.77 = (f32[2,1,1536]{2,1,0:T(1,128)S(1)}, f32[2,1,1536]{2,1,0:T(1,128)S(1)}, f32[2,1,1536]{2,1,0:T(1,128)S(1)}) custom-call(s32[1]{0:T(128)} %bitcast.refs_0_, s32[8]{0:T(128)S(1)} %copy-done.1, bf16[2,1536,128]{2,1,0:T(8,128)(2,1)S(1)} %get-tuple-element.66.refs_2_, bf16[2,1536,128]{2,1,0:T(8,128)(2,1)S(1)} %get-tuple-element.65.refs_3_, ...), custom_call_target="tpu_custom_call" | custom-call | flops 603979776 | bytes 1048576 | tf_op jit(solution)/shard_map/pallas_call | solution.py:207
  26.2 2.1 %collective-permute-done.6.refs_5_.refs_7_ = bf16[2,2,192,128]{3,2,1,0:T(8,128)(2,1)S(1)} collective-permute-done((bf16[2,2,192,128]{3,2,1,0:T(8,128)(2,1)S(1)}, bf16[2,2,192,128]{3,2,1,0:T(8,128)(2,1)S(1)}, u32[]{:S(2)}, u32[]{:S(2)}) %collective-permute-start.6) | collective-permute-done | bytes 196640 | tf_op jit(solution)/shard_map/ppermute | solution.py:186
  28.3 0.0 collective-permute-done.5.refs_4_.refs_6_
  28.3 5.2 %shard_map.78 = (f32[2,1,1536]{2,1,0:T(1,128)S(1)}, f32[2,1,1536]{2,1,0:T(1,128)S(1)}, f32[2,1,1536]{2,1,0:T(1,128)S(1)}) custom-call(s32[1]{0:T(128)} %bitcast.refs_0_, s32[8]{0:T(128)S(1)} %copy-done.1, bf16[2,1536,128]{2,1,0:T(8,128)(2,1)S(1)} %get-tuple-element.66.refs_2_, bf16[2,1536,128]{2,1,0:T(8,128)(2,1)S(1)} %get-tuple-element.65.refs_3_, ...), custom_call_target="tpu_custom_call" | custom-call | flops 1811939328 | bytes 1048576 | tf_op jit(solution)/shard_map/pallas_call | solution.py:207
  33.5 0.0 collective-permute-done.4.refs_6_.refs_8_
  33.5 0.0 collective-permute-done.3.refs_5_.refs_7_
  33.5 0.0 collective-permute-done.2.refs_4_.refs_6_
  33.5 5.9 %shard_map.79 = (f32[2,1,1536]{2,1,0:T(1,128)S(1)}, f32[2,1,1536]{2,1,0:T(1,128)}, f32[2,1,1536]{2,1,0:T(1,128)S(1)}) custom-call(s32[1]{0:T(128)} %bitcast.refs_0_, s32[8]{0:T(128)S(1)} %copy-done.1, bf16[2,1536,128]{2,1,0:T(8,128)(2,1)S(1)} %get-tuple-element.66.refs_2_, bf16[2,1536,128]{2,1,0:T(8,128)(2,1)S(1)} %get-tuple-element.65.refs_3_, ...), custom_call_target="tpu_custom_call" | custom-call | flops 1811939328 | bytes 1048576 | tf_op jit(solution)/shard_map/pallas_call | solution.py:207
  39.4 8.1 %shard_map.80 = (bf16[2,2,192,128]{3,2,1,0:T(8,128)(2,1)S(1)}, bf16[2,2,192,128]{3,2,1,0:T(8,128)(2,1)S(1)}, bf16[2,2,192,128]{3,2,1,0:T(8,128)(2,1)S(1)}, f32[2,128,1536]{2,1,0:T(8,128)S(1)}) custom-call(s32[1]{0:T(128)} %bitcast.refs_0_, s32[8]{0:T(128)S(1)} %copy-done.1, bf16[2,1536,128]{2,1,0:T(8,128)(2,1)S(1)} %get-tuple-element.66.refs_2_, ...), custom_call_target="tpu_custom_call" | custom-call | flops 4529848320 | bytes 1048576 | tf_op jit(solution)/shard_map/pallas_call | solution.py:219
  47.5 0.1 collective-permute-start.8
  47.6 0.1 collective-permute-start.9
  47.7 3.4 %collective-permute-start.10 = (bf16[2,2,192,128]{3,2,1,0:T(8,128)(2,1)S(1)}, bf16[2,2,192,128]{3,2,1,0:T(8,128)(2,1)S(1)}, u32[]{:S(2)}, u32[]{:S(2)}) collective-permute-start(bf16[2,2,192,128]{3,2,1,0:T(8,128)(2,1)S(1)} %get-tuple-element.50), channel_id=1, source_target_pairs={{0,6},{2,4},{4,2},{6,0},{8,14},{10,12},{12,10},{14,8},{16,22},{18,... | collective-permute-start | bytes 589832 | tf_op jit(solution)/shard_map/ppermute | solution.py:186
  51.1 8.3 %shard_map.81 = (bf16[2,2,192,128]{3,2,1,0:T(8,128)(2,1)S(1)}, bf16[2,2,192,128]{3,2,1,0:T(8,128)(2,1)S(1)}, bf16[2,2,192,128]{3,2,1,0:T(8,128)(2,1)S(1)}, f32[2,128,1536]{2,1,0:T(8,128)S(1)}) custom-call(s32[1]{0:T(128)} %bitcast.refs_0_, s32[8]{0:T(128)S(1)} %copy-done.1, bf16[2,1536,128]{2,1,0:T(8,128)(2,1)S(1)} %get-tuple-element.66.refs_2_, ...), custom_call_target="tpu_custom_call" | custom-call | flops 4529848320 | bytes 1048576 | tf_op jit(solution)/shard_map/pallas_call | solution.py:219
  59.4 0.1 collective-permute-start.11
  59.4 0.1 collective-permute-start.12
  59.5 0.0 collective-permute-done.8
  59.5 3.4 %collective-permute-start.13 = (bf16[2,2,192,128]{3,2,1,0:T(8,128)(2,1)S(1)}, bf16[2,2,192,128]{3,2,1,0:T(8,128)(2,1)S(1)}, u32[]{:S(2)}, u32[]{:S(2)}) collective-permute-start(bf16[2,2,192,128]{3,2,1,0:T(8,128)(2,1)S(1)} %get-tuple-element.54), channel_id=1, source_target_pairs={{0,6},{2,4},{4,2},{6,0},{8,14},{10,12},{12,10},{14,8},{16,22},{18,... | collective-permute-start | bytes 589832 | tf_op jit(solution)/shard_map/ppermute | solution.py:186
  62.9 0.0 collective-permute-done.9
  62.9 0.0 collective-permute-done.10
  62.9 0.1 fusion.7
  63.1 1.9 %collective-permute-start.14 = (bf16[2,2,192,128]{3,2,1,0:T(8,128)(2,1)S(1)}, bf16[2,2,192,128]{3,2,1,0:T(8,128)(2,1)S(1)}, u32[]{:S(2)}, u32[]{:S(2)}) collective-permute-start(bf16[2,2,192,128]{3,2,1,0:T(8,128)(2,1)S(1)} %fusion.7), channel_id=1, source_target_pairs={{8,0},{10,2},{12,4},{14,6},{16,8},{18,10},{20,12},{22,14},{24,16},... | collective-permute-start | bytes 589832 | tf_op jit(solution)/shard_map/ppermute | solution.py:186
  65.0 6.0 %shard_map.82 = (bf16[2,2,192,128]{3,2,1,0:T(8,128)(2,1)S(1)}, bf16[2,2,192,128]{3,2,1,0:T(8,128)(2,1)S(1)}, bf16[2,1536,128]{2,1,0:T(8,128)(2,1)S(1)}) custom-call(s32[1]{0:T(128)} %bitcast.refs_0_, s32[8]{0:T(128)S(1)} %copy-done.1, bf16[2,1536,128]{2,1,0:T(8,128)(2,1)S(1)} %get-tuple-element.66.refs_2_, ...), custom_call_target="tpu_custom_call" | custom-call | flops 3019898880 | bytes 1048576 | tf_op jit(solution)/shard_map/pallas_call | solution.py:219
  71.0 0.0 collective-permute-done.11
  71.0 0.0 collective-permute-done.13
  71.0 0.0 collective-permute-done.14
  71.0 0.1 add_convert_fusion
  71.1 1.9 %collective-permute-start.15 = (bf16[2,2,192,128]{3,2,1,0:T(8,128)(2,1)S(1)}, bf16[2,2,192,128]{3,2,1,0:T(8,128)(2,1)S(1)}, u32[]{:S(2)}, u32[]{:S(2)}) collective-permute-start(bf16[2,2,192,128]{3,2,1,0:T(8,128)(2,1)S(1)} %add_convert_fusion), channel_id=1, source_target_pairs={{8,0},{10,2},{12,4},{14,6},{16,8},{18,10},{20,12},{22,14},{24,16},... | collective-permute-start | bytes 589832 | tf_op jit(solution)/shard_map/ppermute | solution.py:186
  73.1 1.0 %copy_bitcast_fusion = bf16[192,16,128]{2,1,0:T(8,128)(2,1)} fusion(bf16[2,1536,128]{2,1,0:T(8,128)(2,1)S(1)} %get-tuple-element.46), kind=kLoop, calls=%fused_computation | loop fusion | bytes 1572864 | tf_op jit(solution)/shard_map/reshape | solution.py:256
  74.1 4.6 %collective-permute-done.15 = bf16[2,2,192,128]{3,2,1,0:T(8,128)(2,1)S(1)} collective-permute-done((bf16[2,2,192,128]{3,2,1,0:T(8,128)(2,1)S(1)}, bf16[2,2,192,128]{3,2,1,0:T(8,128)(2,1)S(1)}, u32[]{:S(2)}, u32[]{:S(2)}) %collective-permute-start.15) | collective-permute-done | bytes 196640 | tf_op jit(solution)/shard_map/ppermute | solution.py:186
  78.7 0.2 fusion.8
  78.9 0.7 copy.14
  79.6 0.7 copy.13
  (6 shorter events, 0.1 us)
Async XLA Ops:
  0.6 4.6 %copy-start = (bf16[192,16,128]{2,1,0:T(8,128)(2,1)S(1)}, bf16[192,16,128]{2,1,0:T(8,128)(2,1)}, u32[]{:S(2)}) copy-start(bf16[192,16,128]{2,1,0:T(8,128)(2,1)} %param.5) | copy-start | bytes 2359300
  1.7 4.9 %copy-start.1 = (s32[8]{0:T(128)S(1)}, s32[8]{0:T(128)}, u32[]{:S(2)}) copy-start(s32[8]{0:T(128)} %refs_1_.13) | copy-start | bytes 100
  1.7 8.5 %collective-permute-start = (bf16[2,2,192,128]{3,2,1,0:T(8,128)(2,1)S(1)}, bf16[2,2,192,128]{3,2,1,0:T(8,128)(2,1)S(1)}, u32[]{:S(2)}, u32[]{:S(2)}) collective-permute-start(bf16[2,2,192,128]{3,2,1,0:T(8,128)(2,1)S(1)} %maximum_bitcast_fusion.refs_4_.refs_7_), channel_id=1, source_target_pairs={{0,8},{2,10},{4,12},{6,14},{8,16},{10,18},{12,20},{14,22},{16,24},... | collective-permute-start | bytes 589832 | tf_op jit(solution)/shard_map/ppermute | solution.py:186
  10.3 7.7 %collective-permute-start.1 = (bf16[2,2,192,128]{3,2,1,0:T(8,128)(2,1)S(1)}, bf16[2,2,192,128]{3,2,1,0:T(8,128)(2,1)S(1)}, u32[]{:S(2)}, u32[]{:S(2)}) collective-permute-start(bf16[2,2,192,128]{3,2,1,0:T(8,128)(2,1)S(1)} %collective-permute-done.refs_4_.refs_6_), channel_id=1, source_target_pairs={{0,8},{2,10},{4,12},{6,14},{8,16},{10,18},{12,20},{14,22},{16,24},... | collective-permute-start | bytes 589832 | tf_op jit(solution)/shard_map/ppermute | solution.py:186
  13.8 8.6 %collective-permute-start.7 = (bf16[2,2,192,128]{3,2,1,0:T(8,128)(2,1)S(1)}, bf16[2,2,192,128]{3,2,1,0:T(8,128)(2,1)S(1)}, u32[]{:S(2)}, u32[]{:S(2)}) collective-permute-start(bf16[2,2,192,128]{3,2,1,0:T(8,128)(2,1)S(1)} %collective-permute-done.refs_4_.refs_6_), channel_id=1, source_target_pairs={{0,6},{2,4},{4,2},{6,0},{8,14},{10,12},{12,10},{14,8},{16,22},{18,... | collective-permute-start | bytes 589832 | tf_op jit(solution)/shard_map/ppermute | solution.py:186
  16.3 12.0 %collective-permute-start.6 = (bf16[2,2,192,128]{3,2,1,0:T(8,128)(2,1)S(1)}, bf16[2,2,192,128]{3,2,1,0:T(8,128)(2,1)S(1)}, u32[]{:S(2)}, u32[]{:S(2)}) collective-permute-start(bf16[2,2,192,128]{3,2,1,0:T(8,128)(2,1)S(1)} %collective-permute-done.refs_4_.refs_6_), channel_id=1, source_target_pairs={{0,4},{2,6},{4,0},{6,2},{8,12},{10,14},{12,8},{14,10},{16,20},{18,... | collective-permute-start | bytes 589832 | tf_op jit(solution)/shard_map/ppermute | solution.py:186
  16.8 11.5 %collective-permute-start.5 = (bf16[2,2,192,128]{3,2,1,0:T(8,128)(2,1)S(1)}, bf16[2,2,192,128]{3,2,1,0:T(8,128)(2,1)S(1)}, u32[]{:S(2)}, u32[]{:S(2)}) collective-permute-start(bf16[2,2,192,128]{3,2,1,0:T(8,128)(2,1)S(1)} %collective-permute-done.refs_4_.refs_6_), channel_id=1, source_target_pairs={{0,2},{2,0},{4,6},{6,4},{8,10},{10,8},{12,14},{14,12},{16,18},{18,... | collective-permute-start | bytes 589832 | tf_op jit(solution)/shard_map/ppermute | solution.py:186
  18.0 15.5 %collective-permute-start.4 = (bf16[2,2,192,128]{3,2,1,0:T(8,128)(2,1)S(1)}, bf16[2,2,192,128]{3,2,1,0:T(8,128)(2,1)S(1)}, u32[]{:S(2)}, u32[]{:S(2)}) collective-permute-start(bf16[2,2,192,128]{3,2,1,0:T(8,128)(2,1)S(1)} %get-tuple-element.58), channel_id=1, source_target_pairs={{0,6},{2,4},{4,2},{6,0},{8,14},{10,12},{12,10},{14,8},{16,22},{18,... | collective-permute-start | bytes 589832 | tf_op jit(solution)/shard_map/ppermute | solution.py:186
  20.5 13.0 %collective-permute-start.3 = (bf16[2,2,192,128]{3,2,1,0:T(8,128)(2,1)S(1)}, bf16[2,2,192,128]{3,2,1,0:T(8,128)(2,1)S(1)}, u32[]{:S(2)}, u32[]{:S(2)}) collective-permute-start(bf16[2,2,192,128]{3,2,1,0:T(8,128)(2,1)S(1)} %get-tuple-element.59), channel_id=1, source_target_pairs={{0,4},{2,6},{4,0},{6,2},{8,12},{10,14},{12,8},{14,10},{16,20},{18,... | collective-permute-start | bytes 589832 | tf_op jit(solution)/shard_map/ppermute | solution.py:186
  22.3 11.2 %collective-permute-start.2 = (bf16[2,2,192,128]{3,2,1,0:T(8,128)(2,1)S(1)}, bf16[2,2,192,128]{3,2,1,0:T(8,128)(2,1)S(1)}, u32[]{:S(2)}, u32[]{:S(2)}) collective-permute-start(bf16[2,2,192,128]{3,2,1,0:T(8,128)(2,1)S(1)} %get-tuple-element.60), channel_id=1, source_target_pairs={{0,2},{2,0},{4,6},{6,4},{8,10},{10,8},{12,14},{14,12},{16,18},{18,... | collective-permute-start | bytes 589832 | tf_op jit(solution)/shard_map/ppermute | solution.py:186
  47.5 12.0 %collective-permute-start.8 = (bf16[2,2,192,128]{3,2,1,0:T(8,128)(2,1)S(1)}, bf16[2,2,192,128]{3,2,1,0:T(8,128)(2,1)S(1)}, u32[]{:S(2)}, u32[]{:S(2)}) collective-permute-start(bf16[2,2,192,128]{3,2,1,0:T(8,128)(2,1)S(1)} %get-tuple-element.48), channel_id=1, source_target_pairs={{0,2},{2,0},{4,6},{6,4},{8,10},{10,8},{12,14},{14,12},{16,18},{18,... | collective-permute-start | bytes 589832 | tf_op jit(solution)/shard_map/ppermute | solution.py:186
  47.6 15.3 %collective-permute-start.9 = (bf16[2,2,192,128]{3,2,1,0:T(8,128)(2,1)S(1)}, bf16[2,2,192,128]{3,2,1,0:T(8,128)(2,1)S(1)}, u32[]{:S(2)}, u32[]{:S(2)}) collective-permute-start(bf16[2,2,192,128]{3,2,1,0:T(8,128)(2,1)S(1)} %get-tuple-element.49), channel_id=1, source_target_pairs={{0,4},{2,6},{4,0},{6,2},{8,12},{10,14},{12,8},{14,10},{16,20},{18,... | collective-permute-start | bytes 589832 | tf_op jit(solution)/shard_map/ppermute | solution.py:186
  47.7 15.2 %collective-permute-start.10 = (bf16[2,2,192,128]{3,2,1,0:T(8,128)(2,1)S(1)}, bf16[2,2,192,128]{3,2,1,0:T(8,128)(2,1)S(1)}, u32[]{:S(2)}, u32[]{:S(2)}) collective-permute-start(bf16[2,2,192,128]{3,2,1,0:T(8,128)(2,1)S(1)} %get-tuple-element.50), channel_id=1, source_target_pairs={{0,6},{2,4},{4,2},{6,0},{8,14},{10,12},{12,10},{14,8},{16,22},{18,... | collective-permute-start | bytes 589832 | tf_op jit(solution)/shard_map/ppermute | solution.py:186
  59.4 11.6 %collective-permute-start.11 = (bf16[2,2,192,128]{3,2,1,0:T(8,128)(2,1)S(1)}, bf16[2,2,192,128]{3,2,1,0:T(8,128)(2,1)S(1)}, u32[]{:S(2)}, u32[]{:S(2)}) collective-permute-start(bf16[2,2,192,128]{3,2,1,0:T(8,128)(2,1)S(1)} %get-tuple-element.52), channel_id=1, source_target_pairs={{0,2},{2,0},{4,6},{6,4},{8,10},{10,8},{12,14},{14,12},{16,18},{18,... | collective-permute-start | bytes 589832 | tf_op jit(solution)/shard_map/ppermute | solution.py:186
  59.4 11.5 %collective-permute-start.12 = (bf16[2,2,192,128]{3,2,1,0:T(8,128)(2,1)S(1)}, bf16[2,2,192,128]{3,2,1,0:T(8,128)(2,1)S(1)}, u32[]{:S(2)}, u32[]{:S(2)}) collective-permute-start(bf16[2,2,192,128]{3,2,1,0:T(8,128)(2,1)S(1)} %get-tuple-element.53), channel_id=1, source_target_pairs={{0,4},{2,6},{4,0},{6,2},{8,12},{10,14},{12,8},{14,10},{16,20},{18,... | collective-permute-start | bytes 589832 | tf_op jit(solution)/shard_map/ppermute | solution.py:186
  59.5 11.4 %collective-permute-start.13 = (bf16[2,2,192,128]{3,2,1,0:T(8,128)(2,1)S(1)}, bf16[2,2,192,128]{3,2,1,0:T(8,128)(2,1)S(1)}, u32[]{:S(2)}, u32[]{:S(2)}) collective-permute-start(bf16[2,2,192,128]{3,2,1,0:T(8,128)(2,1)S(1)} %get-tuple-element.54), channel_id=1, source_target_pairs={{0,6},{2,4},{4,2},{6,0},{8,14},{10,12},{12,10},{14,8},{16,22},{18,... | collective-permute-start | bytes 589832 | tf_op jit(solution)/shard_map/ppermute | solution.py:186
  63.1 7.9 %collective-permute-start.14 = (bf16[2,2,192,128]{3,2,1,0:T(8,128)(2,1)S(1)}, bf16[2,2,192,128]{3,2,1,0:T(8,128)(2,1)S(1)}, u32[]{:S(2)}, u32[]{:S(2)}) collective-permute-start(bf16[2,2,192,128]{3,2,1,0:T(8,128)(2,1)S(1)} %fusion.7), channel_id=1, source_target_pairs={{8,0},{10,2},{12,4},{14,6},{16,8},{18,10},{20,12},{22,14},{24,16},... | collective-permute-start | bytes 589832 | tf_op jit(solution)/shard_map/ppermute | solution.py:186
  71.1 7.6 %collective-permute-start.15 = (bf16[2,2,192,128]{3,2,1,0:T(8,128)(2,1)S(1)}, bf16[2,2,192,128]{3,2,1,0:T(8,128)(2,1)S(1)}, u32[]{:S(2)}, u32[]{:S(2)}) collective-permute-start(bf16[2,2,192,128]{3,2,1,0:T(8,128)(2,1)S(1)} %add_convert_fusion), channel_id=1, source_target_pairs={{8,0},{10,2},{12,4},{14,6},{16,8},{18,10},{20,12},{22,14},{24,16},... | collective-permute-start | bytes 589832 | tf_op jit(solution)/shard_map/ppermute | solution.py:186

commit v3 on v2

--- a/solution.py
+++ b/solution.py
@@ -8,6 +8,7 @@
 from jax.experimental.pallas import tpu as pltpu
 from jax.sharding import PartitionSpec as P
 
+
 PLANE = 4
 FLIPS = (1, 2, 3)
 LOG2E = math.log2(math.e)
@@ -41,6 +42,12 @@
 def mix_slot(flip, me, lane):
     other = jnp.bitwise_xor(lane, flip)
     return me - lane + other - jnp.where(other < lane, 0, 2 * PLANE)
+
+
+def pieces(refs, slots):
+    for ref, held in zip(refs, slots):
+        for k, slot in enumerate(held):
+            yield ref.at[k], slot
 
 
 def mark_rows(place_ref, lens_ref, n_docs, stripe, heads_per, start_ref, pos_ref):
@@ -73,22 +80,17 @@
     kv_refs = refs[4 : 4 + n]
     refs = refs[4 + n :]
     if not first:
-        m_in, l_in, d_in = refs[:3]
         refs = refs[3:]
     m_ref, l_ref, d_ref, start_ref, pos_ref = refs
     groups, cols, dim = q_ref.shape
-    stripe = kv_refs[0].shape[2]
+    stripe = kv_refs[0].shape[-2]
     scale2 = dim**-0.5 * LOG2E
     me, lane, first_key = mark_rows(place_ref, lens_ref, n_docs, stripe, heads_per, start_ref, pos_ref)
     if first:
         m_ref[...] = jnp.full_like(m_ref, NEG_INIT)
         l_ref[...] = jnp.zeros_like(l_ref)
         d_ref[...] = jnp.zeros_like(d_ref)
-    else:
-        m_ref[...] = m_in[...]
-        l_ref[...] = l_in[...]
-        d_ref[...] = d_in[...]
-    for kv_ref, slot in zip(kv_refs, slots):
+    for kv_ref, slot in pieces(kv_refs, slots):
         at = slot(me, lane)
 
         @pl.when((at >= 0) & ((at + 1) * stripe > first_key))
@@ -121,22 +123,17 @@
     kv_refs = refs[6 : 6 + n]
     refs = refs[6 + n :]
     if not first:
-        dq_in = refs[0]
         refs = refs[1:]
     part_refs = refs[:n]
-    dq_out = refs[n]
-    start_ref, pos_ref = refs[n + 1 : n + 3]
+    dqt, start_ref, pos_ref = refs[n : n + 3] if not last else refs[n + 1 : n + 4]
     groups, cols, dim = q_ref.shape
-    stripe = kv_refs[0].shape[2]
+    stripe = kv_refs[0].shape[-2]
     scale = dim**-0.5
     scale2 = scale * LOG2E
     me, lane, first_key = mark_rows(place_ref, lens_ref, n_docs, stripe, heads_per, start_ref, pos_ref)
-    dqt = refs[n + 3] if last else dq_out
     if first:
         dqt[...] = jnp.zeros_like(dqt)
-    else:
-        dqt[...] = dq_in[...]
-    for kv_ref, part_ref, slot in zip(kv_refs, part_refs, slots):
+    for (kv_ref, slot), (part_ref, _) in zip(pieces(kv_refs, slots), pieces(part_refs, slots)):
         at = slot(me, lane)
         live = (at >= 0) & ((at + 1) * stripe > first_key)
 
@@ -168,7 +165,57 @@
 
     if last:
         for g in range(groups):
-            dq_out[g] = (dqt[g] * scale).T.astype(jnp.bfloat16)
+            refs[n][g] = (dqt[g] * scale).T.astype(jnp.bfloat16)
+
+
+def pack_kernel(k_ref, v_ref, own_ref, wide):
+    groups, stripe = own_ref.shape[-3:-1]
+    for n, ref in enumerate((k_ref, v_ref)):
+        wide[...] = ref[...].astype(jnp.float32)
+        for g in range(groups):
+            own_ref[0, n, g] = wide[pl.ds(g, stripe, stride=groups), :].astype(jnp.bfloat16)
+
+
+def outgoing_kernel(place_ref, own_ref, up_ref, up2_ref, *out_refs):
+    lane = lax.rem(place_ref[0], PLANE)
+    for flip, out_ref in zip(FLIPS, out_refs):
+        ahead = jnp.bitwise_xor(lane, flip) > lane
+        out_ref[0] = up_ref[0]
+
+        @pl.when(ahead)
+        def _():
+            out_ref[1] = own_ref[0]
+
+        @pl.when(jnp.logical_not(ahead))
+        def _():
+            out_ref[1] = up2_ref[0]
+
+
+def sums_kernel(place_ref, up_ref, own_ref, *refs):
+    back_refs, (level_ref, far_ref, mine_ref) = refs[:3], refs[3:]
+    lane = lax.rem(place_ref[0], PLANE)
+    level = up_ref[0].astype(jnp.float32)
+    mine = own_ref[0].astype(jnp.float32)
+    far = jnp.zeros_like(mine)
+    for flip, ref in zip(FLIPS, back_refs):
+        ahead = jnp.bitwise_xor(lane, flip) > lane
+        level = level + ref[0].astype(jnp.float32)
+        got = ref[1].astype(jnp.float32)
+        mine = mine + jnp.where(ahead, got, 0.0)
+        far = far + jnp.where(ahead, 0.0, got)
+    level_ref[0] = level.astype(jnp.bfloat16)
+    far_ref[0] = far.astype(jnp.bfloat16)
+    mine_ref[0] = mine
+
+
+def total_kernel(mine_ref, down_ref, down2_ref, k_ref, v_ref, wide):
+    groups, stripe = mine_ref.shape[-3:-1]
+    for n, ref in enumerate((k_ref, v_ref)):
+        for g in range(groups):
+            wide[pl.ds(g, stripe, stride=groups), :] = (
+                mine_ref[0, n, g] + down_ref[0, n, g].astype(jnp.float32) + down2_ref[0, n, g].astype(jnp.float32)
+            )
+        ref[...] = wide[...].astype(jnp.bfloat16)
 
 
 def shards(queries, key_vectors, value_matrix, grad_out, doc_lengths):
@@ -178,19 +225,31 @@
     cols = stripe * heads_per
     length = lax.axis_size("ctx")
     me = lax.axis_index("ctx").astype(jnp.int32)
-    lane = lax.rem(me, PLANE)
     place = me[None]
 
     def send(array, to):
-        pairs = [(i, to(i)) for i in range(length) if 0 <= to(i) < length]
-        return lax.ppermute(array, "ctx", pairs)
+        return lax.ppermute(array, "ctx", [(i, to(i)) for i in range(length)])
 
     def columns(array):
         return array.reshape(stripe, groups, heads_per, dim).transpose(1, 0, 2, 3).reshape(groups, cols, dim)
 
-    own = jnp.stack([key_vectors, value_matrix]).transpose(0, 2, 1, 3)
+    def small(body, ins, shapes, scratch=()):
+        return pl.pallas_call(
+            body,
+            out_shape=shapes,
+            in_specs=[SMEM if x is place else VMEM for x in ins],
+            out_specs=[VMEM] * len(shapes),
+            scratch_shapes=list(scratch),
+            compiler_params=pltpu.CompilerParams(vmem_limit_bytes=8 << 20),
+        )(*ins)
+
+    def shaped(dtype, *dims):
+        return jax.ShapeDtypeStruct(dims + (2, groups, stripe, dim), dtype)
+
+    flat = (stripe * groups, dim)
+    wide = pltpu.VMEM(flat, jnp.float32)
+    (own,) = small(pack_kernel, [key_vectors.reshape(flat), value_matrix.reshape(flat)], [shaped(jnp.bfloat16, 1)], [wide])
     q, do = columns(queries), columns(grad_out)
-    piece = jax.ShapeDtypeStruct(own.shape, jnp.bfloat16)
     stat = jax.ShapeDtypeStruct((groups, 1, cols), jnp.float32)
     total = jax.ShapeDtypeStruct((groups, dim, cols), jnp.float32)
     row = pltpu.VMEM((1, cols), jnp.int32)
@@ -199,7 +258,7 @@
 
     def params(products, n):
         return dict(
-            compiler_params=pltpu.CompilerParams(vmem_limit_bytes=20 << 20),
+            compiler_params=pltpu.CompilerParams(vmem_limit_bytes=8 << 20),
             cost_estimate=pl.CostEstimate(flops=products * n * pair_flops * 2, bytes_accessed=1 << 20, transcendentals=0),
         )
 
@@ -210,51 +269,59 @@
             in_specs=[SMEM, SMEM] + [VMEM] * (2 + len(kvs) + (0 if old is None else 3)),
             out_specs=[VMEM] * 3,
             scratch_shapes=[row, row],
-            **params(2, len(kvs)),
+            input_output_aliases={} if old is None else {4 + len(kvs) + i: i for i in range(3)},
+            **params(2, sum(len(held) for held in slots)),
         )(place, doc_lengths, q, do, *kvs, *(old or ()))
 
     def grads(slots, kvs, m, d, old=None, last=False):
         n = len(kvs)
-        dq_shape = jax.ShapeDtypeStruct(q.shape, jnp.bfloat16) if last else total
+        dq_shape = [jax.ShapeDtypeStruct(q.shape, jnp.bfloat16), total] if last else [total]
         outs = pl.pallas_call(
             functools.partial(grad_kernel, slots, heads_per, n_docs, old is None, last),
-            out_shape=[piece] * n + [dq_shape],
+            out_shape=[jax.ShapeDtypeStruct(kv.shape, jnp.bfloat16) for kv in kvs] + dq_shape,
             in_specs=[SMEM, SMEM] + [VMEM] * (4 + n + (0 if old is None else 1)),
-            out_specs=[VMEM] * (n + 1),
-            scratch_shapes=[row, row] + ([pltpu.VMEM(total.shape, jnp.float32)] if last else []),
-            **params(5, n),
+            out_specs=[VMEM] * (n + len(dq_shape)),
+            scratch_shapes=[row, row],
+            input_output_aliases={} if old is None else {6 + n: n + len(dq_shape) - 1},
+            **params(5, sum(len(held) for held in slots)),
         )(place, doc_lengths, q, do, m, d, *kvs, *(() if old is None else (old,)))
         return outs[:n], outs[n]
 
-    upx_slots = [functools.partial(upx_slot, f) for f in FLIPS]
-    mix_slots = [functools.partial(mix_slot, f) for f in FLIPS]
-    other = [jnp.bitwise_xor(lane, f) for f in FLIPS]
-
-    up = send(own, lambda i: i + PLANE)
-    seen = stats([own_slot], [own])
-    up, seen = lax.optimization_barrier((up, seen))
-    up2 = send(up, lambda i: i + PLANE)
-    upx = [send(up, lambda i, f=f: i ^ f) for f in FLIPS]
-    seen = stats([up_slot], [up], seen)
-    mix = [send(jnp.where(other[k] > lane, own, up2), lambda i, f=f: i ^ f) for k, f in enumerate(FLIPS)]
-    seen = stats(upx_slots, upx, seen)
-    m, _, d = stats(mix_slots, mix, seen, last=True)
-
-    mix_parts, dq = grads(mix_slots, mix, m, d)
-    mixed = [send(part, lambda i, f=f: i ^ f) for part, f in zip(mix_parts, FLIPS)]
-    upx_parts, dq = grads(upx_slots, upx, m, d, dq)
-    level = [send(part, lambda i, f=f: i ^ f) for part, f in zip(upx_parts, FLIPS)]
-    (up_part, own_part), dq = grads([up_slot, own_slot], [up, own], m, d, dq, last=True)
-
-    wide = [x.astype(jnp.float32) for x in mixed]
-    far_sum = sum(jnp.where(other[k] < lane, wide[k], 0.0) for k in range(3))
-    down2 = send(far_sum.astype(jnp.bfloat16), lambda i: i - PLANE).astype(jnp.float32)
-    level_sum = up_part.astype(jnp.float32) + sum(x.astype(jnp.float32) for x in level) + down2
-    down = send(level_sum.astype(jnp.bfloat16), lambda i: i - PLANE).astype(jnp.float32)
-    mine = own_part.astype(jnp.float32) + sum(jnp.where(other[k] > lane, wide[k], 0.0) for k in range(3))
-    kv_grad = (mine + down).astype(jnp.bfloat16).transpose(0, 2, 1, 3)
+    flip_slots = [[functools.partial(upx_slot, f), functools.partial(mix_slot, f)] for f in FLIPS]
+
+    def shift(array, by):
+        return send(array, lambda i: (i + by) % length)
+
+    def swap(array, flip):
+        return send(array, lambda i: i ^ flip)
+
+    up2 = shift(own, 2 * PLANE)
+    up = shift(own, PLANE)
+    seen = stats([[own_slot]], [own])
+    up, up2, seen = lax.optimization_barrier((up, up2, seen))
+    outgoing = small(outgoing_kernel, [place, own, up, up2], [shaped(jnp.bfloat16, 2)] * 3)
+    pairs = [swap(x, f) for x, f in zip(outgoing, FLIPS)]
+    seen = stats([[up_slot]], [up], seen)
+    for k in (2, 1, 0):
+        seen = stats([flip_slots[k]], [pairs[k]], seen, last=k == 0)
+    m, _, d = seen
+
+    dq, back = None, [None] * 3
+    for k in (2, 1, 0):
+        (part,), dq = grads([flip_slots[k]], [pairs[k]], m, d, dq)
+        back[k] = swap(part, FLIPS[k])
+    (up_part, own_part), dq = grads([[up_slot], [own_slot]], [up, own], m, d, dq, last=True)
+    level, far, mine = small(
+        sums_kernel,
+        [place, up_part, own_part, *back],
+        [shaped(jnp.bfloat16, 1), shaped(jnp.bfloat16, 1), shaped(jnp.float32, 1)],
+    )
+    down2 = shift(far, -2 * PLANE)
+    down = shift(level, -PLANE)
+    flat_out = jax.ShapeDtypeStruct(flat, jnp.bfloat16)
+    grad_k, grad_v = small(total_kernel, [mine, down, down2], [flat_out, flat_out], [wide])
     dq = dq.reshape(groups, stripe, heads_per, dim).transpose(1, 0, 2, 3).reshape(stripe, heads, dim)
-    return dq, kv_grad[0], kv_grad[1]
+    return dq, grad_k.reshape(key_vectors.shape), grad_v.reshape(value_matrix.shape)
 
 
 def solution(mesh):

time: 80.9 us -> 97.7 us (1.21)
  the two profiles are of different devices: /device:TPU:16 before, /device:TPU:0 now
where the time goes in v3:
time: 97.7 us; the launch traced here: 97.5 us
  waiting for transfers between devices  48.1 us (49%)
  starting transfers between devices  32.9 us (34%)
  Pallas kernels  11.5 us (12%)
  local copies, waits for them, and re-layouts  4.28 us (4%)
    ppermute x10, waiting for transfers between devices, send(): return lax.ppermute(array, 'ctx', [(i, to(i)) for i in range(length)])  48.1 us
    ppermute x10, starting transfers between devices, send(): return lax.ppermute(array, 'ctx', [(i, to(i)) for i in range(length)])  32.9 us
    pallas_call x4, Pallas kernels, grads(): pl.pallas_call(functools.partial(grad_kernel, slots, heads_per, n_docs, o...  5.65 us
    pallas_call x5, Pallas kernels, stats(): pl.pallas_call(functools.partial(stats_kernel, slots, heads_per, n_docs,...  4.61 us
  transfers between devices with their start and end apart: 10, of which 8 were waited for; matrix products, arithmetic and copies ran while one was open for 2% of the time, Pallas kernels for 8%

profile of v3, /device:TPU:0, one launch (start us, length us, event | category | flops | bytes accessed | tf_op | source)
XLA Modules:
  0.0 97.5 jit_solution(8810935837165423187)
XLA Ops:
  0.6 0.0 copy-start
  0.6 0.0 copy-start.1
  0.7 1.0 copy-done.1
  1.6 0.0 copy-start.2
  1.6 0.9 copy-done.2
  2.5 0.1 shard_map.76.refs_4_.own_ref.refs_7_
  2.6 0.0 copy-start.3
  2.6 4.1 %collective-permute-start.1 = (bf16[1,2,2,192,128]{4,3,2,1,0:T(8,128)(2,1)S(1)}, bf16[1,2,2,192,128]{4,3,2,1,0:T(8,128)(2,1)S(1)}, u32[]{:S(2)}, u32[]{:S(2)}) collective-permute-start(bf16[1,2,2,192,128]{4,3,2,1,0:T(8,128)(2,1)S(1)} %shard_map.76.refs_4_.own_ref.refs_7_), channel_id=1, source_target_pairs={{0,16},{2,18},{4,20},{6,22},{8,24},{10,26},{12,28},{14,30},{16,0},... | collective-permute-start | bytes 589832 | tf_op jit(solution)/shard_map/ppermute | solution.py:231
  6.7 1.6 %collective-permute-start = (bf16[1,2,2,192,128]{4,3,2,1,0:T(8,128)(2,1)S(1)}, bf16[1,2,2,192,128]{4,3,2,1,0:T(8,128)(2,1)S(1)}, u32[]{:S(2)}, u32[]{:S(2)}) collective-permute-start(bf16[1,2,2,192,128]{4,3,2,1,0:T(8,128)(2,1)S(1)} %shard_map.76.refs_4_.own_ref.refs_7_), channel_id=1, source_target_pairs={{0,8},{2,10},{4,12},{6,14},{8,16},{10,18},{12,20},{14,22},{16,24},... | collective-permute-start | bytes 589832 | tf_op jit(solution)/shard_map/ppermute | solution.py:231
  8.3 0.0 copy-done
  8.3 1.4 %copy_bitcast_fusion.1 = (bf16[2,1536,128]{2,1,0:T(8,128)(2,1)S(1)}, bf16[2,1536,128]{2,1,0:T(8,128)(2,1)S(1)}) fusion(bf16[192,16,128]{2,1,0:T(8,128)(2,1)S(1)} %copy-done, bf16[192,16,128]{2,1,0:T(8,128)(2,1)} %param.8), kind=kLoop, calls=%fused_computation.1 | loop fusion | bytes 3145728 | tf_op jit(solution)/shard_map/reshape | solution.py:234
  9.7 0.0 copy-done.3
  9.7 2.1 %shard_map.77 = (f32[2,1,1536]{2,1,0:T(1,128)S(1)}, f32[2,1,1536]{2,1,0:T(1,128)S(1)}, f32[2,1,1536]{2,1,0:T(1,128)S(1)}) custom-call(s32[1]{0:T(128)} %bitcast.refs_0_.place_ref, s32[8]{0:T(128)S(1)} %copy-done.3, bf16[2,1536,128]{2,1,0:T(8,128)(2,1)S(1)} %get-tuple-element.76.refs_2_, bf16[2,1536,128]{2,1,0:T(8,128)(2,1)S(1)} %get-tuple-element.75.refs_3_, ...), custom_call_target="tpu_custom_call" | custom-call | flops 603979776 | bytes 1048576 | tf_op jit(solution)/shard_map/pallas_call | solution.py:266
  11.9 8.2 %collective-permute-done.1.up2_ref = bf16[1,2,2,192,128]{4,3,2,1,0:T(8,128)(2,1)S(1)} collective-permute-done((bf16[1,2,2,192,128]{4,3,2,1,0:T(8,128)(2,1)S(1)}, bf16[1,2,2,192,128]{4,3,2,1,0:T(8,128)(2,1)S(1)}, u32[]{:S(2)}, u32[]{:S(2)}) %collective-permute-start.1) | collective-permute-done | bytes 196640 | tf_op jit(solution)/shard_map/ppermute | solution.py:231
  20.0 0.0 collective-permute-done.up_ref.refs_4_.refs_6_
  20.0 0.1 shard_map.78
  20.1 2.6 %collective-permute-start.4 = (bf16[2,2,2,192,128]{4,3,2,1,0:T(8,128)(2,1)S(1)}, bf16[2,2,2,192,128]{4,3,2,1,0:T(8,128)(2,1)S(1)}, u32[]{:S(2)}, u32[]{:S(2)}) collective-permute-start(bf16[2,2,2,192,128]{4,3,2,1,0:T(8,128)(2,1)S(1)} %get-tuple-element.46), channel_id=1, source_target_pairs={{0,6},{2,4},{4,2},{6,0},{8,14},{10,12},{12,10},{14,8},{16,22},{18,... | collective-permute-start | bytes 1179656 | tf_op jit(solution)/shard_map/ppermute | solution.py:231
  22.7 0.5 collective-permute-start.3
  23.2 0.5 collective-permute-start.2
  23.7 0.6 shard_map.79
  24.3 8.8 %collective-permute-done.4.refs_4_.refs_6_ = bf16[2,2,2,192,128]{4,3,2,1,0:T(8,128)(2,1)S(1)} collective-permute-done((bf16[2,2,2,192,128]{4,3,2,1,0:T(8,128)(2,1)S(1)}, bf16[2,2,2,192,128]{4,3,2,1,0:T(8,128)(2,1)S(1)}, u32[]{:S(2)}, u32[]{:S(2)}) %collective-permute-start.4) | collective-permute-done | bytes 393248 | tf_op jit(solution)/shard_map/ppermute | solution.py:231
  33.1 0.6 shard_map.80
  33.7 6.1 %collective-permute-done.3.refs_4_.refs_6_ = bf16[2,2,2,192,128]{4,3,2,1,0:T(8,128)(2,1)S(1)} collective-permute-done((bf16[2,2,2,192,128]{4,3,2,1,0:T(8,128)(2,1)S(1)}, bf16[2,2,2,192,128]{4,3,2,1,0:T(8,128)(2,1)S(1)}, u32[]{:S(2)}, u32[]{:S(2)}) %collective-permute-start.3) | collective-permute-done | bytes 393248 | tf_op jit(solution)/shard_map/ppermute | solution.py:231
  39.8 0.6 shard_map.81
  40.4 0.0 collective-permute-done.2.refs_4_.refs_6_
  40.4 0.6 shard_map.82
  41.1 0.7 shard_map.83
  41.8 0.7 shard_map.84
  42.5 0.9 shard_map.85
  43.4 5.3 %collective-permute-start.5 = (bf16[2,2,2,192,128]{4,3,2,1,0:T(8,128)(2,1)S(1)}, bf16[2,2,2,192,128]{4,3,2,1,0:T(8,128)(2,1)S(1)}, u32[]{:S(2)}, u32[]{:S(2)}) collective-permute-start(bf16[2,2,2,192,128]{4,3,2,1,0:T(8,128)(2,1)S(1)} %get-tuple-element.67), channel_id=1, source_target_pairs={{0,2},{2,0},{4,6},{6,4},{8,10},{10,8},{12,14},{14,12},{16,18},{18,... | collective-permute-start | bytes 1179656 | tf_op jit(solution)/shard_map/ppermute | solution.py:231
  48.7 2.6 %collective-permute-start.6 = (bf16[2,2,2,192,128]{4,3,2,1,0:T(8,128)(2,1)S(1)}, bf16[2,2,2,192,128]{4,3,2,1,0:T(8,128)(2,1)S(1)}, u32[]{:S(2)}, u32[]{:S(2)}) collective-permute-start(bf16[2,2,2,192,128]{4,3,2,1,0:T(8,128)(2,1)S(1)} %get-tuple-element.68), channel_id=1, source_target_pairs={{0,4},{2,6},{4,0},{6,2},{8,12},{10,14},{12,8},{14,10},{16,20},{18,... | collective-permute-start | bytes 1179656 | tf_op jit(solution)/shard_map/ppermute | solution.py:231
  51.2 1.4 %collective-permute-start.7 = (bf16[2,2,2,192,128]{4,3,2,1,0:T(8,128)(2,1)S(1)}, bf16[2,2,2,192,128]{4,3,2,1,0:T(8,128)(2,1)S(1)}, u32[]{:S(2)}, u32[]{:S(2)}) collective-permute-start(bf16[2,2,2,192,128]{4,3,2,1,0:T(8,128)(2,1)S(1)} %get-tuple-element.69), channel_id=1, source_target_pairs={{0,6},{2,4},{4,2},{6,0},{8,14},{10,12},{12,10},{14,8},{16,22},{18,... | collective-permute-start | bytes 1179656 | tf_op jit(solution)/shard_map/ppermute | solution.py:231
  52.6 3.4 %shard_map.86 = (bf16[1,2,2,192,128]{4,3,2,1,0:T(8,128)(2,1)S(1)}, bf16[1,2,2,192,128]{4,3,2,1,0:T(8,128)(2,1)S(1)}, bf16[2,1536,128]{2,1,0:T(8,128)(2,1)S(1)}, f32[2,128,1536]{2,1,0:T(8,128)S(1)}) custom-call(s32[1]{0:T(128)} %bitcast.refs_0_.place_ref, s32[8]{0:T(128)S(1)} %copy-done.3, ...), custom_call_target="tpu_custom_call", output_to_operand_aliasing={{3}: (8, {})} | custom-call | flops 3019898880 | bytes 1048576 | tf_op jit(solution)/shard_map/pallas_call | solution.py:279
  56.0 2.6 %collective-permute-done.5.refs_0_ = bf16[2,2,2,192,128]{4,3,2,1,0:T(8,128)(2,1)S(1)} collective-permute-done((bf16[2,2,2,192,128]{4,3,2,1,0:T(8,128)(2,1)S(1)}, bf16[2,2,2,192,128]{4,3,2,1,0:T(8,128)(2,1)S(1)}, u32[]{:S(2)}, u32[]{:S(2)}) %collective-permute-start.5) | collective-permute-done | bytes 393248 | tf_op jit(solution)/shard_map/ppermute | solution.py:231
  58.7 9.6 %collective-permute-done.6.refs_1_ = bf16[2,2,2,192,128]{4,3,2,1,0:T(8,128)(2,1)S(1)} collective-permute-done((bf16[2,2,2,192,128]{4,3,2,1,0:T(8,128)(2,1)S(1)}, bf16[2,2,2,192,128]{4,3,2,1,0:T(8,128)(2,1)S(1)}, u32[]{:S(2)}, u32[]{:S(2)}) %collective-permute-start.6) | collective-permute-done | bytes 393248 | tf_op jit(solution)/shard_map/ppermute | solution.py:231
  68.2 1.8 %collective-permute-done.7.refs_2_ = bf16[2,2,2,192,128]{4,3,2,1,0:T(8,128)(2,1)S(1)} collective-permute-done((bf16[2,2,2,192,128]{4,3,2,1,0:T(8,128)(2,1)S(1)}, bf16[2,2,2,192,128]{4,3,2,1,0:T(8,128)(2,1)S(1)}, u32[]{:S(2)}, u32[]{:S(2)}) %collective-permute-start.7) | collective-permute-done | bytes 393248 | tf_op jit(solution)/shard_map/ppermute | solution.py:231
  70.1 0.3 shard_map.87
  70.4 13.9 %collective-permute-start.8 = (bf16[1,2,2,192,128]{4,3,2,1,0:T(8,128)(2,1)S(1)}, bf16[1,2,2,192,128]{4,3,2,1,0:T(8,128)(2,1)S(1)}, u32[]{:S(2)}, u32[]{:S(2)}) collective-permute-start(bf16[1,2,2,192,128]{4,3,2,1,0:T(8,128)(2,1)S(1)} %get-tuple-element.71), channel_id=1, source_target_pairs={{0,24},{2,26},{4,28},{6,30},{8,0},{10,2},{12,4},{14,6},{16,8},{18,... | collective-permute-start | bytes 589832 | tf_op jit(solution)/shard_map/ppermute | solution.py:231
  84.3 0.5 collective-permute-start.9
  84.8 1.0 %copy_bitcast_fusion = bf16[192,16,128]{2,1,0:T(8,128)(2,1)} fusion(bf16[2,1536,128]{2,1,0:T(8,128)(2,1)S(1)} %get-tuple-element.64), kind=kLoop, calls=%fused_computation | loop fusion | bytes 1572864 | tf_op jit(solution)/shard_map/reshape | solution.py:323
  85.8 3.8 %collective-permute-done.8.down_ref = bf16[1,2,2,192,128]{4,3,2,1,0:T(8,128)(2,1)S(1)} collective-permute-done((bf16[1,2,2,192,128]{4,3,2,1,0:T(8,128)(2,1)S(1)}, bf16[1,2,2,192,128]{4,3,2,1,0:T(8,128)(2,1)S(1)}, u32[]{:S(2)}, u32[]{:S(2)}) %collective-permute-start.8) | collective-permute-done | bytes 196640 | tf_op jit(solution)/shard_map/ppermute | solution.py:231
  89.6 7.2 %collective-permute-done.9.down2_ref = bf16[1,2,2,192,128]{4,3,2,1,0:T(8,128)(2,1)S(1)} collective-permute-done((bf16[1,2,2,192,128]{4,3,2,1,0:T(8,128)(2,1)S(1)}, bf16[1,2,2,192,128]{4,3,2,1,0:T(8,128)(2,1)S(1)}, u32[]{:S(2)}, u32[]{:S(2)}) %collective-permute-start.9) | collective-permute-done | bytes 196640 | tf_op jit(solution)/shard_map/ppermute | solution.py:231
  96.8 0.7 shard_map.88
Async XLA Ops:
  0.6 7.6 %copy-start = (bf16[192,16,128]{2,1,0:T(8,128)(2,1)S(1)}, bf16[192,16,128]{2,1,0:T(8,128)(2,1)}, u32[]{:S(2)}) copy-start(bf16[192,16,128]{2,1,0:T(8,128)(2,1)} %param.5) | copy-start | bytes 2359300
  0.6 1.0 copy-start.1
  1.6 0.9 copy-start.2
  2.6 7.1 %copy-start.3 = (s32[8]{0:T(128)S(1)}, s32[8]{0:T(128)}, u32[]{:S(2)}) copy-start(s32[8]{0:T(128)} %refs_1_.17) | copy-start | bytes 100
  2.6 17.5 %collective-permute-start.1 = (bf16[1,2,2,192,128]{4,3,2,1,0:T(8,128)(2,1)S(1)}, bf16[1,2,2,192,128]{4,3,2,1,0:T(8,128)(2,1)S(1)}, u32[]{:S(2)}, u32[]{:S(2)}) collective-permute-start(bf16[1,2,2,192,128]{4,3,2,1,0:T(8,128)(2,1)S(1)} %shard_map.76.refs_4_.own_ref.refs_7_), channel_id=1, source_target_pairs={{0,16},{2,18},{4,20},{6,22},{8,24},{10,26},{12,28},{14,30},{16,0},... | collective-permute-start | bytes 589832 | tf_op jit(solution)/shard_map/ppermute | solution.py:231
  6.7 13.3 %collective-permute-start = (bf16[1,2,2,192,128]{4,3,2,1,0:T(8,128)(2,1)S(1)}, bf16[1,2,2,192,128]{4,3,2,1,0:T(8,128)(2,1)S(1)}, u32[]{:S(2)}, u32[]{:S(2)}) collective-permute-start(bf16[1,2,2,192,128]{4,3,2,1,0:T(8,128)(2,1)S(1)} %shard_map.76.refs_4_.own_ref.refs_7_), channel_id=1, source_target_pairs={{0,8},{2,10},{4,12},{6,14},{8,16},{10,18},{12,20},{14,22},{16,24},... | collective-permute-start | bytes 589832 | tf_op jit(solution)/shard_map/ppermute | solution.py:231
  20.1 13.0 %collective-permute-start.4 = (bf16[2,2,2,192,128]{4,3,2,1,0:T(8,128)(2,1)S(1)}, bf16[2,2,2,192,128]{4,3,2,1,0:T(8,128)(2,1)S(1)}, u32[]{:S(2)}, u32[]{:S(2)}) collective-permute-start(bf16[2,2,2,192,128]{4,3,2,1,0:T(8,128)(2,1)S(1)} %get-tuple-element.46), channel_id=1, source_target_pairs={{0,6},{2,4},{4,2},{6,0},{8,14},{10,12},{12,10},{14,8},{16,22},{18,... | collective-permute-start | bytes 1179656 | tf_op jit(solution)/shard_map/ppermute | solution.py:231
  22.7 17.1 %collective-permute-start.3 = (bf16[2,2,2,192,128]{4,3,2,1,0:T(8,128)(2,1)S(1)}, bf16[2,2,2,192,128]{4,3,2,1,0:T(8,128)(2,1)S(1)}, u32[]{:S(2)}, u32[]{:S(2)}) collective-permute-start(bf16[2,2,2,192,128]{4,3,2,1,0:T(8,128)(2,1)S(1)} %get-tuple-element.45), channel_id=1, source_target_pairs={{0,4},{2,6},{4,0},{6,2},{8,12},{10,14},{12,8},{14,10},{16,20},{18,... | collective-permute-start | bytes 1179656 | tf_op jit(solution)/shard_map/ppermute | solution.py:231
  23.2 17.2 %collective-permute-start.2 = (bf16[2,2,2,192,128]{4,3,2,1,0:T(8,128)(2,1)S(1)}, bf16[2,2,2,192,128]{4,3,2,1,0:T(8,128)(2,1)S(1)}, u32[]{:S(2)}, u32[]{:S(2)}) collective-permute-start(bf16[2,2,2,192,128]{4,3,2,1,0:T(8,128)(2,1)S(1)} %get-tuple-element.44), channel_id=1, source_target_pairs={{0,2},{2,0},{4,6},{6,4},{8,10},{10,8},{12,14},{14,12},{16,18},{18,... | collective-permute-start | bytes 1179656 | tf_op jit(solution)/shard_map/ppermute | solution.py:231
  43.4 15.3 %collective-permute-start.5 = (bf16[2,2,2,192,128]{4,3,2,1,0:T(8,128)(2,1)S(1)}, bf16[2,2,2,192,128]{4,3,2,1,0:T(8,128)(2,1)S(1)}, u32[]{:S(2)}, u32[]{:S(2)}) collective-permute-start(bf16[2,2,2,192,128]{4,3,2,1,0:T(8,128)(2,1)S(1)} %get-tuple-element.67), channel_id=1, source_target_pairs={{0,2},{2,0},{4,6},{6,4},{8,10},{10,8},{12,14},{14,12},{16,18},{18,... | collective-permute-start | bytes 1179656 | tf_op jit(solution)/shard_map/ppermute | solution.py:231
  48.7 19.5 %collective-permute-start.6 = (bf16[2,2,2,192,128]{4,3,2,1,0:T(8,128)(2,1)S(1)}, bf16[2,2,2,192,128]{4,3,2,1,0:T(8,128)(2,1)S(1)}, u32[]{:S(2)}, u32[]{:S(2)}) collective-permute-start(bf16[2,2,2,192,128]{4,3,2,1,0:T(8,128)(2,1)S(1)} %get-tuple-element.68), channel_id=1, source_target_pairs={{0,4},{2,6},{4,0},{6,2},{8,12},{10,14},{12,8},{14,10},{16,20},{18,... | collective-permute-start | bytes 1179656 | tf_op jit(solution)/shard_map/ppermute | solution.py:231
  51.2 18.8 %collective-permute-start.7 = (bf16[2,2,2,192,128]{4,3,2,1,0:T(8,128)(2,1)S(1)}, bf16[2,2,2,192,128]{4,3,2,1,0:T(8,128)(2,1)S(1)}, u32[]{:S(2)}, u32[]{:S(2)}) collective-permute-start(bf16[2,2,2,192,128]{4,3,2,1,0:T(8,128)(2,1)S(1)} %get-tuple-element.69), channel_id=1, source_target_pairs={{0,6},{2,4},{4,2},{6,0},{8,14},{10,12},{12,10},{14,8},{16,22},{18,... | collective-permute-start | bytes 1179656 | tf_op jit(solution)/shard_map/ppermute | solution.py:231
  70.4 19.2 %collective-permute-start.8 = (bf16[1,2,2,192,128]{4,3,2,1,0:T(8,128)(2,1)S(1)}, bf16[1,2,2,192,128]{4,3,2,1,0:T(8,128)(2,1)S(1)}, u32[]{:S(2)}, u32[]{:S(2)}) collective-permute-start(bf16[1,2,2,192,128]{4,3,2,1,0:T(8,128)(2,1)S(1)} %get-tuple-element.71), channel_id=1, source_target_pairs={{0,24},{2,26},{4,28},{6,30},{8,0},{10,2},{12,4},{14,6},{16,8},{18,... | collective-permute-start | bytes 589832 | tf_op jit(solution)/shard_map/ppermute | solution.py:231
  84.3 12.5 %collective-permute-start.9 = (bf16[1,2,2,192,128]{4,3,2,1,0:T(8,128)(2,1)S(1)}, bf16[1,2,2,192,128]{4,3,2,1,0:T(8,128)(2,1)S(1)}, u32[]{:S(2)}, u32[]{:S(2)}) collective-permute-start(bf16[1,2,2,192,128]{4,3,2,1,0:T(8,128)(2,1)S(1)} %get-tuple-element.72), channel_id=1, source_target_pairs={{0,16},{2,18},{4,20},{6,22},{8,24},{10,26},{12,28},{14,30},{16,0},... | collective-permute-start | bytes 589832 | tf_op jit(solution)/shard_map/ppermute | solution.py:231

commit v4 on v3

v4 whole, which is shorter than its diff:
```python
import functools
import math

import jax
import jax.numpy as jnp
from jax import lax
from jax.experimental import pallas as pl
from jax.experimental.pallas import tpu as pltpu
from jax.sharding import PartitionSpec as P


PLANE = 4
FLIPS = (3, 2, 1)
LOG2E = math.log2(math.e)
NEG_INIT = -1e30
NEG_DEAD = -2e30

NT = (((1,), (1,)), ((), ()))
NN = (((1,), (0,)), ((), ()))
TN = (((0,), (0,)), ((), ()))
SMEM = pl.BlockSpec(memory_space=pltpu.SMEM)
VMEM = pl.BlockSpec(memory_space=pltpu.VMEM)


def mm(a, b, dims):
    return lax.dot_general(a, b, dims, preferred_element_type=jnp.float32)


def own_slot(me, lane):
    return me


def up_slot(me, lane):
    return me - PLANE


def upx_slot(flip, me, lane):
    return me - PLANE - lane + jnp.bitwise_xor(lane, flip)


def mix_slot(flip, me, lane):
    other = jnp.bitwise_xor(lane, flip)
    return me - lane + other - jnp.where(other < lane, 0, 2 * PLANE)


def first_live(place_ref):
    me = place_ref[0]
    return me, lax.rem(me, PLANE), place_ref[1]


def start_kernel(heads_per, n_docs, place_ref, lens_ref, start_ref, info_ref):
    groups_cols = start_ref.shape
    stripe = groups_cols[1] // heads_per
    me = place_ref[0]
    col = lax.broadcasted_iota(jnp.int32, groups_cols, 1)
    start = jnp.zeros(groups_cols, jnp.int32)
    end = jnp.int32(0)
    first_key = jnp.int32(0)
    for n in range(n_docs):
        end = end + lens_ref[n]
        start = jnp.where(col >= (end - me * stripe) * heads_per, end, start)
        first_key = jnp.where(me * stripe >= end, end, first_key)
    start_ref[...] = start
    info_ref[0] = me
    info_ref[1] = first_key


def logits(keys, q_g, base, start_ref, heads_per, causal, scale2):
    s = mm(keys, q_g, NT) * scale2
    row = lax.broadcasted_iota(jnp.int32, s.shape, 0)
    live = row >= start_ref[...] - base
    if causal:
        live = live & (row <= lax.div(lax.broadcasted_iota(jnp.int32, start_ref.shape, 1), heads_per))
    return jnp.where(live, s, NEG_DEAD)


def stats_kernel(slots, heads_per, first, last, *refs):
    n = len(slots)
    place_ref, start_ref, q_ref, do_ref = refs[:4]
    kv_refs = refs[4 : 4 + n]
    refs = refs[4 + n :]
    if not first:
        refs = refs[3:]
    m_ref, l_ref, d_ref = refs
    groups, _, dim = q_ref.shape
    stripe = kv_refs[0].shape[-2]
    scale2 = dim**-0.5 * LOG2E
    me, lane, first_key = first_live(place_ref)
    if first:
        m_ref[...] = jnp.full_like(m_ref, NEG_INIT)
        l_ref[...] = jnp.zeros_like(l_ref)
        d_ref[...] = jnp.zeros_like(d_ref)
    for kv_ref, slot in zip(kv_refs, slots):
        at = slot(me, lane)

        @pl.when((at >= 0) & ((at + 1) * stripe > first_key))
        def _():
            for g in range(groups):
                s = logits(kv_ref[0, g], q_ref[g], at * stripe, start_ref, heads_per, slot is own_slot, scale2)
                gp = mm(kv_ref[1, g], do_ref[g], NT)
                m_old = m_ref[g]
                m_new = jnp.maximum(m_old, jnp.max(s, axis=0, keepdims=True))
                e = jnp.exp2(s - m_new)
                fade = jnp.exp2(m_old - m_new)
                m_ref[g] = m_new
                l_ref[g] = l_ref[g] * fade + jnp.sum(e, axis=0, keepdims=True)
                d_ref[g] = d_ref[g] * fade + jnp.sum(e * gp, axis=0, keepdims=True)

    if last:
        d_ref[...] = d_ref[...] / l_ref[...]
        m_ref[...] = m_ref[...] + jnp.log2(l_ref[...])


def grad_kernel(slots, heads_per, first, last, *refs):
    n = len(slots)
    place_ref, start_ref, q_ref, do_ref, m_ref, d_ref = refs[:6]
    kv_refs = refs[6 : 6 + n]
    refs = refs[6 + n :]
    if not first:
        refs = refs[1:]
    part_refs = refs[:n]
    dqt = refs[n + 1] if last else refs[n]
    groups, _, dim = q_ref.shape
    stripe = kv_refs[0].shape[-2]
    scale = dim**-0.5
    scale2 = scale * LOG2E
    me, lane, first_key = first_live(place_ref)
    if first:
        dqt[...] = jnp.zeros_like(dqt)
    for kv_ref, part_ref, slot in zip(kv_refs, part_refs, slots):
        at = slot(me, lane)
        live = (at >= 0) & ((at + 1) * stripe > first_key)

        @pl.when(live)
        def _():
            for g in range(groups):
                keys, vals, q_g, do_g = kv_ref[0, g], kv_ref[1, g], q_ref[g], do_ref[g]
                s = logits(keys, q_g, at * stripe, start_ref, heads_per, slot is own_slot, scale2)
                gp = mm(vals, do_g, NT)
                p = jnp.exp2(s - m_ref[g])
                ds = (p * (gp - d_ref[g])).astype(jnp.bfloat16)
                part_ref[1, g] = mm(p.astype(jnp.bfloat16), do_g, NN).astype(jnp.bfloat16)
                part_ref[0, g] = (mm(ds, q_g, NN) * scale).astype(jnp.bfloat16)
                dqt[g] = dqt[g] + mm(keys, ds, TN)

        @pl.when(jnp.logical_not(live))
        def _():
            part_ref[...] = jnp.zeros_like(part_ref)

    if last:
        for g in range(groups):
            refs[n][g] = (dqt[g] * scale).T.astype(jnp.bfloat16)


def pack_kernel(k_ref, v_ref, own_ref, wide):
    groups, stripe = own_ref.shape[-3:-1]
    for n, ref in enumerate((k_ref, v_ref)):
        wide[...] = ref[...].astype(jnp.float32)
        for g in range(groups):
            own_ref[n, g] = wide[pl.ds(g, stripe, stride=groups), :].astype(jnp.bfloat16)


def outgoing_kernel(place_ref, own_ref, up2_ref, *out_refs):
    lane = lax.rem(place_ref[0], PLANE)
    for flip, out_ref in zip(FLIPS, out_refs):
        ahead = jnp.bitwise_xor(lane, flip) > lane

        @pl.when(ahead)
        def _():
            out_ref[...] = own_ref[...]

        @pl.when(jnp.logical_not(ahead))
        def _():
            out_ref[...] = up2_ref[...]


def far_kernel(place_ref, *refs):
    mix_refs, (far_ref, mine_ref) = refs[:3], refs[3:]
    lane = lax.rem(place_ref[0], PLANE)
    mine = jnp.zeros(mine_ref.shape, jnp.float32)
    far = jnp.zeros_like(mine)
    for flip, ref in zip(FLIPS, mix_refs):
        ahead = jnp.bitwise_xor(lane, flip) > lane
        got = ref[...].astype(jnp.float32)
        mine = mine + jnp.where(ahead, got, 0.0)
        far = far + jnp.where(ahead, 0.0, got)
    far_ref[...] = far.astype(jnp.bfloat16)
    mine_ref[...] = mine


def level_kernel(*refs):
    total = refs[0][...].astype(jnp.float32)
    for ref in refs[1:-1]:
        total = total + ref[...].astype(jnp.float32)
    refs[-1][...] = total.astype(jnp.bfloat16)


def total_kernel(mine_ref, own_ref, down_ref, k_ref, v_ref, wide):
    groups, stripe = mine_ref.shape[-3:-1]
    for n, ref in enumerate((k_ref, v_ref)):
        for g in range(groups):
            wide[pl.ds(g, stripe, stride=groups), :] = (
                mine_ref[n, g] + own_ref[n, g].astype(jnp.float32) + down_ref[n, g].astype(jnp.float32)
            )
        ref[...] = wide[...].astype(jnp.bfloat16)


def shards(queries, key_vectors, value_matrix, grad_out, doc_lengths):
    stripe, heads, dim = queries.shape
    groups = key_vectors.shape[1]
    heads_per = heads // groups
    cols = stripe * heads_per
    length = lax.axis_size("ctx")
    me = lax.axis_index("ctx").astype(jnp.int32)
    place = me[None]

    def send(array, to):
        return lax.ppermute(array, "ctx", [(i, to(i)) for i in range(length)])

    def columns(array):
        return array.reshape(stripe, groups, heads_per, dim).transpose(1, 0, 2, 3).reshape(groups, cols, dim)

    def small(body, ins, shapes, scratch=()):
        return pl.pallas_call(
            body,
            out_shape=shapes,
            in_specs=[SMEM if x is place else VMEM for x in ins],
            out_specs=[VMEM] * len(shapes),
            scratch_shapes=list(scratch),
            compiler_params=pltpu.CompilerParams(vmem_limit_bytes=8 << 20),
        )(*ins)

    def shaped(dtype):
        return jax.ShapeDtypeStruct((2, groups, stripe, dim), dtype)

    flat = (stripe * groups, dim)
    wide = pltpu.VMEM(flat, jnp.float32)
    (own,) = small(pack_kernel, [key_vectors.reshape(flat), value_matrix.reshape(flat)], [shaped(jnp.bfloat16)], [wide])
    q, do = columns(queries), columns(grad_out)
    stat = jax.ShapeDtypeStruct((groups, 1, cols), jnp.float32)
    total = jax.ShapeDtypeStruct((groups, dim, cols), jnp.float32)
    n_docs = doc_lengths.shape[0]
    pair_flops = groups * stripe * cols * dim * 2
    start, info = pl.pallas_call(
        functools.partial(start_kernel, heads_per, n_docs),
        out_shape=[jax.ShapeDtypeStruct((1, cols), jnp.int32), jax.ShapeDtypeStruct((2,), jnp.int32)],
        in_specs=[SMEM, SMEM],
        out_specs=[VMEM, SMEM],
        compiler_params=pltpu.CompilerParams(vmem_limit_bytes=8 << 20),
    )(place, doc_lengths)

    def params(products, n):
        return dict(
            compiler_params=pltpu.CompilerParams(vmem_limit_bytes=16 << 20),
            cost_estimate=pl.CostEstimate(flops=products * n * pair_flops * 2, bytes_accessed=1 << 20, transcendentals=0),
        )

    def stats(slots, kvs, old=None, last=False):
        return pl.pallas_call(
            functools.partial(stats_kernel, slots, heads_per, old is None, last),
            out_shape=[stat] * 3,
            in_specs=[SMEM] + [VMEM] * (3 + len(kvs) + (0 if old is None else 3)),
            out_specs=[VMEM] * 3,
            input_output_aliases={} if old is None else {4 + len(kvs) + i: i for i in range(3)},
            **params(2, len(kvs)),
        )(info, start, q, do, *kvs, *(old or ()))

    def grads(slots, kvs, old=None, last=False):
        n = len(kvs)
        dq_shape = [jax.ShapeDtypeStruct(q.shape, jnp.bfloat16), total] if last else [total]
        outs = pl.pallas_call(
            functools.partial(grad_kernel, slots, heads_per, old is None, last),
            out_shape=[shaped(jnp.bfloat16)] * n + dq_shape,
            in_specs=[SMEM] + [VMEM] * (5 + n + (0 if old is None else 1)),
            out_specs=[VMEM] * (n + len(dq_shape)),
            input_output_aliases={} if old is None else {6 + n: n + len(dq_shape) - 1},
            **params(5, n),
        )(info, start, q, do, m, d, *kvs, *(() if old is None else (old,)))
        return outs[:n], outs[n]

    upx_slots = [functools.partial(upx_slot, f) for f in FLIPS]
    mix_slots = [functools.partial(mix_slot, f) for f in FLIPS]

    def shift(array, by):
        return send(array, lambda i: (i + by) % length)

    def swap(array, flip):
        return send(array, lambda i: i ^ flip)

    up = shift(own, PLANE)
    seen = stats([own_slot], [own])
    up, seen = lax.optimization_barrier((up, seen))
    up2 = shift(up, PLANE)
    upx = [swap(up, f) for f in FLIPS]
    seen = stats([up_slot], [up], seen)
    outgoing = small(outgoing_kernel, [place, own, up2], [shaped(jnp.bfloat16)] * 3)
    mix = [swap(x, f) for x, f in zip(outgoing, FLIPS)]
    seen = stats(upx_slots, upx, seen)
    for k, f in enumerate(FLIPS):
        seen = stats([mix_slots[k]], [mix[k]], seen, last=k == 2)
    m, _, d = seen

    dq, mixed, level = None, [], []
    for k, f in enumerate(FLIPS):
        (part,), dq = grads([mix_slots[k]], [mix[k]], dq)
        mixed.append(swap(part, f))
    for k, f in enumerate(FLIPS):
        (part,), dq = grads([upx_slots[k]], [upx[k]], dq)
        level.append(swap(part, f))
    (own_part, up_part), dq = grads([own_slot, up_slot], [own, up], dq, last=True)

    far, mine = small(far_kernel, [place, *mixed], [shaped(jnp.bfloat16), shaped(jnp.float32)])
    down2 = shift(far, -PLANE)
    (below,) = small(level_kernel, [up_part, down2, *level], [shaped(jnp.bfloat16)])
    down = shift(below, -PLANE)
    flat_out = jax.ShapeDtypeStruct(flat, jnp.bfloat16)
    grad_k, grad_v = small(total_kernel, [mine, own_part, down], [flat_out, flat_out], [wide])
    dq = dq.reshape(groups, stripe, heads_per, dim).transpose(1, 0, 2, 3).reshape(stripe, heads, dim)
    return dq, grad_k.reshape(key_vectors.shape), grad_v.reshape(value_matrix.shape)


def solution(mesh):
    spec = P("ctx", "tp", None)
    return jax.shard_map(
        shards,
        mesh=mesh,
        in_specs=(spec, spec, spec, spec, P()),
        out_specs=(spec, spec, spec),
        check_vma=False,
    )
```

time: 97.7 us -> 73.3 us (0.75)
  waiting for transfers between devices: 48.1 us -> 20.4 us
  starting transfers between devices: 32.9 us -> 34.5 us
  Pallas kernels: 11.5 us -> 13.1 us
    ppermute x10 -> x16, waiting for transfers between devices: 48.1 us -> 20.4 us  [send(): return lax.ppermute(array, 'ctx', [(i, to(i)) for i in range(length)])]
    pallas_call x9 -> x14, Pallas kernels: 10.3 us -> 11.9 us  [the longest x7 6.56 us: grads(): pl.pallas_call(functools.partial(grad_kernel, slots, heads_per, old is No...]
    ppermute x10 -> x16, starting transfers between devices: 32.9 us -> 34.5 us  [send(): return lax.ppermute(array, 'ctx', [(i, to(i)) for i in range(length)])]
  transfers between devices with their start and end apart: 10 -> 16, of which waited for: 8 -> 9; matrix products, arithmetic and copies ran while one was open for 2% -> 3% of each run, Pallas kernels for 8% -> 13%
where the time goes in v4:
time: 73.3 us; the launch traced here: 73.1 us
  starting transfers between devices  34.5 us (47%)
  waiting for transfers between devices  20.4 us (28%)
  Pallas kernels  13.1 us (18%)
  local copies, waits for them, and re-layouts  4.28 us (6%)
  between operations  0.84 us (1%)
    ppermute x16, starting transfers between devices, send(): return lax.ppermute(array, 'ctx', [(i, to(i)) for i in range(length)])  34.5 us
    ppermute x16, waiting for transfers between devices, send(): return lax.ppermute(array, 'ctx', [(i, to(i)) for i in range(length)])  20.4 us
    pallas_call x7, Pallas kernels, grads(): pl.pallas_call(functools.partial(grad_kernel, slots, heads_per, old is No...  6.56 us
    pallas_call x6, Pallas kernels, stats(): pl.pallas_call(functools.partial(stats_kernel, slots, heads_per, old is N...  4.23 us
    unnamed x8, local copies, waits for them, and re-layouts  1.87 us
  transfers between devices with their start and end apart: 16, of which 9 were waited for; matrix products, arithmetic and copies ran while one was open for 3% of the time, Pallas kernels for 13%

profile of v4, /device:TPU:0, one launch (start us, length us, event | category | flops | bytes accessed | tf_op | source)
XLA Modules:
  0.0 73.1 jit_solution(10952332828808333064)
XLA Ops:
  0.6 0.0 copy-start
  0.7 1.0 %copy-done.1 = bf16[192,2,128]{2,1,0:T(2,128)(2,1)S(1)} copy-done((bf16[192,2,128]{2,1,0:T(2,128)(2,1)S(1)}, bf16[192,2,128]{2,1,0:T(2,128)(2,1)}, u32[]{:S(2)}) %copy-start.1) | copy-done | bytes 98328
  1.6 0.9 %copy-done.2 = bf16[192,2,128]{2,1,0:T(2,128)(2,1)S(1)} copy-done((bf16[192,2,128]{2,1,0:T(2,128)(2,1)S(1)}, bf16[192,2,128]{2,1,0:T(2,128)(2,1)}, u32[]{:S(2)}) %copy-start.2) | copy-done | bytes 98328
  2.5 0.1 shard_map.77.refs_4_.own_ref.refs_6_
  2.6 3.1 %collective-permute-start = (bf16[2,2,192,128]{3,2,1,0:T(8,128)(2,1)S(1)}, bf16[2,2,192,128]{3,2,1,0:T(8,128)(2,1)S(1)}, u32[]{:S(2)}, u32[]{:S(2)}) collective-permute-start(bf16[2,2,192,128]{3,2,1,0:T(8,128)(2,1)S(1)} %shard_map.77.refs_4_.own_ref.refs_6_), channel_id=1, source_target_pairs={{0,8},{2,10},{4,12},{6,14},{8,16},{10,18},{12,20},{14,22},{16,24},... | collective-permute-start | bytes 589832 | tf_op jit(solution)/shard_map/ppermute | solution.py:218
  5.7 1.4 %copy_bitcast_fusion.1 = (bf16[2,1536,128]{2,1,0:T(8,128)(2,1)S(1)}, bf16[2,1536,128]{2,1,0:T(8,128)(2,1)S(1)}) fusion(bf16[192,16,128]{2,1,0:T(8,128)(2,1)S(1)} %copy-done, bf16[192,16,128]{2,1,0:T(8,128)(2,1)} %param.8), kind=kLoop, calls=%fused_computation.1 | loop fusion | bytes 3145728 | tf_op jit(solution)/shard_map/reshape | solution.py:221
  7.1 1.2 %shard_map.76 = (s32[1,1536]{1,0:T(1,128)S(1)}, s32[2]{0:T(128)S(1)}) custom-call(s32[1]{0:T(128)} %bitcast.place_ref, s32[8]{0:T(128)S(1)} %copy-done.3), custom_call_target="tpu_custom_call" | custom-call | tf_op jit(solution)/shard_map/pallas_call | solution.py:244
  8.3 1.4 %shard_map.78 = (f32[2,1,1536]{2,1,0:T(1,128)S(1)}, f32[2,1,1536]{2,1,0:T(1,128)S(1)}, f32[2,1,1536]{2,1,0:T(1,128)S(1)}) custom-call(s32[2]{0:T(128)S(1)} %get-tuple-element.48.refs_0_, s32[1,1536]{1,0:T(1,128)S(1)} %get-tuple-element.49.refs_1_, bf16[2,1536,128]{2,1,0:T(8,128)(2,1)S(1)} %get-tuple-element.94.refs_2_, ...), custom_call_target="tpu_custom_call" | custom-call | flops 603979776 | bytes 1048576 | tf_op jit(solution)/shard_map/pallas_call | solution.py:259
  9.7 2.9 %collective-permute-done.refs_4_.refs_7_ = bf16[2,2,192,128]{3,2,1,0:T(8,128)(2,1)S(1)} collective-permute-done((bf16[2,2,192,128]{3,2,1,0:T(8,128)(2,1)S(1)}, bf16[2,2,192,128]{3,2,1,0:T(8,128)(2,1)S(1)}, u32[]{:S(2)}, u32[]{:S(2)}) %collective-permute-start) | collective-permute-done | bytes 196640 | tf_op jit(solution)/shard_map/ppermute | solution.py:218
  12.6 2.4 %collective-permute-start.5 = (bf16[2,2,192,128]{3,2,1,0:T(8,128)(2,1)S(1)}, bf16[2,2,192,128]{3,2,1,0:T(8,128)(2,1)S(1)}, u32[]{:S(2)}, u32[]{:S(2)}) collective-permute-start(bf16[2,2,192,128]{3,2,1,0:T(8,128)(2,1)S(1)} %collective-permute-done.refs_4_.refs_7_), channel_id=1, source_target_pairs={{0,6},{2,4},{4,2},{6,0},{8,14},{10,12},{12,10},{14,8},{16,22},{18,... | collective-permute-start | bytes 589832 | tf_op jit(solution)/shard_map/ppermute | solution.py:218
  15.1 0.5 collective-permute-start.6
  15.6 0.5 collective-permute-start.7
  16.1 4.4 %collective-permute-done.1.up2_ref = bf16[2,2,192,128]{3,2,1,0:T(8,128)(2,1)S(1)} collective-permute-done((bf16[2,2,192,128]{3,2,1,0:T(8,128)(2,1)S(1)}, bf16[2,2,192,128]{3,2,1,0:T(8,128)(2,1)S(1)}, u32[]{:S(2)}, u32[]{:S(2)}) %collective-permute-start.1) | collective-permute-done | bytes 196640 | tf_op jit(solution)/shard_map/ppermute | solution.py:218
  20.5 0.1 shard_map.79
  20.5 2.3 %collective-permute-start.4 = (bf16[2,2,192,128]{3,2,1,0:T(8,128)(2,1)S(1)}, bf16[2,2,192,128]{3,2,1,0:T(8,128)(2,1)S(1)}, u32[]{:S(2)}, u32[]{:S(2)}) collective-permute-start(bf16[2,2,192,128]{3,2,1,0:T(8,128)(2,1)S(1)} %get-tuple-element.56), channel_id=1, source_target_pairs={{0,6},{2,4},{4,2},{6,0},{8,14},{10,12},{12,10},{14,8},{16,22},{18,... | collective-permute-start | bytes 589832 | tf_op jit(solution)/shard_map/ppermute | solution.py:218
  22.8 0.5 shard_map.80
  23.4 0.6 collective-permute-start.3
  24.0 0.8 %collective-permute-start.2 = (bf16[2,2,192,128]{3,2,1,0:T(8,128)(2,1)S(1)}, bf16[2,2,192,128]{3,2,1,0:T(8,128)(2,1)S(1)}, u32[]{:S(2)}, u32[]{:S(2)}) collective-permute-start(bf16[2,2,192,128]{3,2,1,0:T(8,128)(2,1)S(1)} %get-tuple-element.54), channel_id=1, source_target_pairs={{0,2},{2,0},{4,6},{6,4},{8,10},{10,8},{12,14},{14,12},{16,18},{18,... | collective-permute-start | bytes 589832 | tf_op jit(solution)/shard_map/ppermute | solution.py:218
  24.7 2.7 %collective-permute-done.6.refs_5_.refs_6_ = bf16[2,2,192,128]{3,2,1,0:T(8,128)(2,1)S(1)} collective-permute-done((bf16[2,2,192,128]{3,2,1,0:T(8,128)(2,1)S(1)}, bf16[2,2,192,128]{3,2,1,0:T(8,128)(2,1)S(1)}, u32[]{:S(2)}, u32[]{:S(2)}) %collective-permute-start.6) | collective-permute-done | bytes 196640 | tf_op jit(solution)/shard_map/ppermute | solution.py:218
  27.4 0.6 shard_map.81
  28.0 1.4 %collective-permute-done.4.refs_4_.refs_6_ = bf16[2,2,192,128]{3,2,1,0:T(8,128)(2,1)S(1)} collective-permute-done((bf16[2,2,192,128]{3,2,1,0:T(8,128)(2,1)S(1)}, bf16[2,2,192,128]{3,2,1,0:T(8,128)(2,1)S(1)}, u32[]{:S(2)}, u32[]{:S(2)}) %collective-permute-start.4) | collective-permute-done | bytes 196640 | tf_op jit(solution)/shard_map/ppermute | solution.py:218
  29.3 0.6 shard_map.82
  29.9 2.3 %collective-permute-done.3.refs_4_.refs_6_ = bf16[2,2,192,128]{3,2,1,0:T(8,128)(2,1)S(1)} collective-permute-done((bf16[2,2,192,128]{3,2,1,0:T(8,128)(2,1)S(1)}, bf16[2,2,192,128]{3,2,1,0:T(8,128)(2,1)S(1)}, u32[]{:S(2)}, u32[]{:S(2)}) %collective-permute-start.3) | collective-permute-done | bytes 196640 | tf_op jit(solution)/shard_map/ppermute | solution.py:218
  32.2 0.6 shard_map.83
  32.8 0.6 shard_map.84
  33.4 0.7 shard_map.85
  34.0 0.8 %shard_map.86 = (bf16[2,2,192,128]{3,2,1,0:T(8,128)(2,1)S(1)}, f32[2,128,1536]{2,1,0:T(8,128)S(1)}) custom-call(s32[2]{0:T(128)S(1)} %get-tuple-element.48.refs_0_, s32[1,1536]{1,0:T(1,128)S(1)} %get-tuple-element.49.refs_1_, bf16[2,1536,128]{2,1,0:T(8,128)(2,1)S(1)} %get-tuple-element.94.refs_2_, ...), custom_call_target="tpu_custom_call", output_to_operand_aliasing={{1}: (7, {})} | custom-call | flops 1509949440 | bytes 1048576 | tf_op jit(solution)/shard_map/pallas_call | solution.py:271
  34.8 0.6 shard_map.87
  35.4 4.2 %collective-permute-start.10 = (bf16[2,2,192,128]{3,2,1,0:T(8,128)(2,1)S(1)}, bf16[2,2,192,128]{3,2,1,0:T(8,128)(2,1)S(1)}, u32[]{:S(2)}, u32[]{:S(2)}) collective-permute-start(bf16[2,2,192,128]{3,2,1,0:T(8,128)(2,1)S(1)} %get-tuple-element.83), channel_id=1, source_target_pairs={{0,2},{2,0},{4,6},{6,4},{8,10},{10,8},{12,14},{14,12},{16,18},{18,... | collective-permute-start | bytes 589832 | tf_op jit(solution)/shard_map/ppermute | solution.py:218
  39.6 1.9 %collective-permute-start.9 = (bf16[2,2,192,128]{3,2,1,0:T(8,128)(2,1)S(1)}, bf16[2,2,192,128]{3,2,1,0:T(8,128)(2,1)S(1)}, u32[]{:S(2)}, u32[]{:S(2)}) collective-permute-start(bf16[2,2,192,128]{3,2,1,0:T(8,128)(2,1)S(1)} %get-tuple-element.82), channel_id=1, source_target_pairs={{0,4},{2,6},{4,0},{6,2},{8,12},{10,14},{12,8},{14,10},{16,20},{18,... | collective-permute-start | bytes 589832 | tf_op jit(solution)/shard_map/ppermute | solution.py:218
  41.5 1.4 %collective-permute-start.8 = (bf16[2,2,192,128]{3,2,1,0:T(8,128)(2,1)S(1)}, bf16[2,2,192,128]{3,2,1,0:T(8,128)(2,1)S(1)}, u32[]{:S(2)}, u32[]{:S(2)}) collective-permute-start(bf16[2,2,192,128]{3,2,1,0:T(8,128)(2,1)S(1)} %get-tuple-element.81), channel_id=1, source_target_pairs={{0,6},{2,4},{4,2},{6,0},{8,14},{10,12},{12,10},{14,8},{16,22},{18,... | collective-permute-start | bytes 589832 | tf_op jit(solution)/shard_map/ppermute | solution.py:218
  42.9 0.6 shard_map.88
  43.5 0.6 shard_map.89
  44.0 0.6 shard_map.90
  44.6 0.6 collective-permute-start.14
  45.3 1.5 %collective-permute-start.13 = (bf16[2,2,192,128]{3,2,1,0:T(8,128)(2,1)S(1)}, bf16[2,2,192,128]{3,2,1,0:T(8,128)(2,1)S(1)}, u32[]{:S(2)}, u32[]{:S(2)}) collective-permute-start(bf16[2,2,192,128]{3,2,1,0:T(8,128)(2,1)S(1)} %get-tuple-element.89), channel_id=1, source_target_pairs={{0,4},{2,6},{4,0},{6,2},{8,12},{10,14},{12,8},{14,10},{16,20},{18,... | collective-permute-start | bytes 589832 | tf_op jit(solution)/shard_map/ppermute | solution.py:218
  46.8 1.8 %collective-permute-start.12 = (bf16[2,2,192,128]{3,2,1,0:T(8,128)(2,1)S(1)}, bf16[2,2,192,128]{3,2,1,0:T(8,128)(2,1)S(1)}, u32[]{:S(2)}, u32[]{:S(2)}) collective-permute-start(bf16[2,2,192,128]{3,2,1,0:T(8,128)(2,1)S(1)} %get-tuple-element.88), channel_id=1, source_target_pairs={{0,6},{2,4},{4,2},{6,0},{8,14},{10,12},{12,10},{14,8},{16,22},{18,... | collective-permute-start | bytes 589832 | tf_op jit(solution)/shard_map/ppermute | solution.py:218
  48.6 2.4 %collective-permute-done.9.refs_1_ = bf16[2,2,192,128]{3,2,1,0:T(8,128)(2,1)S(1)} collective-permute-done((bf16[2,2,192,128]{3,2,1,0:T(8,128)(2,1)S(1)}, bf16[2,2,192,128]{3,2,1,0:T(8,128)(2,1)S(1)}, u32[]{:S(2)}, u32[]{:S(2)}) %collective-permute-start.9) | collective-permute-done | bytes 196640 | tf_op jit(solution)/shard_map/ppermute | solution.py:218
  51.0 1.9 %collective-permute-done.8.refs_0_ = bf16[2,2,192,128]{3,2,1,0:T(8,128)(2,1)S(1)} collective-permute-done((bf16[2,2,192,128]{3,2,1,0:T(8,128)(2,1)S(1)}, bf16[2,2,192,128]{3,2,1,0:T(8,128)(2,1)S(1)}, u32[]{:S(2)}, u32[]{:S(2)}) %collective-permute-start.8) | collective-permute-done | bytes 196640 | tf_op jit(solution)/shard_map/ppermute | solution.py:218
  52.9 0.2 shard_map.92
  53.1 8.5 %collective-permute-start.11 = (bf16[2,2,192,128]{3,2,1,0:T(8,128)(2,1)S(1)}, bf16[2,2,192,128]{3,2,1,0:T(8,128)(2,1)S(1)}, u32[]{:S(2)}, u32[]{:S(2)}) collective-permute-start(bf16[2,2,192,128]{3,2,1,0:T(8,128)(2,1)S(1)} %get-tuple-element.87), channel_id=1, source_target_pairs={{0,24},{2,26},{4,28},{6,30},{8,0},{10,2},{12,4},{14,6},{16,8},{18,... | collective-permute-start | bytes 589832 | tf_op jit(solution)/shard_map/ppermute | solution.py:218
  61.6 2.8 %shard_map.91 = (bf16[2,2,192,128]{3,2,1,0:T(8,128)(2,1)S(1)}, bf16[2,2,192,128]{3,2,1,0:T(8,128)(2,1)S(1)}, bf16[2,1536,128]{2,1,0:T(8,128)(2,1)S(1)}, f32[2,128,1536]{2,1,0:T(8,128)S(1)}) custom-call(s32[2]{0:T(128)S(1)} %get-tuple-element.48.refs_0_, s32[1,1536]{1,0:T(1,128)S(1)} %get-tuple-element.49.refs_1_, ...), custom_call_target="tpu_custom_call", output_to_operand_aliasing={{3}: (8, {})} | custom-call | flops 3019898880 | bytes 1048576 | tf_op jit(solution)/shard_map/pallas_call | solution.py:271
  64.4 0.3 collective-permute-done.11.refs_1_
  64.8 0.1 shard_map.93
  64.9 4.3 %collective-permute-start.15 = (bf16[2,2,192,128]{3,2,1,0:T(8,128)(2,1)S(1)}, bf16[2,2,192,128]{3,2,1,0:T(8,128)(2,1)S(1)}, u32[]{:S(2)}, u32[]{:S(2)}) collective-permute-start(bf16[2,2,192,128]{3,2,1,0:T(8,128)(2,1)S(1)} %shard_map.93), channel_id=1, source_target_pairs={{0,24},{2,26},{4,28},{6,30},{8,0},{10,2},{12,4},{14,6},{16,8},{18,... | collective-permute-start | bytes 589832 | tf_op jit(solution)/shard_map/ppermute | solution.py:218
  69.2 1.0 %copy_bitcast_fusion = bf16[192,16,128]{2,1,0:T(8,128)(2,1)} fusion(bf16[2,1536,128]{2,1,0:T(8,128)(2,1)S(1)} %get-tuple-element.80), kind=kLoop, calls=%fused_computation | loop fusion | bytes 1572864 | tf_op jit(solution)/shard_map/reshape | solution.py:318
  70.2 2.2 %collective-permute-done.15.down_ref = bf16[2,2,192,128]{3,2,1,0:T(8,128)(2,1)S(1)} collective-permute-done((bf16[2,2,192,128]{3,2,1,0:T(8,128)(2,1)S(1)}, bf16[2,2,192,128]{3,2,1,0:T(8,128)(2,1)S(1)}, u32[]{:S(2)}, u32[]{:S(2)}) %collective-permute-start.15) | collective-permute-done | bytes 196640 | tf_op jit(solution)/shard_map/ppermute | solution.py:218
  72.4 0.7 shard_map.94
  (13 shorter events, 0.0 us)
Async XLA Ops:
  0.6 5.0 %copy-start = (bf16[192,16,128]{2,1,0:T(8,128)(2,1)S(1)}, bf16[192,16,128]{2,1,0:T(8,128)(2,1)}, u32[]{:S(2)}) copy-start(bf16[192,16,128]{2,1,0:T(8,128)(2,1)} %param.5) | copy-start | bytes 2359300
  0.6 1.0 %copy-start.1 = (bf16[192,2,128]{2,1,0:T(2,128)(2,1)S(1)}, bf16[192,2,128]{2,1,0:T(2,128)(2,1)}, u32[]{:S(2)}) copy-start(bf16[192,2,128]{2,1,0:T(2,128)(2,1)} %param.6) | copy-start | bytes 294916
  1.6 0.9 %copy-start.2 = (bf16[192,2,128]{2,1,0:T(2,128)(2,1)S(1)}, bf16[192,2,128]{2,1,0:T(2,128)(2,1)}, u32[]{:S(2)}) copy-start(bf16[192,2,128]{2,1,0:T(2,128)(2,1)} %param.7) | copy-start | bytes 294916
  2.6 4.5 %copy-start.3 = (s32[8]{0:T(128)S(1)}, s32[8]{0:T(128)}, u32[]{:S(2)}) copy-start(s32[8]{0:T(128)} %lens_ref.1) | copy-start | bytes 100
  2.6 10.0 %collective-permute-start = (bf16[2,2,192,128]{3,2,1,0:T(8,128)(2,1)S(1)}, bf16[2,2,192,128]{3,2,1,0:T(8,128)(2,1)S(1)}, u32[]{:S(2)}, u32[]{:S(2)}) collective-permute-start(bf16[2,2,192,128]{3,2,1,0:T(8,128)(2,1)S(1)} %shard_map.77.refs_4_.own_ref.refs_6_), channel_id=1, source_target_pairs={{0,8},{2,10},{4,12},{6,14},{8,16},{10,18},{12,20},{14,22},{16,24},... | collective-permute-start | bytes 589832 | tf_op jit(solution)/shard_map/ppermute | solution.py:218
  12.6 7.9 %collective-permute-start.1 = (bf16[2,2,192,128]{3,2,1,0:T(8,128)(2,1)S(1)}, bf16[2,2,192,128]{3,2,1,0:T(8,128)(2,1)S(1)}, u32[]{:S(2)}, u32[]{:S(2)}) collective-permute-start(bf16[2,2,192,128]{3,2,1,0:T(8,128)(2,1)S(1)} %collective-permute-done.refs_4_.refs_7_), channel_id=1, source_target_pairs={{0,8},{2,10},{4,12},{6,14},{8,16},{10,18},{12,20},{14,22},{16,24},... | collective-permute-start | bytes 589832 | tf_op jit(solution)/shard_map/ppermute | solution.py:218
  12.6 11.3 %collective-permute-start.5 = (bf16[2,2,192,128]{3,2,1,0:T(8,128)(2,1)S(1)}, bf16[2,2,192,128]{3,2,1,0:T(8,128)(2,1)S(1)}, u32[]{:S(2)}, u32[]{:S(2)}) collective-permute-start(bf16[2,2,192,128]{3,2,1,0:T(8,128)(2,1)S(1)} %collective-permute-done.refs_4_.refs_7_), channel_id=1, source_target_pairs={{0,6},{2,4},{4,2},{6,0},{8,14},{10,12},{12,10},{14,8},{16,22},{18,... | collective-permute-start | bytes 589832 | tf_op jit(solution)/shard_map/ppermute | solution.py:218
  15.1 12.3 %collective-permute-start.6 = (bf16[2,2,192,128]{3,2,1,0:T(8,128)(2,1)S(1)}, bf16[2,2,192,128]{3,2,1,0:T(8,128)(2,1)S(1)}, u32[]{:S(2)}, u32[]{:S(2)}) collective-permute-start(bf16[2,2,192,128]{3,2,1,0:T(8,128)(2,1)S(1)} %collective-permute-done.refs_4_.refs_7_), channel_id=1, source_target_pairs={{0,4},{2,6},{4,0},{6,2},{8,12},{10,14},{12,8},{14,10},{16,20},{18,... | collective-permute-start | bytes 589832 | tf_op jit(solution)/shard_map/ppermute | solution.py:218
  15.6 11.8 %collective-permute-start.7 = (bf16[2,2,192,128]{3,2,1,0:T(8,128)(2,1)S(1)}, bf16[2,2,192,128]{3,2,1,0:T(8,128)(2,1)S(1)}, u32[]{:S(2)}, u32[]{:S(2)}) collective-permute-start(bf16[2,2,192,128]{3,2,1,0:T(8,128)(2,1)S(1)} %collective-permute-done.refs_4_.refs_7_), channel_id=1, source_target_pairs={{0,2},{2,0},{4,6},{6,4},{8,10},{10,8},{12,14},{14,12},{16,18},{18,... | collective-permute-start | bytes 589832 | tf_op jit(solution)/shard_map/ppermute | solution.py:218
  20.5 8.8 %collective-permute-start.4 = (bf16[2,2,192,128]{3,2,1,0:T(8,128)(2,1)S(1)}, bf16[2,2,192,128]{3,2,1,0:T(8,128)(2,1)S(1)}, u32[]{:S(2)}, u32[]{:S(2)}) collective-permute-start(bf16[2,2,192,128]{3,2,1,0:T(8,128)(2,1)S(1)} %get-tuple-element.56), channel_id=1, source_target_pairs={{0,6},{2,4},{4,2},{6,0},{8,14},{10,12},{12,10},{14,8},{16,22},{18,... | collective-permute-start | bytes 589832 | tf_op jit(solution)/shard_map/ppermute | solution.py:218
  23.4 8.8 %collective-permute-start.3 = (bf16[2,2,192,128]{3,2,1,0:T(8,128)(2,1)S(1)}, bf16[2,2,192,128]{3,2,1,0:T(8,128)(2,1)S(1)}, u32[]{:S(2)}, u32[]{:S(2)}) collective-permute-start(bf16[2,2,192,128]{3,2,1,0:T(8,128)(2,1)S(1)} %get-tuple-element.55), channel_id=1, source_target_pairs={{0,4},{2,6},{4,0},{6,2},{8,12},{10,14},{12,8},{14,10},{16,20},{18,... | collective-permute-start | bytes 589832 | tf_op jit(solution)/shard_map/ppermute | solution.py:218
  24.0 8.8 %collective-permute-start.2 = (bf16[2,2,192,128]{3,2,1,0:T(8,128)(2,1)S(1)}, bf16[2,2,192,128]{3,2,1,0:T(8,128)(2,1)S(1)}, u32[]{:S(2)}, u32[]{:S(2)}) collective-permute-start(bf16[2,2,192,128]{3,2,1,0:T(8,128)(2,1)S(1)} %get-tuple-element.54), channel_id=1, source_target_pairs={{0,2},{2,0},{4,6},{6,4},{8,10},{10,8},{12,14},{14,12},{16,18},{18,... | collective-permute-start | bytes 589832 | tf_op jit(solution)/shard_map/ppermute | solution.py:218
  35.4 11.4 %collective-permute-start.10 = (bf16[2,2,192,128]{3,2,1,0:T(8,128)(2,1)S(1)}, bf16[2,2,192,128]{3,2,1,0:T(8,128)(2,1)S(1)}, u32[]{:S(2)}, u32[]{:S(2)}) collective-permute-start(bf16[2,2,192,128]{3,2,1,0:T(8,128)(2,1)S(1)} %get-tuple-element.83), channel_id=1, source_target_pairs={{0,2},{2,0},{4,6},{6,4},{8,10},{10,8},{12,14},{14,12},{16,18},{18,... | collective-permute-start | bytes 589832 | tf_op jit(solution)/shard_map/ppermute | solution.py:218
  39.6 11.4 %collective-permute-start.9 = (bf16[2,2,192,128]{3,2,1,0:T(8,128)(2,1)S(1)}, bf16[2,2,192,128]{3,2,1,0:T(8,128)(2,1)S(1)}, u32[]{:S(2)}, u32[]{:S(2)}) collective-permute-start(bf16[2,2,192,128]{3,2,1,0:T(8,128)(2,1)S(1)} %get-tuple-element.82), channel_id=1, source_target_pairs={{0,4},{2,6},{4,0},{6,2},{8,12},{10,14},{12,8},{14,10},{16,20},{18,... | collective-permute-start | bytes 589832 | tf_op jit(solution)/shard_map/ppermute | solution.py:218
  41.5 11.4 %collective-permute-start.8 = (bf16[2,2,192,128]{3,2,1,0:T(8,128)(2,1)S(1)}, bf16[2,2,192,128]{3,2,1,0:T(8,128)(2,1)S(1)}, u32[]{:S(2)}, u32[]{:S(2)}) collective-permute-start(bf16[2,2,192,128]{3,2,1,0:T(8,128)(2,1)S(1)} %get-tuple-element.81), channel_id=1, source_target_pairs={{0,6},{2,4},{4,2},{6,0},{8,14},{10,12},{12,10},{14,8},{16,22},{18,... | collective-permute-start | bytes 589832 | tf_op jit(solution)/shard_map/ppermute | solution.py:218
  44.6 19.8 %collective-permute-start.14 = (bf16[2,2,192,128]{3,2,1,0:T(8,128)(2,1)S(1)}, bf16[2,2,192,128]{3,2,1,0:T(8,128)(2,1)S(1)}, u32[]{:S(2)}, u32[]{:S(2)}) collective-permute-start(bf16[2,2,192,128]{3,2,1,0:T(8,128)(2,1)S(1)} %get-tuple-element.90), channel_id=1, source_target_pairs={{0,2},{2,0},{4,6},{6,4},{8,10},{10,8},{12,14},{14,12},{16,18},{18,... | collective-permute-start | bytes 589832 | tf_op jit(solution)/shard_map/ppermute | solution.py:218
  45.3 19.1 %collective-permute-start.13 = (bf16[2,2,192,128]{3,2,1,0:T(8,128)(2,1)S(1)}, bf16[2,2,192,128]{3,2,1,0:T(8,128)(2,1)S(1)}, u32[]{:S(2)}, u32[]{:S(2)}) collective-permute-start(bf16[2,2,192,128]{3,2,1,0:T(8,128)(2,1)S(1)} %get-tuple-element.89), channel_id=1, source_target_pairs={{0,4},{2,6},{4,0},{6,2},{8,12},{10,14},{12,8},{14,10},{16,20},{18,... | collective-permute-start | bytes 589832 | tf_op jit(solution)/shard_map/ppermute | solution.py:218
  46.8 17.6 %collective-permute-start.12 = (bf16[2,2,192,128]{3,2,1,0:T(8,128)(2,1)S(1)}, bf16[2,2,192,128]{3,2,1,0:T(8,128)(2,1)S(1)}, u32[]{:S(2)}, u32[]{:S(2)}) collective-permute-start(bf16[2,2,192,128]{3,2,1,0:T(8,128)(2,1)S(1)} %get-tuple-element.88), channel_id=1, source_target_pairs={{0,6},{2,4},{4,2},{6,0},{8,14},{10,12},{12,10},{14,8},{16,22},{18,... | collective-permute-start | bytes 589832 | tf_op jit(solution)/shard_map/ppermute | solution.py:218
  53.1 11.7 %collective-permute-start.11 = (bf16[2,2,192,128]{3,2,1,0:T(8,128)(2,1)S(1)}, bf16[2,2,192,128]{3,2,1,0:T(8,128)(2,1)S(1)}, u32[]{:S(2)}, u32[]{:S(2)}) collective-permute-start(bf16[2,2,192,128]{3,2,1,0:T(8,128)(2,1)S(1)} %get-tuple-element.87), channel_id=1, source_target_pairs={{0,24},{2,26},{4,28},{6,30},{8,0},{10,2},{12,4},{14,6},{16,8},{18,... | collective-permute-start | bytes 589832 | tf_op jit(solution)/shard_map/ppermute | solution.py:218
  64.9 7.5 %collective-permute-start.15 = (bf16[2,2,192,128]{3,2,1,0:T(8,128)(2,1)S(1)}, bf16[2,2,192,128]{3,2,1,0:T(8,128)(2,1)S(1)}, u32[]{:S(2)}, u32[]{:S(2)}) collective-permute-start(bf16[2,2,192,128]{3,2,1,0:T(8,128)(2,1)S(1)} %shard_map.93), channel_id=1, source_target_pairs={{0,24},{2,26},{4,28},{6,30},{8,0},{10,2},{12,4},{14,6},{16,8},{18,... | collective-permute-start | bytes 589832 | tf_op jit(solution)/shard_map/ppermute | solution.py:218

commit v5 on v4

--- a/solution.py
+++ b/solution.py
@@ -10,7 +10,8 @@
 
 
 PLANE = 4
-FLIPS = (3, 2, 1)
+FLIPS = (1, 2, 3)
+BACK = (2, 1, 0)
 LOG2E = math.log2(math.e)
 NEG_INIT = -1e30
 NEG_DEAD = -2e30
@@ -43,26 +44,22 @@
     return me - lane + other - jnp.where(other < lane, 0, 2 * PLANE)
 
 
-def first_live(place_ref):
+def first_live(place_ref, start_ref):
     me = place_ref[0]
-    return me, lax.rem(me, PLANE), place_ref[1]
-
-
-def start_kernel(heads_per, n_docs, place_ref, lens_ref, start_ref, info_ref):
+    return me, lax.rem(me, PLANE), jnp.min(start_ref[:, :128])
+
+
+def start_kernel(heads_per, n_docs, place_ref, lens_ref, start_ref):
     groups_cols = start_ref.shape
     stripe = groups_cols[1] // heads_per
     me = place_ref[0]
     col = lax.broadcasted_iota(jnp.int32, groups_cols, 1)
     start = jnp.zeros(groups_cols, jnp.int32)
     end = jnp.int32(0)
-    first_key = jnp.int32(0)
     for n in range(n_docs):
         end = end + lens_ref[n]
         start = jnp.where(col >= (end - me * stripe) * heads_per, end, start)
-        first_key = jnp.where(me * stripe >= end, end, first_key)
     start_ref[...] = start
-    info_ref[0] = me
-    info_ref[1] = first_key
 
 
 def logits(keys, q_g, base, start_ref, heads_per, causal, scale2):
@@ -85,7 +82,7 @@
     groups, _, dim = q_ref.shape
     stripe = kv_refs[0].shape[-2]
     scale2 = dim**-0.5 * LOG2E
-    me, lane, first_key = first_live(place_ref)
+    me, lane, first_key = first_live(place_ref, start_ref)
     if first:
         m_ref[...] = jnp.full_like(m_ref, NEG_INIT)
         l_ref[...] = jnp.zeros_like(l_ref)
@@ -124,7 +121,7 @@
     stripe = kv_refs[0].shape[-2]
     scale = dim**-0.5
     scale2 = scale * LOG2E
-    me, lane, first_key = first_live(place_ref)
+    me, lane, first_key = first_live(place_ref, start_ref)
     if first:
         dqt[...] = jnp.zeros_like(dqt)
     for kv_ref, part_ref, slot in zip(kv_refs, part_refs, slots):
@@ -152,10 +149,14 @@
             refs[n][g] = (dqt[g] * scale).T.astype(jnp.bfloat16)
 
 
-def pack_kernel(k_ref, v_ref, own_ref, wide):
+def pack_kernel(k_hbm, v_hbm, own_ref, wide, narrow, sems):
     groups, stripe = own_ref.shape[-3:-1]
-    for n, ref in enumerate((k_ref, v_ref)):
-        wide[...] = ref[...].astype(jnp.float32)
+    copies = [pltpu.make_async_copy(x, narrow.at[n], sems.at[n]) for n, x in enumerate((k_hbm, v_hbm))]
+    for copy in copies:
+        copy.start()
+    for n, copy in enumerate(copies):
+        copy.wait()
+        wide[...] = narrow[n].astype(jnp.float32)
         for g in range(groups):
             own_ref[n, g] = wide[pl.ds(g, stripe, stride=groups), :].astype(jnp.bfloat16)
 
@@ -220,11 +221,11 @@
     def columns(array):
         return array.reshape(stripe, groups, heads_per, dim).transpose(1, 0, 2, 3).reshape(groups, cols, dim)
 
-    def small(body, ins, shapes, scratch=()):
+    def small(body, ins, shapes, scratch=(), where=VMEM):
         return pl.pallas_call(
             body,
             out_shape=shapes,
-            in_specs=[SMEM if x is place else VMEM for x in ins],
+            in_specs=[SMEM if x is place else where for x in ins],
             out_specs=[VMEM] * len(shapes),
             scratch_shapes=list(scratch),
             compiler_params=pltpu.CompilerParams(vmem_limit_bytes=8 << 20),
@@ -235,17 +236,17 @@
 
     flat = (stripe * groups, dim)
     wide = pltpu.VMEM(flat, jnp.float32)
-    (own,) = small(pack_kernel, [key_vectors.reshape(flat), value_matrix.reshape(flat)], [shaped(jnp.bfloat16)], [wide])
+    (own,) = small(pack_kernel, [pltpu.with_memory_space_constraint(x.reshape(flat), pltpu.HBM) for x in (key_vectors, value_matrix)], [shaped(jnp.bfloat16)], [wide, pltpu.VMEM((2,) + flat, jnp.bfloat16), pltpu.SemaphoreType.DMA((2,))], pl.BlockSpec(memory_space=pltpu.HBM))
     q, do = columns(queries), columns(grad_out)
     stat = jax.ShapeDtypeStruct((groups, 1, cols), jnp.float32)
     total = jax.ShapeDtypeStruct((groups, dim, cols), jnp.float32)
     n_docs = doc_lengths.shape[0]
     pair_flops = groups * stripe * cols * dim * 2
-    start, info = pl.pallas_call(
+    (start,) = pl.pallas_call(
         functools.partial(start_kernel, heads_per, n_docs),
-        out_shape=[jax.ShapeDtypeStruct((1, cols), jnp.int32), jax.ShapeDtypeStruct((2,), jnp.int32)],
+        out_shape=[jax.ShapeDtypeStruct((1, cols), jnp.int32)],
         in_specs=[SMEM, SMEM],
-        out_specs=[VMEM, SMEM],
+        out_specs=[VMEM],
         compiler_params=pltpu.CompilerParams(vmem_limit_bytes=8 << 20),
     )(place, doc_lengths)
 
@@ -263,7 +264,7 @@
             out_specs=[VMEM] * 3,
             input_output_aliases={} if old is None else {4 + len(kvs) + i: i for i in range(3)},
             **params(2, len(kvs)),
-        )(info, start, q, do, *kvs, *(old or ()))
+        )(place, start, q, do, *kvs, *(old or ()))
 
     def grads(slots, kvs, old=None, last=False):
         n = len(kvs)
@@ -275,7 +276,7 @@
             out_specs=[VMEM] * (n + len(dq_shape)),
             input_output_aliases={} if old is None else {6 + n: n + len(dq_shape) - 1},
             **params(5, n),
-        )(info, start, q, do, m, d, *kvs, *(() if old is None else (old,)))
+        )(place, start, q, do, m, d, *kvs, *(() if old is None else (old,)))
         return outs[:n], outs[n]
 
     upx_slots = [functools.partial(upx_slot, f) for f in FLIPS]
@@ -295,21 +296,22 @@
     seen = stats([up_slot], [up], seen)
     outgoing = small(outgoing_kernel, [place, own, up2], [shaped(jnp.bfloat16)] * 3)
     mix = [swap(x, f) for x, f in zip(outgoing, FLIPS)]
-    seen = stats(upx_slots, upx, seen)
+    for k, f in enumerate(FLIPS):
+        seen = stats([upx_slots[k]], [upx[k]], seen)
     for k, f in enumerate(FLIPS):
         seen = stats([mix_slots[k]], [mix[k]], seen, last=k == 2)
     m, _, d = seen
 
     dq, mixed, level = None, [], []
-    for k, f in enumerate(FLIPS):
+    for k, f in zip(BACK, FLIPS[::-1]):
         (part,), dq = grads([mix_slots[k]], [mix[k]], dq)
         mixed.append(swap(part, f))
-    for k, f in enumerate(FLIPS):
+    for k, f in zip(BACK, FLIPS[::-1]):
         (part,), dq = grads([upx_slots[k]], [upx[k]], dq)
         level.append(swap(part, f))
     (own_part, up_part), dq = grads([own_slot, up_slot], [own, up], dq, last=True)
 
-    far, mine = small(far_kernel, [place, *mixed], [shaped(jnp.bfloat16), shaped(jnp.float32)])
+    far, mine = small(far_kernel, [place, *mixed[::-1]], [shaped(jnp.bfloat16), shaped(jnp.float32)])
     down2 = shift(far, -PLANE)
     (below,) = small(level_kernel, [up_part, down2, *level], [shaped(jnp.bfloat16)])
     down = shift(below, -PLANE)

time: 73.3 us -> 71 us (0.969)
  waiting for transfers between devices: 20.4 us -> 24.7 us
  Pallas kernels: 13.1 us -> 9.3 us
  local copies, waits for them, and re-layouts: 4.28 us -> 2.43 us
  starting transfers between devices: 34.5 us -> 33.5 us
    ppermute x16, waiting for transfers between devices: 20.4 us -> 24.7 us  [send(): return lax.ppermute(array, 'ctx', [(i, to(i)) for i in range(length)])]
    pallas_call x7, Pallas kernels: 6.56 us -> 4.03 us  [grads(): pl.pallas_call(functools.partial(grad_kernel, slots, heads_per, old is No...]
    unnamed x8 -> x4, local copies, waits for them, and re-layouts: 1.87 us -> 0.02 us
    pallas_call x6 -> x8, Pallas kernels: 4.23 us -> 2.52 us  [stats(): pl.pallas_call(functools.partial(stats_kernel, slots, heads_per, old is N...]
    pallas_call x5, Pallas kernels: 1.17 us -> 2.17 us  [small(): pl.pallas_call(body, out_shape=shapes, in_specs=[SMEM if x is place else...]
    ppermute x16, starting transfers between devices: 34.5 us -> 33.5 us  [send(): return lax.ppermute(array, 'ctx', [(i, to(i)) for i in range(length)])]
  transfers between devices with their start and end apart: 16 -> 16, of which waited for: 9 -> 9; matrix products, arithmetic and copies ran while one was open for 3% -> 3% of each run, Pallas kernels for 13% -> 9%
where the time goes in v5:
time: 71 us; the launch traced here: 70.8 us
  starting transfers between devices  33.5 us (47%)
  waiting for transfers between devices  24.7 us (35%)
  Pallas kernels  9.3 us (13%)
  local copies, waits for them, and re-layouts  2.43 us (3%)
  between operations  0.86 us (1%)
    ppermute x16, starting transfers between devices, send(): return lax.ppermute(array, 'ctx', [(i, to(i)) for i in range(length)])  33.5 us
    ppermute x16, waiting for transfers between devices, send(): return lax.ppermute(array, 'ctx', [(i, to(i)) for i in range(length)])  24.7 us
    pallas_call x7, Pallas kernels, grads(): pl.pallas_call(functools.partial(grad_kernel, slots, heads_per, old is No...  4.03 us
    pallas_call x8, Pallas kernels, stats(): pl.pallas_call(functools.partial(stats_kernel, slots, heads_per, old is N...  2.52 us
    pallas_call x5, Pallas kernels, small(): pl.pallas_call(body, out_shape=shapes, in_specs=[SMEM if x is place else...  2.17 us
  transfers between devices with their start and end apart: 16, of which 9 were waited for; matrix products, arithmetic and copies ran while one was open for 3% of the time, Pallas kernels for 9%

profile of v5, /device:TPU:0, one launch (start us, length us, event | category | flops | bytes accessed | tf_op | source)
XLA Modules:
  0.0 70.8 jit_solution(3420773793251014757)
XLA Ops:
  0.6 0.0 copy-start
  0.6 1.1 %shard_map.77.refs_4_.own_ref.refs_6_ = bf16[2,2,192,128]{3,2,1,0:T(8,128)(2,1)S(1)} custom-call(bf16[384,128]{1,0:T(8,128)(2,1)} %bitcast.26, bf16[384,128]{1,0:T(8,128)(2,1)} %bitcast.27), custom_call_target="tpu_custom_call" | custom-call | tf_op jit(solution)/shard_map/pallas_call | solution.py:225
  1.7 3.1 %collective-permute-start = (bf16[2,2,192,128]{3,2,1,0:T(8,128)(2,1)S(1)}, bf16[2,2,192,128]{3,2,1,0:T(8,128)(2,1)S(1)}, u32[]{:S(2)}, u32[]{:S(2)}) collective-permute-start(bf16[2,2,192,128]{3,2,1,0:T(8,128)(2,1)S(1)} %shard_map.77.refs_4_.own_ref.refs_6_), channel_id=1, source_target_pairs={{0,8},{2,10},{4,12},{6,14},{8,16},{10,18},{12,20},{14,22},{16,24},... | collective-permute-start | bytes 589832 | tf_op jit(solution)/shard_map/ppermute | solution.py:219
  4.8 1.4 %copy_bitcast_fusion.1 = (bf16[2,1536,128]{2,1,0:T(8,128)(2,1)S(1)}, bf16[2,1536,128]{2,1,0:T(8,128)(2,1)S(1)}) fusion(bf16[192,16,128]{2,1,0:T(8,128)(2,1)S(1)} %copy-done, bf16[192,16,128]{2,1,0:T(8,128)(2,1)} %param.8), kind=kLoop, calls=%fused_computation.1 | loop fusion | bytes 3145728 | tf_op jit(solution)/shard_map/reshape | solution.py:222
  6.3 0.6 shard_map.76.refs_1_
  6.8 1.1 %shard_map.78 = (f32[2,1,1536]{2,1,0:T(1,128)S(1)}, f32[2,1,1536]{2,1,0:T(1,128)S(1)}, f32[2,1,1536]{2,1,0:T(1,128)S(1)}) custom-call(s32[1]{0:T(128)} %bitcast.place_ref.refs_0_, s32[1,1536]{1,0:T(1,128)S(1)} %shard_map.76.refs_1_, bf16[2,1536,128]{2,1,0:T(8,128)(2,1)S(1)} %get-tuple-element.102.refs_2_, ...), custom_call_target="tpu_custom_call" | custom-call | flops 603979776 | bytes 1048576 | tf_op jit(solution)/shard_map/pallas_call | solution.py:260
  7.9 3.8 %collective-permute-done.refs_4_.refs_7_ = bf16[2,2,192,128]{3,2,1,0:T(8,128)(2,1)S(1)} collective-permute-done((bf16[2,2,192,128]{3,2,1,0:T(8,128)(2,1)S(1)}, bf16[2,2,192,128]{3,2,1,0:T(8,128)(2,1)S(1)}, u32[]{:S(2)}, u32[]{:S(2)}) %collective-permute-start) | collective-permute-done | bytes 196640 | tf_op jit(solution)/shard_map/ppermute | solution.py:219
  11.8 1.5 %collective-permute-start.7 = (bf16[2,2,192,128]{3,2,1,0:T(8,128)(2,1)S(1)}, bf16[2,2,192,128]{3,2,1,0:T(8,128)(2,1)S(1)}, u32[]{:S(2)}, u32[]{:S(2)}) collective-permute-start(bf16[2,2,192,128]{3,2,1,0:T(8,128)(2,1)S(1)} %collective-permute-done.refs_4_.refs_7_), channel_id=1, source_target_pairs={{0,2},{2,0},{4,6},{6,4},{8,10},{10,8},{12,14},{14,12},{16,18},{18,... | collective-permute-start | bytes 589832 | tf_op jit(solution)/shard_map/ppermute | solution.py:219
  13.2 1.5 %collective-permute-start.6 = (bf16[2,2,192,128]{3,2,1,0:T(8,128)(2,1)S(1)}, bf16[2,2,192,128]{3,2,1,0:T(8,128)(2,1)S(1)}, u32[]{:S(2)}, u32[]{:S(2)}) collective-permute-start(bf16[2,2,192,128]{3,2,1,0:T(8,128)(2,1)S(1)} %collective-permute-done.refs_4_.refs_7_), channel_id=1, source_target_pairs={{0,4},{2,6},{4,0},{6,2},{8,12},{10,14},{12,8},{14,10},{16,20},{18,... | collective-permute-start | bytes 589832 | tf_op jit(solution)/shard_map/ppermute | solution.py:219
  14.8 0.5 collective-permute-start.5
  15.2 4.4 %collective-permute-done.1.up2_ref = bf16[2,2,192,128]{3,2,1,0:T(8,128)(2,1)S(1)} collective-permute-done((bf16[2,2,192,128]{3,2,1,0:T(8,128)(2,1)S(1)}, bf16[2,2,192,128]{3,2,1,0:T(8,128)(2,1)S(1)}, u32[]{:S(2)}, u32[]{:S(2)}) %collective-permute-start.1) | collective-permute-done | bytes 196640 | tf_op jit(solution)/shard_map/ppermute | solution.py:219
  19.6 0.1 shard_map.79
  19.7 1.3 %collective-permute-start.4 = (bf16[2,2,192,128]{3,2,1,0:T(8,128)(2,1)S(1)}, bf16[2,2,192,128]{3,2,1,0:T(8,128)(2,1)S(1)}, u32[]{:S(2)}, u32[]{:S(2)}) collective-permute-start(bf16[2,2,192,128]{3,2,1,0:T(8,128)(2,1)S(1)} %get-tuple-element.58), channel_id=1, source_target_pairs={{0,2},{2,0},{4,6},{6,4},{8,10},{10,8},{12,14},{14,12},{16,18},{18,... | collective-permute-start | bytes 589832 | tf_op jit(solution)/shard_map/ppermute | solution.py:219
  21.0 0.2 shard_map.80
  21.2 1.6 %collective-permute-start.2 = (bf16[2,2,192,128]{3,2,1,0:T(8,128)(2,1)S(1)}, bf16[2,2,192,128]{3,2,1,0:T(8,128)(2,1)S(1)}, u32[]{:S(2)}, u32[]{:S(2)}) collective-permute-start(bf16[2,2,192,128]{3,2,1,0:T(8,128)(2,1)S(1)} %get-tuple-element.56), channel_id=1, source_target_pairs={{0,6},{2,4},{4,2},{6,0},{8,14},{10,12},{12,10},{14,8},{16,22},{18,... | collective-permute-start | bytes 589832 | tf_op jit(solution)/shard_map/ppermute | solution.py:219
  22.8 0.7 %collective-permute-start.3 = (bf16[2,2,192,128]{3,2,1,0:T(8,128)(2,1)S(1)}, bf16[2,2,192,128]{3,2,1,0:T(8,128)(2,1)S(1)}, u32[]{:S(2)}, u32[]{:S(2)}) collective-permute-start(bf16[2,2,192,128]{3,2,1,0:T(8,128)(2,1)S(1)} %get-tuple-element.57), channel_id=1, source_target_pairs={{0,4},{2,6},{4,0},{6,2},{8,12},{10,14},{12,8},{14,10},{16,20},{18,... | collective-permute-start | bytes 589832 | tf_op jit(solution)/shard_map/ppermute | solution.py:219
  23.5 0.2 shard_map.81
  23.7 0.2 shard_map.82
  23.9 0.3 collective-permute-done.5.refs_4_.refs_6_
  24.3 0.2 shard_map.83
  24.5 3.1 %collective-permute-done.4.refs_4_.refs_6_ = bf16[2,2,192,128]{3,2,1,0:T(8,128)(2,1)S(1)} collective-permute-done((bf16[2,2,192,128]{3,2,1,0:T(8,128)(2,1)S(1)}, bf16[2,2,192,128]{3,2,1,0:T(8,128)(2,1)S(1)}, u32[]{:S(2)}, u32[]{:S(2)}) %collective-permute-start.4) | collective-permute-done | bytes 196640 | tf_op jit(solution)/shard_map/ppermute | solution.py:219
  27.6 0.2 shard_map.84
  27.8 4.4 %collective-permute-done.3.refs_4_.refs_6_ = bf16[2,2,192,128]{3,2,1,0:T(8,128)(2,1)S(1)} collective-permute-done((bf16[2,2,192,128]{3,2,1,0:T(8,128)(2,1)S(1)}, bf16[2,2,192,128]{3,2,1,0:T(8,128)(2,1)S(1)}, u32[]{:S(2)}, u32[]{:S(2)}) %collective-permute-start.3) | collective-permute-done | bytes 196640 | tf_op jit(solution)/shard_map/ppermute | solution.py:219
  32.2 0.2 shard_map.85
  32.5 0.2 shard_map.86
  32.7 0.2 shard_map.87
  32.9 0.4 shard_map.88
  33.3 0.2 shard_map.89
  33.6 3.3 %collective-permute-start.8 = (bf16[2,2,192,128]{3,2,1,0:T(8,128)(2,1)S(1)}, bf16[2,2,192,128]{3,2,1,0:T(8,128)(2,1)S(1)}, u32[]{:S(2)}, u32[]{:S(2)}) collective-permute-start(bf16[2,2,192,128]{3,2,1,0:T(8,128)(2,1)S(1)} %get-tuple-element.89), channel_id=1, source_target_pairs={{0,2},{2,0},{4,6},{6,4},{8,10},{10,8},{12,14},{14,12},{16,18},{18,... | collective-permute-start | bytes 589832 | tf_op jit(solution)/shard_map/ppermute | solution.py:219
  36.9 3.4 %collective-permute-start.9 = (bf16[2,2,192,128]{3,2,1,0:T(8,128)(2,1)S(1)}, bf16[2,2,192,128]{3,2,1,0:T(8,128)(2,1)S(1)}, u32[]{:S(2)}, u32[]{:S(2)}) collective-permute-start(bf16[2,2,192,128]{3,2,1,0:T(8,128)(2,1)S(1)} %get-tuple-element.90), channel_id=1, source_target_pairs={{0,4},{2,6},{4,0},{6,2},{8,12},{10,14},{12,8},{14,10},{16,20},{18,... | collective-permute-start | bytes 589832 | tf_op jit(solution)/shard_map/ppermute | solution.py:219
  40.3 1.4 %collective-permute-start.10 = (bf16[2,2,192,128]{3,2,1,0:T(8,128)(2,1)S(1)}, bf16[2,2,192,128]{3,2,1,0:T(8,128)(2,1)S(1)}, u32[]{:S(2)}, u32[]{:S(2)}) collective-permute-start(bf16[2,2,192,128]{3,2,1,0:T(8,128)(2,1)S(1)} %get-tuple-element.91), channel_id=1, source_target_pairs={{0,6},{2,4},{4,2},{6,0},{8,14},{10,12},{12,10},{14,8},{16,22},{18,... | collective-permute-start | bytes 589832 | tf_op jit(solution)/shard_map/ppermute | solution.py:219
  41.7 0.2 shard_map.90
  41.9 0.2 shard_map.91
  42.1 0.2 shard_map.92
  42.4 0.6 collective-permute-start.14
  43.0 1.5 %collective-permute-start.13 = (bf16[2,2,192,128]{3,2,1,0:T(8,128)(2,1)S(1)}, bf16[2,2,192,128]{3,2,1,0:T(8,128)(2,1)S(1)}, u32[]{:S(2)}, u32[]{:S(2)}) collective-permute-start(bf16[2,2,192,128]{3,2,1,0:T(8,128)(2,1)S(1)} %get-tuple-element.97), channel_id=1, source_target_pairs={{0,4},{2,6},{4,0},{6,2},{8,12},{10,14},{12,8},{14,10},{16,20},{18,... | collective-permute-start | bytes 589832 | tf_op jit(solution)/shard_map/ppermute | solution.py:219
  44.5 2.9 %collective-permute-start.12 = (bf16[2,2,192,128]{3,2,1,0:T(8,128)(2,1)S(1)}, bf16[2,2,192,128]{3,2,1,0:T(8,128)(2,1)S(1)}, u32[]{:S(2)}, u32[]{:S(2)}) collective-permute-start(bf16[2,2,192,128]{3,2,1,0:T(8,128)(2,1)S(1)} %get-tuple-element.96), channel_id=1, source_target_pairs={{0,6},{2,4},{4,2},{6,0},{8,14},{10,12},{12,10},{14,8},{16,22},{18,... | collective-permute-start | bytes 589832 | tf_op jit(solution)/shard_map/ppermute | solution.py:219
  47.4 2.2 %collective-permute-done.9.refs_1_ = bf16[2,2,192,128]{3,2,1,0:T(8,128)(2,1)S(1)} collective-permute-done((bf16[2,2,192,128]{3,2,1,0:T(8,128)(2,1)S(1)}, bf16[2,2,192,128]{3,2,1,0:T(8,128)(2,1)S(1)}, u32[]{:S(2)}, u32[]{:S(2)}) %collective-permute-start.9) | collective-permute-done | bytes 196640 | tf_op jit(solution)/shard_map/ppermute | solution.py:219
  49.6 1.8 %collective-permute-done.10.refs_2_ = bf16[2,2,192,128]{3,2,1,0:T(8,128)(2,1)S(1)} collective-permute-done((bf16[2,2,192,128]{3,2,1,0:T(8,128)(2,1)S(1)}, bf16[2,2,192,128]{3,2,1,0:T(8,128)(2,1)S(1)}, u32[]{:S(2)}, u32[]{:S(2)}) %collective-permute-start.10) | collective-permute-done | bytes 196640 | tf_op jit(solution)/shard_map/ppermute | solution.py:219
  51.4 0.2 shard_map.94
  51.6 5.9 %collective-permute-start.11 = (bf16[2,2,192,128]{3,2,1,0:T(8,128)(2,1)S(1)}, bf16[2,2,192,128]{3,2,1,0:T(8,128)(2,1)S(1)}, u32[]{:S(2)}, u32[]{:S(2)}) collective-permute-start(bf16[2,2,192,128]{3,2,1,0:T(8,128)(2,1)S(1)} %get-tuple-element.95), channel_id=1, source_target_pairs={{0,24},{2,26},{4,28},{6,30},{8,0},{10,2},{12,4},{14,6},{16,8},{18,... | collective-permute-start | bytes 589832 | tf_op jit(solution)/shard_map/ppermute | solution.py:219
  57.5 2.5 %shard_map.93 = (bf16[2,2,192,128]{3,2,1,0:T(8,128)(2,1)S(1)}, bf16[2,2,192,128]{3,2,1,0:T(8,128)(2,1)S(1)}, bf16[2,1536,128]{2,1,0:T(8,128)(2,1)S(1)}, f32[2,128,1536]{2,1,0:T(8,128)S(1)}) custom-call(s32[1]{0:T(128)} %bitcast.place_ref.refs_0_, s32[1,1536]{1,0:T(1,128)S(1)} %shard_map.76.refs_1_, ...), custom_call_target="tpu_custom_call", output_to_operand_aliasing={{3}: (8, {})} | custom-call | flops 3019898880 | bytes 1048576 | tf_op jit(solution)/shard_map/pallas_call | solution.py:272
  60.0 2.4 %collective-permute-done.11.refs_1_ = bf16[2,2,192,128]{3,2,1,0:T(8,128)(2,1)S(1)} collective-permute-done((bf16[2,2,192,128]{3,2,1,0:T(8,128)(2,1)S(1)}, bf16[2,2,192,128]{3,2,1,0:T(8,128)(2,1)S(1)}, u32[]{:S(2)}, u32[]{:S(2)}) %collective-permute-start.11) | collective-permute-done | bytes 196640 | tf_op jit(solution)/shard_map/ppermute | solution.py:219
  62.4 0.1 shard_map.95
  62.5 4.3 %collective-permute-start.15 = (bf16[2,2,192,128]{3,2,1,0:T(8,128)(2,1)S(1)}, bf16[2,2,192,128]{3,2,1,0:T(8,128)(2,1)S(1)}, u32[]{:S(2)}, u32[]{:S(2)}) collective-permute-start(bf16[2,2,192,128]{3,2,1,0:T(8,128)(2,1)S(1)} %shard_map.95), channel_id=1, source_target_pairs={{0,24},{2,26},{4,28},{6,30},{8,0},{10,2},{12,4},{14,6},{16,8},{18,... | collective-permute-start | bytes 589832 | tf_op jit(solution)/shard_map/ppermute | solution.py:219
  66.9 1.0 %copy_bitcast_fusion = bf16[192,16,128]{2,1,0:T(8,128)(2,1)} fusion(bf16[2,1536,128]{2,1,0:T(8,128)(2,1)S(1)} %get-tuple-element.88), kind=kLoop, calls=%fused_computation | loop fusion | bytes 1572864 | tf_op jit(solution)/shard_map/reshape | solution.py:320
  67.9 2.2 %collective-permute-done.15.down_ref = bf16[2,2,192,128]{3,2,1,0:T(8,128)(2,1)S(1)} collective-permute-done((bf16[2,2,192,128]{3,2,1,0:T(8,128)(2,1)S(1)}, bf16[2,2,192,128]{3,2,1,0:T(8,128)(2,1)S(1)}, u32[]{:S(2)}, u32[]{:S(2)}) %collective-permute-start.15) | collective-permute-done | bytes 196640 | tf_op jit(solution)/shard_map/ppermute | solution.py:219
  70.1 0.7 %shard_map.96 = (bf16[384,128]{1,0:T(8,128)(2,1)}, bf16[384,128]{1,0:T(8,128)(2,1)}) custom-call(f32[2,2,192,128]{3,2,1,0:T(8,128)S(1)} %get-tuple-element.92.mine_ref, bf16[2,2,192,128]{3,2,1,0:T(8,128)(2,1)S(1)} %get-tuple-element.93.own_ref, bf16[2,2,192,128]{3,2,1,0:T(8,128)(2,1)S(1)} %collective-permute-done.15.down_ref), custom_call_target="tpu_custom_call" | custom-call | tf_op jit(solution)/shard_map/pallas_call | solution.py:225
  (11 shorter events, 0.0 us)
Async XLA Ops:
  0.6 4.2 %copy-start = (bf16[192,16,128]{2,1,0:T(8,128)(2,1)S(1)}, bf16[192,16,128]{2,1,0:T(8,128)(2,1)}, u32[]{:S(2)}) copy-start(bf16[192,16,128]{2,1,0:T(8,128)(2,1)} %param.5) | copy-start | bytes 2359300
  1.7 4.5 %copy-start.1 = (s32[8]{0:T(128)S(1)}, s32[8]{0:T(128)}, u32[]{:S(2)}) copy-start(s32[8]{0:T(128)} %lens_ref.1) | copy-start | bytes 100
  1.7 10.0 %collective-permute-start = (bf16[2,2,192,128]{3,2,1,0:T(8,128)(2,1)S(1)}, bf16[2,2,192,128]{3,2,1,0:T(8,128)(2,1)S(1)}, u32[]{:S(2)}, u32[]{:S(2)}) collective-permute-start(bf16[2,2,192,128]{3,2,1,0:T(8,128)(2,1)S(1)} %shard_map.77.refs_4_.own_ref.refs_6_), channel_id=1, source_target_pairs={{0,8},{2,10},{4,12},{6,14},{8,16},{10,18},{12,20},{14,22},{16,24},... | collective-permute-start | bytes 589832 | tf_op jit(solution)/shard_map/ppermute | solution.py:219
  11.8 7.9 %collective-permute-start.1 = (bf16[2,2,192,128]{3,2,1,0:T(8,128)(2,1)S(1)}, bf16[2,2,192,128]{3,2,1,0:T(8,128)(2,1)S(1)}, u32[]{:S(2)}, u32[]{:S(2)}) collective-permute-start(bf16[2,2,192,128]{3,2,1,0:T(8,128)(2,1)S(1)} %collective-permute-done.refs_4_.refs_7_), channel_id=1, source_target_pairs={{0,8},{2,10},{4,12},{6,14},{8,16},{10,18},{12,20},{14,22},{16,24},... | collective-permute-start | bytes 589832 | tf_op jit(solution)/shard_map/ppermute | solution.py:219
  11.8 11.0 %collective-permute-start.7 = (bf16[2,2,192,128]{3,2,1,0:T(8,128)(2,1)S(1)}, bf16[2,2,192,128]{3,2,1,0:T(8,128)(2,1)S(1)}, u32[]{:S(2)}, u32[]{:S(2)}) collective-permute-start(bf16[2,2,192,128]{3,2,1,0:T(8,128)(2,1)S(1)} %collective-permute-done.refs_4_.refs_7_), channel_id=1, source_target_pairs={{0,2},{2,0},{4,6},{6,4},{8,10},{10,8},{12,14},{14,12},{16,18},{18,... | collective-permute-start | bytes 589832 | tf_op jit(solution)/shard_map/ppermute | solution.py:219
  13.2 10.5 %collective-permute-start.6 = (bf16[2,2,192,128]{3,2,1,0:T(8,128)(2,1)S(1)}, bf16[2,2,192,128]{3,2,1,0:T(8,128)(2,1)S(1)}, u32[]{:S(2)}, u32[]{:S(2)}) collective-permute-start(bf16[2,2,192,128]{3,2,1,0:T(8,128)(2,1)S(1)} %collective-permute-done.refs_4_.refs_7_), channel_id=1, source_target_pairs={{0,4},{2,6},{4,0},{6,2},{8,12},{10,14},{12,8},{14,10},{16,20},{18,... | collective-permute-start | bytes 589832 | tf_op jit(solution)/shard_map/ppermute | solution.py:219
  14.8 9.5 %collective-permute-start.5 = (bf16[2,2,192,128]{3,2,1,0:T(8,128)(2,1)S(1)}, bf16[2,2,192,128]{3,2,1,0:T(8,128)(2,1)S(1)}, u32[]{:S(2)}, u32[]{:S(2)}) collective-permute-start(bf16[2,2,192,128]{3,2,1,0:T(8,128)(2,1)S(1)} %collective-permute-done.refs_4_.refs_7_), channel_id=1, source_target_pairs={{0,6},{2,4},{4,2},{6,0},{8,14},{10,12},{12,10},{14,8},{16,22},{18,... | collective-permute-start | bytes 589832 | tf_op jit(solution)/shard_map/ppermute | solution.py:219
  19.7 8.0 %collective-permute-start.4 = (bf16[2,2,192,128]{3,2,1,0:T(8,128)(2,1)S(1)}, bf16[2,2,192,128]{3,2,1,0:T(8,128)(2,1)S(1)}, u32[]{:S(2)}, u32[]{:S(2)}) collective-permute-start(bf16[2,2,192,128]{3,2,1,0:T(8,128)(2,1)S(1)} %get-tuple-element.58), channel_id=1, source_target_pairs={{0,2},{2,0},{4,6},{6,4},{8,10},{10,8},{12,14},{14,12},{16,18},{18,... | collective-permute-start | bytes 589832 | tf_op jit(solution)/shard_map/ppermute | solution.py:219
  21.2 11.2 %collective-permute-start.2 = (bf16[2,2,192,128]{3,2,1,0:T(8,128)(2,1)S(1)}, bf16[2,2,192,128]{3,2,1,0:T(8,128)(2,1)S(1)}, u32[]{:S(2)}, u32[]{:S(2)}) collective-permute-start(bf16[2,2,192,128]{3,2,1,0:T(8,128)(2,1)S(1)} %get-tuple-element.56), channel_id=1, source_target_pairs={{0,6},{2,4},{4,2},{6,0},{8,14},{10,12},{12,10},{14,8},{16,22},{18,... | collective-permute-start | bytes 589832 | tf_op jit(solution)/shard_map/ppermute | solution.py:219
  22.8 9.4 %collective-permute-start.3 = (bf16[2,2,192,128]{3,2,1,0:T(8,128)(2,1)S(1)}, bf16[2,2,192,128]{3,2,1,0:T(8,128)(2,1)S(1)}, u32[]{:S(2)}, u32[]{:S(2)}) collective-permute-start(bf16[2,2,192,128]{3,2,1,0:T(8,128)(2,1)S(1)} %get-tuple-element.57), channel_id=1, source_target_pairs={{0,4},{2,6},{4,0},{6,2},{8,12},{10,14},{12,8},{14,10},{16,20},{18,... | collective-permute-start | bytes 589832 | tf_op jit(solution)/shard_map/ppermute | solution.py:219
  33.6 11.0 %collective-permute-start.8 = (bf16[2,2,192,128]{3,2,1,0:T(8,128)(2,1)S(1)}, bf16[2,2,192,128]{3,2,1,0:T(8,128)(2,1)S(1)}, u32[]{:S(2)}, u32[]{:S(2)}) collective-permute-start(bf16[2,2,192,128]{3,2,1,0:T(8,128)(2,1)S(1)} %get-tuple-element.89), channel_id=1, source_target_pairs={{0,2},{2,0},{4,6},{6,4},{8,10},{10,8},{12,14},{14,12},{16,18},{18,... | collective-permute-start | bytes 589832 | tf_op jit(solution)/shard_map/ppermute | solution.py:219
  36.9 12.7 %collective-permute-start.9 = (bf16[2,2,192,128]{3,2,1,0:T(8,128)(2,1)S(1)}, bf16[2,2,192,128]{3,2,1,0:T(8,128)(2,1)S(1)}, u32[]{:S(2)}, u32[]{:S(2)}) collective-permute-start(bf16[2,2,192,128]{3,2,1,0:T(8,128)(2,1)S(1)} %get-tuple-element.90), channel_id=1, source_target_pairs={{0,4},{2,6},{4,0},{6,2},{8,12},{10,14},{12,8},{14,10},{16,20},{18,... | collective-permute-start | bytes 589832 | tf_op jit(solution)/shard_map/ppermute | solution.py:219
  40.3 11.1 %collective-permute-start.10 = (bf16[2,2,192,128]{3,2,1,0:T(8,128)(2,1)S(1)}, bf16[2,2,192,128]{3,2,1,0:T(8,128)(2,1)S(1)}, u32[]{:S(2)}, u32[]{:S(2)}) collective-permute-start(bf16[2,2,192,128]{3,2,1,0:T(8,128)(2,1)S(1)} %get-tuple-element.91), channel_id=1, source_target_pairs={{0,6},{2,4},{4,2},{6,0},{8,14},{10,12},{12,10},{14,8},{16,22},{18,... | collective-permute-start | bytes 589832 | tf_op jit(solution)/shard_map/ppermute | solution.py:219
  42.4 17.6 %collective-permute-start.14 = (bf16[2,2,192,128]{3,2,1,0:T(8,128)(2,1)S(1)}, bf16[2,2,192,128]{3,2,1,0:T(8,128)(2,1)S(1)}, u32[]{:S(2)}, u32[]{:S(2)}) collective-permute-start(bf16[2,2,192,128]{3,2,1,0:T(8,128)(2,1)S(1)} %get-tuple-element.98), channel_id=1, source_target_pairs={{0,2},{2,0},{4,6},{6,4},{8,10},{10,8},{12,14},{14,12},{16,18},{18,... | collective-permute-start | bytes 589832 | tf_op jit(solution)/shard_map/ppermute | solution.py:219
  43.0 17.0 %collective-permute-start.13 = (bf16[2,2,192,128]{3,2,1,0:T(8,128)(2,1)S(1)}, bf16[2,2,192,128]{3,2,1,0:T(8,128)(2,1)S(1)}, u32[]{:S(2)}, u32[]{:S(2)}) collective-permute-start(bf16[2,2,192,128]{3,2,1,0:T(8,128)(2,1)S(1)} %get-tuple-element.97), channel_id=1, source_target_pairs={{0,4},{2,6},{4,0},{6,2},{8,12},{10,14},{12,8},{14,10},{16,20},{18,... | collective-permute-start | bytes 589832 | tf_op jit(solution)/shard_map/ppermute | solution.py:219
  44.5 15.4 %collective-permute-start.12 = (bf16[2,2,192,128]{3,2,1,0:T(8,128)(2,1)S(1)}, bf16[2,2,192,128]{3,2,1,0:T(8,128)(2,1)S(1)}, u32[]{:S(2)}, u32[]{:S(2)}) collective-permute-start(bf16[2,2,192,128]{3,2,1,0:T(8,128)(2,1)S(1)} %get-tuple-element.96), channel_id=1, source_target_pairs={{0,6},{2,4},{4,2},{6,0},{8,14},{10,12},{12,10},{14,8},{16,22},{18,... | collective-permute-start | bytes 589832 | tf_op jit(solution)/shard_map/ppermute | solution.py:219
  51.6 10.8 %collective-permute-start.11 = (bf16[2,2,192,128]{3,2,1,0:T(8,128)(2,1)S(1)}, bf16[2,2,192,128]{3,2,1,0:T(8,128)(2,1)S(1)}, u32[]{:S(2)}, u32[]{:S(2)}) collective-permute-start(bf16[2,2,192,128]{3,2,1,0:T(8,128)(2,1)S(1)} %get-tuple-element.95), channel_id=1, source_target_pairs={{0,24},{2,26},{4,28},{6,30},{8,0},{10,2},{12,4},{14,6},{16,8},{18,... | collective-permute-start | bytes 589832 | tf_op jit(solution)/shard_map/ppermute | solution.py:219
  62.5 7.5 %collective-permute-start.15 = (bf16[2,2,192,128]{3,2,1,0:T(8,128)(2,1)S(1)}, bf16[2,2,192,128]{3,2,1,0:T(8,128)(2,1)S(1)}, u32[]{:S(2)}, u32[]{:S(2)}) collective-permute-start(bf16[2,2,192,128]{3,2,1,0:T(8,128)(2,1)S(1)} %shard_map.95), channel_id=1, source_target_pairs={{0,24},{2,26},{4,28},{6,30},{8,0},{10,2},{12,4},{14,6},{16,8},{18,... | collective-permute-start | bytes 589832 | tf_op jit(solution)/shard_map/ppermute | solution.py:219

commit v6 on v5

--- a/solution.py
+++ b/solution.py
@@ -12,6 +12,7 @@
 PLANE = 4
 FLIPS = (1, 2, 3)
 BACK = (2, 1, 0)
+DIAGONAL = 3
 LOG2E = math.log2(math.e)
 NEG_INIT = -1e30
 NEG_DEAD = -2e30
@@ -175,6 +176,19 @@
             out_ref[...] = up2_ref[...]
 
 
+def pick_kernel(place_ref, near_ref, far_ref, out_ref):
+    lane = lax.rem(place_ref[0], PLANE)
+    ahead = jnp.bitwise_xor(lane, DIAGONAL) > lane
+
+    @pl.when(ahead)
+    def _():
+        out_ref[...] = far_ref[...]
+
+    @pl.when(jnp.logical_not(ahead))
+    def _():
+        out_ref[...] = near_ref[...]
+
+
 def far_kernel(place_ref, *refs):
     mix_refs, (far_ref, mine_ref) = refs[:3], refs[3:]
     lane = lax.rem(place_ref[0], PLANE)
@@ -289,17 +303,22 @@
         return send(array, lambda i: i ^ flip)
 
     up = shift(own, PLANE)
+    near = swap(own, DIAGONAL)
     seen = stats([own_slot], [own])
     up, seen = lax.optimization_barrier((up, seen))
+    upx = [swap(up, f) for f in FLIPS]
     up2 = shift(up, PLANE)
-    upx = [swap(up, f) for f in FLIPS]
+    up3 = shift(upx[2], PLANE)
     seen = stats([up_slot], [up], seen)
-    outgoing = small(outgoing_kernel, [place, own, up2], [shaped(jnp.bfloat16)] * 3)
+    outgoing = small(outgoing_kernel, [place, own, up2], [shaped(jnp.bfloat16)] * 2)
     mix = [swap(x, f) for x, f in zip(outgoing, FLIPS)]
-    for k, f in enumerate(FLIPS):
+    for k in (2, 0, 1):
         seen = stats([upx_slots[k]], [upx[k]], seen)
-    for k, f in enumerate(FLIPS):
-        seen = stats([mix_slots[k]], [mix[k]], seen, last=k == 2)
+    for k in (0, 1):
+        seen = stats([mix_slots[k]], [mix[k]], seen)
+    up3, seen = lax.optimization_barrier((up3, seen))
+    mix += small(pick_kernel, [place, near, up3], [shaped(jnp.bfloat16)])
+    seen = stats([mix_slots[2]], [mix[2]], seen, last=True)
     m, _, d = seen
 
     dq, mixed, level = None, [], []

time: 71 us -> 70.3 us (level)
  waiting for transfers between devices: 24.7 us -> 20.1 us
  starting transfers between devices: 33.5 us -> 37.4 us
    ppermute x16 -> x17, waiting for transfers between devices: 24.7 us -> 20.1 us  [send(): return lax.ppermute(array, 'ctx', [(i, to(i)) for i in range(length)])]
    ppermute x16 -> x17, starting transfers between devices: 33.5 us -> 37.4 us  [send(): return lax.ppermute(array, 'ctx', [(i, to(i)) for i in range(length)])]
    pallas_call x5 -> x6, Pallas kernels: 2.17 us -> 2.17 us  [small(): pl.pallas_call(body, out_shape=shapes, in_specs=[SMEM if x is place else...]
  transfers between devices with their start and end apart: 16 -> 17, of which waited for: 9 -> 10; matrix products, arithmetic and copies ran while one was open for 3% -> 3% of each run, Pallas kernels for 9% -> 9%
where the time goes in v6:
time: 70.3 us; the launch traced here: 70.1 us
  starting transfers between devices  37.4 us (53%)
  waiting for transfers between devices  20.1 us (29%)
  Pallas kernels  9.29 us (13%)
  local copies, waits for them, and re-layouts  2.43 us (3%)
  between operations  0.87 us (1%)
    ppermute x17, starting transfers between devices, send(): return lax.ppermute(array, 'ctx', [(i, to(i)) for i in range(length)])  37.4 us
    ppermute x17, waiting for transfers between devices, send(): return lax.ppermute(array, 'ctx', [(i, to(i)) for i in range(length)])  20.1 us
    pallas_call x7, Pallas kernels, grads(): pl.pallas_call(functools.partial(grad_kernel, slots, heads_per, old is No...  4.02 us
    pallas_call x8, Pallas kernels, stats(): pl.pallas_call(functools.partial(stats_kernel, slots, heads_per, old is N...  2.52 us
    pallas_call x6, Pallas kernels, small(): pl.pallas_call(body, out_shape=shapes, in_specs=[SMEM if x is place else...  2.17 us
  transfers between devices with their start and end apart: 17, of which 10 were waited for; matrix products, arithmetic and copies ran while one was open for 3% of the time, Pallas kernels for 9%

profile of v6, /device:TPU:0, one launch (start us, length us, event | category | flops | bytes accessed | tf_op | source)
XLA Modules:
  0.0 70.1 jit_solution(11571925182058926826)
XLA Ops:
  0.6 1.1 %shard_map.77.refs_4_.own_ref.refs_6_ = bf16[2,2,192,128]{3,2,1,0:T(8,128)(2,1)S(1)} custom-call(bf16[384,128]{1,0:T(8,128)(2,1)} %bitcast.26, bf16[384,128]{1,0:T(8,128)(2,1)} %bitcast.27), custom_call_target="tpu_custom_call" | custom-call | tf_op jit(solution)/shard_map/pallas_call | solution.py:239
  1.7 3.1 %collective-permute-start.1 = (bf16[2,2,192,128]{3,2,1,0:T(8,128)(2,1)S(1)}, bf16[2,2,192,128]{3,2,1,0:T(8,128)(2,1)S(1)}, u32[]{:S(2)}, u32[]{:S(2)}) collective-permute-start(bf16[2,2,192,128]{3,2,1,0:T(8,128)(2,1)S(1)} %shard_map.77.refs_4_.own_ref.refs_6_), channel_id=1, source_target_pairs={{0,8},{2,10},{4,12},{6,14},{8,16},{10,18},{12,20},{14,22},{16,24},... | collective-permute-start | bytes 589832 | tf_op jit(solution)/shard_map/ppermute | solution.py:233
  4.8 1.4 %copy_bitcast_fusion.1 = (bf16[2,1536,128]{2,1,0:T(8,128)(2,1)S(1)}, bf16[2,1536,128]{2,1,0:T(8,128)(2,1)S(1)}) fusion(bf16[192,16,128]{2,1,0:T(8,128)(2,1)S(1)} %copy-done, bf16[192,16,128]{2,1,0:T(8,128)(2,1)} %param.8), kind=kLoop, calls=%fused_computation.1 | loop fusion | bytes 3145728 | tf_op jit(solution)/shard_map/reshape | solution.py:236
  6.3 0.6 shard_map.76.refs_1_
  6.8 1.1 %shard_map.78 = (f32[2,1,1536]{2,1,0:T(1,128)S(1)}, f32[2,1,1536]{2,1,0:T(1,128)S(1)}, f32[2,1,1536]{2,1,0:T(1,128)S(1)}) custom-call(s32[1]{0:T(128)} %bitcast.place_ref.refs_0_, s32[1,1536]{1,0:T(1,128)S(1)} %shard_map.76.refs_1_, bf16[2,1536,128]{2,1,0:T(8,128)(2,1)S(1)} %get-tuple-element.108.refs_2_, ...), custom_call_target="tpu_custom_call" | custom-call | flops 603979776 | bytes 1048576 | tf_op jit(solution)/shard_map/pallas_call | solution.py:274
  7.9 3.8 %collective-permute-done.1.refs_4_.refs_7_ = bf16[2,2,192,128]{3,2,1,0:T(8,128)(2,1)S(1)} collective-permute-done((bf16[2,2,192,128]{3,2,1,0:T(8,128)(2,1)S(1)}, bf16[2,2,192,128]{3,2,1,0:T(8,128)(2,1)S(1)}, u32[]{:S(2)}, u32[]{:S(2)}) %collective-permute-start.1) | collective-permute-done | bytes 196640 | tf_op jit(solution)/shard_map/ppermute | solution.py:233
  11.8 2.4 %collective-permute-start.2 = (bf16[2,2,192,128]{3,2,1,0:T(8,128)(2,1)S(1)}, bf16[2,2,192,128]{3,2,1,0:T(8,128)(2,1)S(1)}, u32[]{:S(2)}, u32[]{:S(2)}) collective-permute-start(bf16[2,2,192,128]{3,2,1,0:T(8,128)(2,1)S(1)} %collective-permute-done.1.refs_4_.refs_7_), channel_id=1, source_target_pairs={{0,6},{2,4},{4,2},{6,0},{8,14},{10,12},{12,10},{14,8},{16,22},{18,... | collective-permute-start | bytes 589832 | tf_op jit(solution)/shard_map/ppermute | solution.py:233
  14.2 0.5 collective-permute-start.8
  14.7 0.5 collective-permute-start.7
  15.2 2.4 %collective-permute-start = (bf16[2,2,192,128]{3,2,1,0:T(8,128)(2,1)S(1)}, bf16[2,2,192,128]{3,2,1,0:T(8,128)(2,1)S(1)}, u32[]{:S(2)}, u32[]{:S(2)}) collective-permute-start(bf16[2,2,192,128]{3,2,1,0:T(8,128)(2,1)S(1)} %shard_map.77.refs_4_.own_ref.refs_6_), channel_id=1, source_target_pairs={{0,6},{2,4},{4,2},{6,0},{8,14},{10,12},{12,10},{14,8},{16,22},{18,... | collective-permute-start | bytes 589832 | tf_op jit(solution)/shard_map/ppermute | solution.py:233
  17.7 1.9 %collective-permute-done.4.up2_ref = bf16[2,2,192,128]{3,2,1,0:T(8,128)(2,1)S(1)} collective-permute-done((bf16[2,2,192,128]{3,2,1,0:T(8,128)(2,1)S(1)}, bf16[2,2,192,128]{3,2,1,0:T(8,128)(2,1)S(1)}, u32[]{:S(2)}, u32[]{:S(2)}) %collective-permute-start.4) | collective-permute-done | bytes 196640 | tf_op jit(solution)/shard_map/ppermute | solution.py:233
  19.7 1.3 %collective-permute-start.6 = (bf16[2,2,192,128]{3,2,1,0:T(8,128)(2,1)S(1)}, bf16[2,2,192,128]{3,2,1,0:T(8,128)(2,1)S(1)}, u32[]{:S(2)}, u32[]{:S(2)}) collective-permute-start(bf16[2,2,192,128]{3,2,1,0:T(8,128)(2,1)S(1)} %get-tuple-element.60), channel_id=1, source_target_pairs={{0,2},{2,0},{4,6},{6,4},{8,10},{10,8},{12,14},{14,12},{16,18},{18,... | collective-permute-start | bytes 589832 | tf_op jit(solution)/shard_map/ppermute | solution.py:233
  21.0 0.2 shard_map.80
  21.2 1.6 %collective-permute-start.5 = (bf16[2,2,192,128]{3,2,1,0:T(8,128)(2,1)S(1)}, bf16[2,2,192,128]{3,2,1,0:T(8,128)(2,1)S(1)}, u32[]{:S(2)}, u32[]{:S(2)}) collective-permute-start(bf16[2,2,192,128]{3,2,1,0:T(8,128)(2,1)S(1)} %get-tuple-element.59), channel_id=1, source_target_pairs={{0,4},{2,6},{4,0},{6,2},{8,12},{10,14},{12,8},{14,10},{16,20},{18,... | collective-permute-start | bytes 589832 | tf_op jit(solution)/shard_map/ppermute | solution.py:233
  22.8 0.2 shard_map.81
  23.0 1.7 %collective-permute-done.8.refs_4_.refs_6_ = bf16[2,2,192,128]{3,2,1,0:T(8,128)(2,1)S(1)} collective-permute-done((bf16[2,2,192,128]{3,2,1,0:T(8,128)(2,1)S(1)}, bf16[2,2,192,128]{3,2,1,0:T(8,128)(2,1)S(1)}, u32[]{:S(2)}, u32[]{:S(2)}) %collective-permute-start.8) | collective-permute-done | bytes 196640 | tf_op jit(solution)/shard_map/ppermute | solution.py:233
  24.7 1.3 %collective-permute-start.3 = (bf16[2,2,192,128]{3,2,1,0:T(8,128)(2,1)S(1)}, bf16[2,2,192,128]{3,2,1,0:T(8,128)(2,1)S(1)}, u32[]{:S(2)}, u32[]{:S(2)}) collective-permute-start(bf16[2,2,192,128]{3,2,1,0:T(8,128)(2,1)S(1)} %collective-permute-done.2.refs_4_.refs_6_), channel_id=1, source_target_pairs={{0,8},{2,10},{4,12},{6,14},{8,16},{10,18},{12,20},{14,22},{16,24},... | collective-permute-start | bytes 589832 | tf_op jit(solution)/shard_map/ppermute | solution.py:233
  26.0 0.2 shard_map.82
  26.2 0.5 collective-permute-done.7.refs_4_.refs_6_
  26.7 0.2 shard_map.83
  26.9 4.3 %collective-permute-done.6.refs_4_.refs_6_ = bf16[2,2,192,128]{3,2,1,0:T(8,128)(2,1)S(1)} collective-permute-done((bf16[2,2,192,128]{3,2,1,0:T(8,128)(2,1)S(1)}, bf16[2,2,192,128]{3,2,1,0:T(8,128)(2,1)S(1)}, u32[]{:S(2)}, u32[]{:S(2)}) %collective-permute-start.6) | collective-permute-done | bytes 196640 | tf_op jit(solution)/shard_map/ppermute | solution.py:233
  31.2 0.2 shard_map.84
  31.4 0.2 shard_map.85
  31.6 0.5 collective-permute-done.3.far_ref
  32.2 0.2 shard_map.87
  32.4 0.2 shard_map.88
  32.7 0.4 shard_map.89
  33.1 0.2 shard_map.90
  33.3 3.9 %collective-permute-start.9 = (bf16[2,2,192,128]{3,2,1,0:T(8,128)(2,1)S(1)}, bf16[2,2,192,128]{3,2,1,0:T(8,128)(2,1)S(1)}, u32[]{:S(2)}, u32[]{:S(2)}) collective-permute-start(bf16[2,2,192,128]{3,2,1,0:T(8,128)(2,1)S(1)} %get-tuple-element.95), channel_id=1, source_target_pairs={{0,2},{2,0},{4,6},{6,4},{8,10},{10,8},{12,14},{14,12},{16,18},{18,... | collective-permute-start | bytes 589832 | tf_op jit(solution)/shard_map/ppermute | solution.py:233
  37.3 2.6 %collective-permute-start.10 = (bf16[2,2,192,128]{3,2,1,0:T(8,128)(2,1)S(1)}, bf16[2,2,192,128]{3,2,1,0:T(8,128)(2,1)S(1)}, u32[]{:S(2)}, u32[]{:S(2)}) collective-permute-start(bf16[2,2,192,128]{3,2,1,0:T(8,128)(2,1)S(1)} %get-tuple-element.96), channel_id=1, source_target_pairs={{0,4},{2,6},{4,0},{6,2},{8,12},{10,14},{12,8},{14,10},{16,20},{18,... | collective-permute-start | bytes 589832 | tf_op jit(solution)/shard_map/ppermute | solution.py:233
  39.9 1.4 %collective-permute-start.11 = (bf16[2,2,192,128]{3,2,1,0:T(8,128)(2,1)S(1)}, bf16[2,2,192,128]{3,2,1,0:T(8,128)(2,1)S(1)}, u32[]{:S(2)}, u32[]{:S(2)}) collective-permute-start(bf16[2,2,192,128]{3,2,1,0:T(8,128)(2,1)S(1)} %get-tuple-element.97), channel_id=1, source_target_pairs={{0,6},{2,4},{4,2},{6,0},{8,14},{10,12},{12,10},{14,8},{16,22},{18,... | collective-permute-start | bytes 589832 | tf_op jit(solution)/shard_map/ppermute | solution.py:233
  41.3 0.2 shard_map.91
  41.5 0.2 shard_map.92
  41.8 0.2 shard_map.93
  42.0 0.6 collective-permute-start.15
  42.7 1.5 %collective-permute-start.14 = (bf16[2,2,192,128]{3,2,1,0:T(8,128)(2,1)S(1)}, bf16[2,2,192,128]{3,2,1,0:T(8,128)(2,1)S(1)}, u32[]{:S(2)}, u32[]{:S(2)}) collective-permute-start(bf16[2,2,192,128]{3,2,1,0:T(8,128)(2,1)S(1)} %get-tuple-element.103), channel_id=1, source_target_pairs={{0,4},{2,6},{4,0},{6,2},{8,12},{10,14},{12,8},{14,10},{16,20},{18,... | collective-permute-start | bytes 589832 | tf_op jit(solution)/shard_map/ppermute | solution.py:233
  44.2 2.9 %collective-permute-start.13 = (bf16[2,2,192,128]{3,2,1,0:T(8,128)(2,1)S(1)}, bf16[2,2,192,128]{3,2,1,0:T(8,128)(2,1)S(1)}, u32[]{:S(2)}, u32[]{:S(2)}) collective-permute-start(bf16[2,2,192,128]{3,2,1,0:T(8,128)(2,1)S(1)} %get-tuple-element.102), channel_id=1, source_target_pairs={{0,6},{2,4},{4,2},{6,0},{8,14},{10,12},{12,10},{14,8},{16,22},{18,... | collective-permute-start | bytes 589832 | tf_op jit(solution)/shard_map/ppermute | solution.py:233
  47.1 3.4 %collective-permute-done.10.refs_1_ = bf16[2,2,192,128]{3,2,1,0:T(8,128)(2,1)S(1)} collective-permute-done((bf16[2,2,192,128]{3,2,1,0:T(8,128)(2,1)S(1)}, bf16[2,2,192,128]{3,2,1,0:T(8,128)(2,1)S(1)}, u32[]{:S(2)}, u32[]{:S(2)}) %collective-permute-start.10) | collective-permute-done | bytes 196640 | tf_op jit(solution)/shard_map/ppermute | solution.py:233
  50.4 0.9 %collective-permute-done.11.refs_2_ = bf16[2,2,192,128]{3,2,1,0:T(8,128)(2,1)S(1)} collective-permute-done((bf16[2,2,192,128]{3,2,1,0:T(8,128)(2,1)S(1)}, bf16[2,2,192,128]{3,2,1,0:T(8,128)(2,1)S(1)}, u32[]{:S(2)}, u32[]{:S(2)}) %collective-permute-start.11) | collective-permute-done | bytes 196640 | tf_op jit(solution)/shard_map/ppermute | solution.py:233
  51.3 0.2 shard_map.95
  51.5 6.8 %collective-permute-start.12 = (bf16[2,2,192,128]{3,2,1,0:T(8,128)(2,1)S(1)}, bf16[2,2,192,128]{3,2,1,0:T(8,128)(2,1)S(1)}, u32[]{:S(2)}, u32[]{:S(2)}) collective-permute-start(bf16[2,2,192,128]{3,2,1,0:T(8,128)(2,1)S(1)} %get-tuple-element.101), channel_id=1, source_target_pairs={{0,24},{2,26},{4,28},{6,30},{8,0},{10,2},{12,4},{14,6},{16,8},{18,... | collective-permute-start | bytes 589832 | tf_op jit(solution)/shard_map/ppermute | solution.py:233
  58.3 2.5 %shard_map.94 = (bf16[2,2,192,128]{3,2,1,0:T(8,128)(2,1)S(1)}, bf16[2,2,192,128]{3,2,1,0:T(8,128)(2,1)S(1)}, bf16[2,1536,128]{2,1,0:T(8,128)(2,1)S(1)}, f32[2,128,1536]{2,1,0:T(8,128)S(1)}) custom-call(s32[1]{0:T(128)} %bitcast.place_ref.refs_0_, s32[1,1536]{1,0:T(1,128)S(1)} %shard_map.76.refs_1_, ...), custom_call_target="tpu_custom_call", output_to_operand_aliasing={{3}: (8, {})} | custom-call | flops 3019898880 | bytes 1048576 | tf_op jit(solution)/shard_map/pallas_call | solution.py:286
  60.8 0.9 %collective-permute-done.12.refs_1_ = bf16[2,2,192,128]{3,2,1,0:T(8,128)(2,1)S(1)} collective-permute-done((bf16[2,2,192,128]{3,2,1,0:T(8,128)(2,1)S(1)}, bf16[2,2,192,128]{3,2,1,0:T(8,128)(2,1)S(1)}, u32[]{:S(2)}, u32[]{:S(2)}) %collective-permute-start.12) | collective-permute-done | bytes 196640 | tf_op jit(solution)/shard_map/ppermute | solution.py:233
  61.7 0.1 shard_map.96
  61.9 4.3 %collective-permute-start.16 = (bf16[2,2,192,128]{3,2,1,0:T(8,128)(2,1)S(1)}, bf16[2,2,192,128]{3,2,1,0:T(8,128)(2,1)S(1)}, u32[]{:S(2)}, u32[]{:S(2)}) collective-permute-start(bf16[2,2,192,128]{3,2,1,0:T(8,128)(2,1)S(1)} %shard_map.96), channel_id=1, source_target_pairs={{0,24},{2,26},{4,28},{6,30},{8,0},{10,2},{12,4},{14,6},{16,8},{18,... | collective-permute-start | bytes 589832 | tf_op jit(solution)/shard_map/ppermute | solution.py:233
  66.2 1.0 %copy_bitcast_fusion = bf16[192,16,128]{2,1,0:T(8,128)(2,1)} fusion(bf16[2,1536,128]{2,1,0:T(8,128)(2,1)S(1)} %get-tuple-element.94), kind=kLoop, calls=%fused_computation | loop fusion | bytes 1572864 | tf_op jit(solution)/shard_map/reshape | solution.py:339
  67.2 2.2 %collective-permute-done.16.down_ref = bf16[2,2,192,128]{3,2,1,0:T(8,128)(2,1)S(1)} collective-permute-done((bf16[2,2,192,128]{3,2,1,0:T(8,128)(2,1)S(1)}, bf16[2,2,192,128]{3,2,1,0:T(8,128)(2,1)S(1)}, u32[]{:S(2)}, u32[]{:S(2)}) %collective-permute-start.16) | collective-permute-done | bytes 196640 | tf_op jit(solution)/shard_map/ppermute | solution.py:233
  69.4 0.7 %shard_map.97 = (bf16[384,128]{1,0:T(8,128)(2,1)}, bf16[384,128]{1,0:T(8,128)(2,1)}) custom-call(f32[2,2,192,128]{3,2,1,0:T(8,128)S(1)} %get-tuple-element.98.mine_ref, bf16[2,2,192,128]{3,2,1,0:T(8,128)(2,1)S(1)} %get-tuple-element.99.own_ref, bf16[2,2,192,128]{3,2,1,0:T(8,128)(2,1)S(1)} %collective-permute-done.16.down_ref), custom_call_target="tpu_custom_call" | custom-call | tf_op jit(solution)/shard_map/pallas_call | solution.py:239
  (14 shorter events, 0.1 us)
Async XLA Ops:
  0.6 4.2 %copy-start = (bf16[192,16,128]{2,1,0:T(8,128)(2,1)S(1)}, bf16[192,16,128]{2,1,0:T(8,128)(2,1)}, u32[]{:S(2)}) copy-start(bf16[192,16,128]{2,1,0:T(8,128)(2,1)} %param.5) | copy-start | bytes 2359300
  1.7 4.5 %copy-start.1 = (s32[8]{0:T(128)S(1)}, s32[8]{0:T(128)}, u32[]{:S(2)}) copy-start(s32[8]{0:T(128)} %lens_ref.1) | copy-start | bytes 100
  1.7 10.0 %collective-permute-start.1 = (bf16[2,2,192,128]{3,2,1,0:T(8,128)(2,1)S(1)}, bf16[2,2,192,128]{3,2,1,0:T(8,128)(2,1)S(1)}, u32[]{:S(2)}, u32[]{:S(2)}) collective-permute-start(bf16[2,2,192,128]{3,2,1,0:T(8,128)(2,1)S(1)} %shard_map.77.refs_4_.own_ref.refs_6_), channel_id=1, source_target_pairs={{0,8},{2,10},{4,12},{6,14},{8,16},{10,18},{12,20},{14,22},{16,24},... | collective-permute-start | bytes 589832 | tf_op jit(solution)/shard_map/ppermute | solution.py:233
  11.8 7.9 %collective-permute-start.4 = (bf16[2,2,192,128]{3,2,1,0:T(8,128)(2,1)S(1)}, bf16[2,2,192,128]{3,2,1,0:T(8,128)(2,1)S(1)}, u32[]{:S(2)}, u32[]{:S(2)}) collective-permute-start(bf16[2,2,192,128]{3,2,1,0:T(8,128)(2,1)S(1)} %collective-permute-done.1.refs_4_.refs_7_), channel_id=1, source_target_pairs={{0,8},{2,10},{4,12},{6,14},{8,16},{10,18},{12,20},{14,22},{16,24},... | collective-permute-start | bytes 589832 | tf_op jit(solution)/shard_map/ppermute | solution.py:233
  11.8 9.4 %collective-permute-start.2 = (bf16[2,2,192,128]{3,2,1,0:T(8,128)(2,1)S(1)}, bf16[2,2,192,128]{3,2,1,0:T(8,128)(2,1)S(1)}, u32[]{:S(2)}, u32[]{:S(2)}) collective-permute-start(bf16[2,2,192,128]{3,2,1,0:T(8,128)(2,1)S(1)} %collective-permute-done.1.refs_4_.refs_7_), channel_id=1, source_target_pairs={{0,6},{2,4},{4,2},{6,0},{8,14},{10,12},{12,10},{14,8},{16,22},{18,... | collective-permute-start | bytes 589832 | tf_op jit(solution)/shard_map/ppermute | solution.py:233
  14.2 10.5 %collective-permute-start.8 = (bf16[2,2,192,128]{3,2,1,0:T(8,128)(2,1)S(1)}, bf16[2,2,192,128]{3,2,1,0:T(8,128)(2,1)S(1)}, u32[]{:S(2)}, u32[]{:S(2)}) collective-permute-start(bf16[2,2,192,128]{3,2,1,0:T(8,128)(2,1)S(1)} %collective-permute-done.1.refs_4_.refs_7_), channel_id=1, source_target_pairs={{0,2},{2,0},{4,6},{6,4},{8,10},{10,8},{12,14},{14,12},{16,18},{18,... | collective-permute-start | bytes 589832 | tf_op jit(solution)/shard_map/ppermute | solution.py:233
  14.7 12.0 %collective-permute-start.7 = (bf16[2,2,192,128]{3,2,1,0:T(8,128)(2,1)S(1)}, bf16[2,2,192,128]{3,2,1,0:T(8,128)(2,1)S(1)}, u32[]{:S(2)}, u32[]{:S(2)}) collective-permute-start(bf16[2,2,192,128]{3,2,1,0:T(8,128)(2,1)S(1)} %collective-permute-done.1.refs_4_.refs_7_), channel_id=1, source_target_pairs={{0,4},{2,6},{4,0},{6,2},{8,12},{10,14},{12,8},{14,10},{16,20},{18,... | collective-permute-start | bytes 589832 | tf_op jit(solution)/shard_map/ppermute | solution.py:233
  15.2 16.9 %collective-permute-start = (bf16[2,2,192,128]{3,2,1,0:T(8,128)(2,1)S(1)}, bf16[2,2,192,128]{3,2,1,0:T(8,128)(2,1)S(1)}, u32[]{:S(2)}, u32[]{:S(2)}) collective-permute-start(bf16[2,2,192,128]{3,2,1,0:T(8,128)(2,1)S(1)} %shard_map.77.refs_4_.own_ref.refs_6_), channel_id=1, source_target_pairs={{0,6},{2,4},{4,2},{6,0},{8,14},{10,12},{12,10},{14,8},{16,22},{18,... | collective-permute-start | bytes 589832 | tf_op jit(solution)/shard_map/ppermute | solution.py:233
  19.7 11.5 %collective-permute-start.6 = (bf16[2,2,192,128]{3,2,1,0:T(8,128)(2,1)S(1)}, bf16[2,2,192,128]{3,2,1,0:T(8,128)(2,1)S(1)}, u32[]{:S(2)}, u32[]{:S(2)}) collective-permute-start(bf16[2,2,192,128]{3,2,1,0:T(8,128)(2,1)S(1)} %get-tuple-element.60), channel_id=1, source_target_pairs={{0,2},{2,0},{4,6},{6,4},{8,10},{10,8},{12,14},{14,12},{16,18},{18,... | collective-permute-start | bytes 589832 | tf_op jit(solution)/shard_map/ppermute | solution.py:233
  21.2 10.2 %collective-permute-start.5 = (bf16[2,2,192,128]{3,2,1,0:T(8,128)(2,1)S(1)}, bf16[2,2,192,128]{3,2,1,0:T(8,128)(2,1)S(1)}, u32[]{:S(2)}, u32[]{:S(2)}) collective-permute-start(bf16[2,2,192,128]{3,2,1,0:T(8,128)(2,1)S(1)} %get-tuple-element.59), channel_id=1, source_target_pairs={{0,4},{2,6},{4,0},{6,2},{8,12},{10,14},{12,8},{14,10},{16,20},{18,... | collective-permute-start | bytes 589832 | tf_op jit(solution)/shard_map/ppermute | solution.py:233
  24.7 7.5 %collective-permute-start.3 = (bf16[2,2,192,128]{3,2,1,0:T(8,128)(2,1)S(1)}, bf16[2,2,192,128]{3,2,1,0:T(8,128)(2,1)S(1)}, u32[]{:S(2)}, u32[]{:S(2)}) collective-permute-start(bf16[2,2,192,128]{3,2,1,0:T(8,128)(2,1)S(1)} %collective-permute-done.2.refs_4_.refs_6_), channel_id=1, source_target_pairs={{0,8},{2,10},{4,12},{6,14},{8,16},{10,18},{12,20},{14,22},{16,24},... | collective-permute-start | bytes 589832 | tf_op jit(solution)/shard_map/ppermute | solution.py:233
  33.3 10.9 %collective-permute-start.9 = (bf16[2,2,192,128]{3,2,1,0:T(8,128)(2,1)S(1)}, bf16[2,2,192,128]{3,2,1,0:T(8,128)(2,1)S(1)}, u32[]{:S(2)}, u32[]{:S(2)}) collective-permute-start(bf16[2,2,192,128]{3,2,1,0:T(8,128)(2,1)S(1)} %get-tuple-element.95), channel_id=1, source_target_pairs={{0,2},{2,0},{4,6},{6,4},{8,10},{10,8},{12,14},{14,12},{16,18},{18,... | collective-permute-start | bytes 589832 | tf_op jit(solution)/shard_map/ppermute | solution.py:233
  37.3 13.1 %collective-permute-start.10 = (bf16[2,2,192,128]{3,2,1,0:T(8,128)(2,1)S(1)}, bf16[2,2,192,128]{3,2,1,0:T(8,128)(2,1)S(1)}, u32[]{:S(2)}, u32[]{:S(2)}) collective-permute-start(bf16[2,2,192,128]{3,2,1,0:T(8,128)(2,1)S(1)} %get-tuple-element.96), channel_id=1, source_target_pairs={{0,4},{2,6},{4,0},{6,2},{8,12},{10,14},{12,8},{14,10},{16,20},{18,... | collective-permute-start | bytes 589832 | tf_op jit(solution)/shard_map/ppermute | solution.py:233
  39.9 11.4 %collective-permute-start.11 = (bf16[2,2,192,128]{3,2,1,0:T(8,128)(2,1)S(1)}, bf16[2,2,192,128]{3,2,1,0:T(8,128)(2,1)S(1)}, u32[]{:S(2)}, u32[]{:S(2)}) collective-permute-start(bf16[2,2,192,128]{3,2,1,0:T(8,128)(2,1)S(1)} %get-tuple-element.97), channel_id=1, source_target_pairs={{0,6},{2,4},{4,2},{6,0},{8,14},{10,12},{12,10},{14,8},{16,22},{18,... | collective-permute-start | bytes 589832 | tf_op jit(solution)/shard_map/ppermute | solution.py:233
  42.0 18.8 %collective-permute-start.15 = (bf16[2,2,192,128]{3,2,1,0:T(8,128)(2,1)S(1)}, bf16[2,2,192,128]{3,2,1,0:T(8,128)(2,1)S(1)}, u32[]{:S(2)}, u32[]{:S(2)}) collective-permute-start(bf16[2,2,192,128]{3,2,1,0:T(8,128)(2,1)S(1)} %get-tuple-element.104), channel_id=1, source_target_pairs={{0,2},{2,0},{4,6},{6,4},{8,10},{10,8},{12,14},{14,12},{16,18},{18,... | collective-permute-start | bytes 589832 | tf_op jit(solution)/shard_map/ppermute | solution.py:233
  42.7 18.2 %collective-permute-start.14 = (bf16[2,2,192,128]{3,2,1,0:T(8,128)(2,1)S(1)}, bf16[2,2,192,128]{3,2,1,0:T(8,128)(2,1)S(1)}, u32[]{:S(2)}, u32[]{:S(2)}) collective-permute-start(bf16[2,2,192,128]{3,2,1,0:T(8,128)(2,1)S(1)} %get-tuple-element.103), channel_id=1, source_target_pairs={{0,4},{2,6},{4,0},{6,2},{8,12},{10,14},{12,8},{14,10},{16,20},{18,... | collective-permute-start | bytes 589832 | tf_op jit(solution)/shard_map/ppermute | solution.py:233
  44.2 16.6 %collective-permute-start.13 = (bf16[2,2,192,128]{3,2,1,0:T(8,128)(2,1)S(1)}, bf16[2,2,192,128]{3,2,1,0:T(8,128)(2,1)S(1)}, u32[]{:S(2)}, u32[]{:S(2)}) collective-permute-start(bf16[2,2,192,128]{3,2,1,0:T(8,128)(2,1)S(1)} %get-tuple-element.102), channel_id=1, source_target_pairs={{0,6},{2,4},{4,2},{6,0},{8,14},{10,12},{12,10},{14,8},{16,22},{18,... | collective-permute-start | bytes 589832 | tf_op jit(solution)/shard_map/ppermute | solution.py:233
  51.5 10.2 %collective-permute-start.12 = (bf16[2,2,192,128]{3,2,1,0:T(8,128)(2,1)S(1)}, bf16[2,2,192,128]{3,2,1,0:T(8,128)(2,1)S(1)}, u32[]{:S(2)}, u32[]{:S(2)}) collective-permute-start(bf16[2,2,192,128]{3,2,1,0:T(8,128)(2,1)S(1)} %get-tuple-element.101), channel_id=1, source_target_pairs={{0,24},{2,26},{4,28},{6,30},{8,0},{10,2},{12,4},{14,6},{16,8},{18,... | collective-permute-start | bytes 589832 | tf_op jit(solution)/shard_map/ppermute | solution.py:233
  61.9 7.5 %collective-permute-start.16 = (bf16[2,2,192,128]{3,2,1,0:T(8,128)(2,1)S(1)}, bf16[2,2,192,128]{3,2,1,0:T(8,128)(2,1)S(1)}, u32[]{:S(2)}, u32[]{:S(2)}) collective-permute-start(bf16[2,2,192,128]{3,2,1,0:T(8,128)(2,1)S(1)} %shard_map.96), channel_id=1, source_target_pairs={{0,24},{2,26},{4,28},{6,30},{8,0},{10,2},{12,4},{14,6},{16,8},{18,... | collective-permute-start | bytes 589832 | tf_op jit(solution)/shard_map/ppermute | solution.py:233

commit v7 on v6

--- a/solution.py
+++ b/solution.py
@@ -79,7 +79,8 @@
     refs = refs[4 + n :]
     if not first:
         refs = refs[3:]
-    m_ref, l_ref, d_ref = refs
+    m_ref, l_ref, d_ref = refs[:3]
+    e_refs, top_refs = refs[3 : 3 + n], refs[3 + n :]
     groups, _, dim = q_ref.shape
     stripe = kv_refs[0].shape[-2]
     scale2 = dim**-0.5 * LOG2E
@@ -88,7 +89,7 @@
         m_ref[...] = jnp.full_like(m_ref, NEG_INIT)
         l_ref[...] = jnp.zeros_like(l_ref)
         d_ref[...] = jnp.zeros_like(d_ref)
-    for kv_ref, slot in zip(kv_refs, slots):
+    for kv_ref, e_ref, top_ref, slot in zip(kv_refs, e_refs, top_refs, slots):
         at = slot(me, lane)
 
         @pl.when((at >= 0) & ((at + 1) * stripe > first_key))
@@ -99,6 +100,8 @@
                 m_old = m_ref[g]
                 m_new = jnp.maximum(m_old, jnp.max(s, axis=0, keepdims=True))
                 e = jnp.exp2(s - m_new)
+                e_ref[g] = e.astype(jnp.bfloat16)
+                top_ref[g] = m_new
                 fade = jnp.exp2(m_old - m_new)
                 m_ref[g] = m_new
                 l_ref[g] = l_ref[g] * fade + jnp.sum(e, axis=0, keepdims=True)
@@ -109,11 +112,11 @@
         m_ref[...] = m_ref[...] + jnp.log2(l_ref[...])
 
 
-def grad_kernel(slots, heads_per, first, last, *refs):
+def grad_kernel(slots, first, last, *refs):
     n = len(slots)
     place_ref, start_ref, q_ref, do_ref, m_ref, d_ref = refs[:6]
-    kv_refs = refs[6 : 6 + n]
-    refs = refs[6 + n :]
+    kv_refs, e_refs, top_refs = refs[6 : 6 + n], refs[6 + n : 6 + 2 * n], refs[6 + 2 * n : 6 + 3 * n]
+    refs = refs[6 + 3 * n :]
     if not first:
         refs = refs[1:]
     part_refs = refs[:n]
@@ -121,11 +124,10 @@
     groups, _, dim = q_ref.shape
     stripe = kv_refs[0].shape[-2]
     scale = dim**-0.5
-    scale2 = scale * LOG2E
     me, lane, first_key = first_live(place_ref, start_ref)
     if first:
         dqt[...] = jnp.zeros_like(dqt)
-    for kv_ref, part_ref, slot in zip(kv_refs, part_refs, slots):
+    for kv_ref, part_ref, e_ref, top_ref, slot in zip(kv_refs, part_refs, e_refs, top_refs, slots):
         at = slot(me, lane)
         live = (at >= 0) & ((at + 1) * stripe > first_key)
 
@@ -133,9 +135,8 @@
         def _():
             for g in range(groups):
                 keys, vals, q_g, do_g = kv_ref[0, g], kv_ref[1, g], q_ref[g], do_ref[g]
-                s = logits(keys, q_g, at * stripe, start_ref, heads_per, slot is own_slot, scale2)
                 gp = mm(vals, do_g, NT)
-                p = jnp.exp2(s - m_ref[g])
+                p = e_ref[g].astype(jnp.float32) * jnp.exp2(top_ref[g] - m_ref[g])
                 ds = (p * (gp - d_ref[g])).astype(jnp.bfloat16)
                 part_ref[1, g] = mm(p.astype(jnp.bfloat16), do_g, NN).astype(jnp.bfloat16)
                 part_ref[0, g] = (mm(ds, q_g, NN) * scale).astype(jnp.bfloat16)
@@ -253,6 +254,8 @@
     (own,) = small(pack_kernel, [pltpu.with_memory_space_constraint(x.reshape(flat), pltpu.HBM) for x in (key_vectors, value_matrix)], [shaped(jnp.bfloat16)], [wide, pltpu.VMEM((2,) + flat, jnp.bfloat16), pltpu.SemaphoreType.DMA((2,))], pl.BlockSpec(memory_space=pltpu.HBM))
     q, do = columns(queries), columns(grad_out)
     stat = jax.ShapeDtypeStruct((groups, 1, cols), jnp.float32)
+    weight = jax.ShapeDtypeStruct((groups, stripe, cols), jnp.bfloat16)
+    kept = {}
     total = jax.ShapeDtypeStruct((groups, dim, cols), jnp.float32)
     n_docs = doc_lengths.shape[0]
     pair_flops = groups * stripe * cols * dim * 2
@@ -270,27 +273,31 @@
             cost_estimate=pl.CostEstimate(flops=products * n * pair_flops * 2, bytes_accessed=1 << 20, transcendentals=0),
         )
 
-    def stats(slots, kvs, old=None, last=False):
-        return pl.pallas_call(
+    def stats(name, slots, kvs, old=None, last=False):
+        outs = pl.pallas_call(
             functools.partial(stats_kernel, slots, heads_per, old is None, last),
-            out_shape=[stat] * 3,
+            out_shape=[stat] * 3 + [weight] * len(kvs) + [stat] * len(kvs),
             in_specs=[SMEM] + [VMEM] * (3 + len(kvs) + (0 if old is None else 3)),
-            out_specs=[VMEM] * 3,
+            out_specs=[VMEM] * (3 + 2 * len(kvs)),
             input_output_aliases={} if old is None else {4 + len(kvs) + i: i for i in range(3)},
             **params(2, len(kvs)),
         )(place, start, q, do, *kvs, *(old or ()))
-
-    def grads(slots, kvs, old=None, last=False):
+        kept[name] = outs[3:]
+        return outs[:3]
+
+    def grads(name, slots, kvs, old=None, last=False):
         n = len(kvs)
+        es = [kept[x][0] for x in name.split()]
+        tops = [kept[x][1] for x in name.split()]
         dq_shape = [jax.ShapeDtypeStruct(q.shape, jnp.bfloat16), total] if last else [total]
         outs = pl.pallas_call(
-            functools.partial(grad_kernel, slots, heads_per, old is None, last),
+            functools.partial(grad_kernel, slots, old is None, last),
             out_shape=[shaped(jnp.bfloat16)] * n + dq_shape,
-            in_specs=[SMEM] + [VMEM] * (5 + n + (0 if old is None else 1)),
+            in_specs=[SMEM] + [VMEM] * (5 + 3 * n + (0 if old is None else 1)),
             out_specs=[VMEM] * (n + len(dq_shape)),
-            input_output_aliases={} if old is None else {6 + n: n + len(dq_shape) - 1},
+            input_output_aliases={} if old is None else {6 + 3 * n: n + len(dq_shape) - 1},
             **params(5, n),
-        )(place, start, q, do, m, d, *kvs, *(() if old is None else (old,)))
+        )(place, start, q, do, m, d, *kvs, *es, *tops, *(() if old is None else (old,)))
         return outs[:n], outs[n]
 
     upx_slots = [functools.partial(upx_slot, f) for f in FLIPS]
@@ -304,31 +311,31 @@
 
     up = shift(own, PLANE)
     near = swap(own, DIAGONAL)
-    seen = stats([own_slot], [own])
+    seen = stats("own", [own_slot], [own])
     up, seen = lax.optimization_barrier((up, seen))
     upx = [swap(up, f) for f in FLIPS]
     up2 = shift(up, PLANE)
     up3 = shift(upx[2], PLANE)
-    seen = stats([up_slot], [up], seen)
+    seen = stats("up", [up_slot], [up], seen)
     outgoing = small(outgoing_kernel, [place, own, up2], [shaped(jnp.bfloat16)] * 2)
     mix = [swap(x, f) for x, f in zip(outgoing, FLIPS)]
     for k in (2, 0, 1):
-        seen = stats([upx_slots[k]], [upx[k]], seen)
+        seen = stats(f"upx{FLIPS[k]}", [upx_slots[k]], [upx[k]], seen)
     for k in (0, 1):
-        seen = stats([mix_slots[k]], [mix[k]], seen)
+        seen = stats(f"mix{FLIPS[k]}", [mix_slots[k]], [mix[k]], seen)
     up3, seen = lax.optimization_barrier((up3, seen))
     mix += small(pick_kernel, [place, near, up3], [shaped(jnp.bfloat16)])
-    seen = stats([mix_slots[2]], [mix[2]], seen, last=True)
+    seen = stats("mix3", [mix_slots[2]], [mix[2]], seen, last=True)
     m, _, d = seen
 
     dq, mixed, level = None, [], []
     for k, f in zip(BACK, FLIPS[::-1]):
-        (part,), dq = grads([mix_slots[k]], [mix[k]], dq)
+        (part,), dq = grads(f"mix{f}", [mix_slots[k]], [mix[k]], dq)
         mixed.append(swap(part, f))
     for k, f in zip(BACK, FLIPS[::-1]):
-        (part,), dq = grads([upx_slots[k]], [upx[k]], dq)
+        (part,), dq = grads(f"upx{f}", [upx_slots[k]], [upx[k]], dq)
         level.append(swap(part, f))
-    (own_part, up_part), dq = grads([own_slot, up_slot], [own, up], dq, last=True)
+    (own_part, up_part), dq = grads("own up", [own_slot, up_slot], [own, up], dq, last=True)
 
     far, mine = small(far_kernel, [place, *mixed[::-1]], [shaped(jnp.bfloat16), shaped(jnp.float32)])
     down2 = shift(far, -PLANE)

time: 70.3 us -> 68 us (0.967)
  starting transfers between devices: 37.4 us -> 35.3 us
    ppermute x17, starting transfers between devices: 37.4 us -> 35.3 us  [send(): return lax.ppermute(array, 'ctx', [(i, to(i)) for i in range(length)])]
  transfers between devices with their start and end apart: 17 -> 17, of which waited for: 10 -> 10; matrix products, arithmetic and copies ran while one was open for 3% -> 4% of each run, Pallas kernels for 9% -> 9%
where the time goes in v7:
time: 68 us; the launch traced here: 67.8 us
  starting transfers between devices  35.3 us (52%)
  waiting for transfers between devices  20.4 us (30%)
  Pallas kernels  8.82 us (13%)
  local copies, waits for them, and re-layouts  2.43 us (4%)
  between operations  0.87 us (1%)
    ppermute x17, starting transfers between devices, send(): return lax.ppermute(array, 'ctx', [(i, to(i)) for i in range(length)])  35.3 us
    ppermute x17, waiting for transfers between devices, send(): return lax.ppermute(array, 'ctx', [(i, to(i)) for i in range(length)])  20.4 us
    pallas_call x7, Pallas kernels, grads(): pl.pallas_call(functools.partial(grad_kernel, slots, old is None, last),...  3.49 us
    pallas_call x8, Pallas kernels, stats(): pl.pallas_call(functools.partial(stats_kernel, slots, heads_per, old is N...  2.58 us
    pallas_call x6, Pallas kernels, small(): pl.pallas_call(body, out_shape=shapes, in_specs=[SMEM if x is place else...  2.17 us
    reshape x1, local copies, waits for them, and re-layouts, columns(): array.reshape(stripe, groups, heads_per, dim).transpose(1, 0, 2, 3)  1.4 us
  transfers between devices with their start and end apart: 17, of which 10 were waited for; matrix products, arithmetic and copies ran while one was open for 4% of the time, Pallas kernels for 9%

profile of v7, /device:TPU:0, one launch (start us, length us, event | category | flops | bytes accessed | tf_op | source)
XLA Modules:
  0.0 67.8 jit_solution(15570017129193576244)
XLA Ops:
  0.6 1.1 %shard_map.77.refs_4_.own_ref.refs_6_ = bf16[2,2,192,128]{3,2,1,0:T(8,128)(2,1)S(1)} custom-call(bf16[384,128]{1,0:T(8,128)(2,1)} %bitcast.26, bf16[384,128]{1,0:T(8,128)(2,1)} %bitcast.27), custom_call_target="tpu_custom_call" | custom-call | tf_op jit(solution)/shard_map/pallas_call | solution.py:240
  1.7 3.1 %collective-permute-start.1 = (bf16[2,2,192,128]{3,2,1,0:T(8,128)(2,1)S(1)}, bf16[2,2,192,128]{3,2,1,0:T(8,128)(2,1)S(1)}, u32[]{:S(2)}, u32[]{:S(2)}) collective-permute-start(bf16[2,2,192,128]{3,2,1,0:T(8,128)(2,1)S(1)} %shard_map.77.refs_4_.own_ref.refs_6_), channel_id=1, source_target_pairs={{0,8},{2,10},{4,12},{6,14},{8,16},{10,18},{12,20},{14,22},{16,24},... | collective-permute-start | bytes 589832 | tf_op jit(solution)/shard_map/ppermute | solution.py:234
  4.8 1.4 %copy_bitcast_fusion.1 = (bf16[2,1536,128]{2,1,0:T(8,128)(2,1)S(1)}, bf16[2,1536,128]{2,1,0:T(8,128)(2,1)S(1)}) fusion(bf16[192,16,128]{2,1,0:T(8,128)(2,1)S(1)} %copy-done, bf16[192,16,128]{2,1,0:T(8,128)(2,1)} %param.8), kind=kLoop, calls=%fused_computation.1 | loop fusion | bytes 3145728 | tf_op jit(solution)/shard_map/reshape | solution.py:237
  6.3 0.6 shard_map.76.refs_1_
  6.8 1.1 %shard_map.78 = (f32[2,1,1536]{2,1,0:T(1,128)S(1)}, f32[2,1,1536]{2,1,0:T(1,128)S(1)}, f32[2,1,1536]{2,1,0:T(1,128)S(1)}, bf16[2,192,1536]{2,1,0:T(8,128)(2,1)S(1)}, f32[2,1,1536]{2,1,0:T(1,128)S(1)}) custom-call(s32[1]{0:T(128)} %bitcast.place_ref.refs_0_, s32[1,1536]{1,0:T(1,128)S(1)} %shard_map.76.refs_1_, ...), custom_call_target="tpu_custom_call" | custom-call | flops 603979776 | bytes 1048576 | tf_op jit(solution)/shard_map/pallas_call | solution.py:277
  8.0 3.8 %collective-permute-done.1.refs_4_.refs_7_ = bf16[2,2,192,128]{3,2,1,0:T(8,128)(2,1)S(1)} collective-permute-done((bf16[2,2,192,128]{3,2,1,0:T(8,128)(2,1)S(1)}, bf16[2,2,192,128]{3,2,1,0:T(8,128)(2,1)S(1)}, u32[]{:S(2)}, u32[]{:S(2)}) %collective-permute-start.1) | collective-permute-done | bytes 196640 | tf_op jit(solution)/shard_map/ppermute | solution.py:234
  11.8 2.4 %collective-permute-start.2 = (bf16[2,2,192,128]{3,2,1,0:T(8,128)(2,1)S(1)}, bf16[2,2,192,128]{3,2,1,0:T(8,128)(2,1)S(1)}, u32[]{:S(2)}, u32[]{:S(2)}) collective-permute-start(bf16[2,2,192,128]{3,2,1,0:T(8,128)(2,1)S(1)} %collective-permute-done.1.refs_4_.refs_7_), channel_id=1, source_target_pairs={{0,6},{2,4},{4,2},{6,0},{8,14},{10,12},{12,10},{14,8},{16,22},{18,... | collective-permute-start | bytes 589832 | tf_op jit(solution)/shard_map/ppermute | solution.py:234
  14.2 0.5 collective-permute-start.8
  14.7 0.5 collective-permute-start.7
  15.2 2.4 %collective-permute-start = (bf16[2,2,192,128]{3,2,1,0:T(8,128)(2,1)S(1)}, bf16[2,2,192,128]{3,2,1,0:T(8,128)(2,1)S(1)}, u32[]{:S(2)}, u32[]{:S(2)}) collective-permute-start(bf16[2,2,192,128]{3,2,1,0:T(8,128)(2,1)S(1)} %shard_map.77.refs_4_.own_ref.refs_6_), channel_id=1, source_target_pairs={{0,6},{2,4},{4,2},{6,0},{8,14},{10,12},{12,10},{14,8},{16,22},{18,... | collective-permute-start | bytes 589832 | tf_op jit(solution)/shard_map/ppermute | solution.py:234
  17.7 1.9 %collective-permute-done.4.up2_ref = bf16[2,2,192,128]{3,2,1,0:T(8,128)(2,1)S(1)} collective-permute-done((bf16[2,2,192,128]{3,2,1,0:T(8,128)(2,1)S(1)}, bf16[2,2,192,128]{3,2,1,0:T(8,128)(2,1)S(1)}, u32[]{:S(2)}, u32[]{:S(2)}) %collective-permute-start.4) | collective-permute-done | bytes 196640 | tf_op jit(solution)/shard_map/ppermute | solution.py:234
  19.7 1.3 %collective-permute-start.6 = (bf16[2,2,192,128]{3,2,1,0:T(8,128)(2,1)S(1)}, bf16[2,2,192,128]{3,2,1,0:T(8,128)(2,1)S(1)}, u32[]{:S(2)}, u32[]{:S(2)}) collective-permute-start(bf16[2,2,192,128]{3,2,1,0:T(8,128)(2,1)S(1)} %get-tuple-element.76), channel_id=1, source_target_pairs={{0,2},{2,0},{4,6},{6,4},{8,10},{10,8},{12,14},{14,12},{16,18},{18,... | collective-permute-start | bytes 589832 | tf_op jit(solution)/shard_map/ppermute | solution.py:234
  21.0 0.2 shard_map.80
  21.2 1.6 %collective-permute-start.5 = (bf16[2,2,192,128]{3,2,1,0:T(8,128)(2,1)S(1)}, bf16[2,2,192,128]{3,2,1,0:T(8,128)(2,1)S(1)}, u32[]{:S(2)}, u32[]{:S(2)}) collective-permute-start(bf16[2,2,192,128]{3,2,1,0:T(8,128)(2,1)S(1)} %get-tuple-element.75), channel_id=1, source_target_pairs={{0,4},{2,6},{4,0},{6,2},{8,12},{10,14},{12,8},{14,10},{16,20},{18,... | collective-permute-start | bytes 589832 | tf_op jit(solution)/shard_map/ppermute | solution.py:234
  22.8 0.2 shard_map.81
  23.0 1.7 %collective-permute-done.8.refs_4_.refs_6_ = bf16[2,2,192,128]{3,2,1,0:T(8,128)(2,1)S(1)} collective-permute-done((bf16[2,2,192,128]{3,2,1,0:T(8,128)(2,1)S(1)}, bf16[2,2,192,128]{3,2,1,0:T(8,128)(2,1)S(1)}, u32[]{:S(2)}, u32[]{:S(2)}) %collective-permute-start.8) | collective-permute-done | bytes 196640 | tf_op jit(solution)/shard_map/ppermute | solution.py:234
  24.7 1.3 %collective-permute-start.3 = (bf16[2,2,192,128]{3,2,1,0:T(8,128)(2,1)S(1)}, bf16[2,2,192,128]{3,2,1,0:T(8,128)(2,1)S(1)}, u32[]{:S(2)}, u32[]{:S(2)}) collective-permute-start(bf16[2,2,192,128]{3,2,1,0:T(8,128)(2,1)S(1)} %collective-permute-done.2.refs_4_.refs_6_), channel_id=1, source_target_pairs={{0,8},{2,10},{4,12},{6,14},{8,16},{10,18},{12,20},{14,22},{16,24},... | collective-permute-start | bytes 589832 | tf_op jit(solution)/shard_map/ppermute | solution.py:234
  26.0 0.2 shard_map.82
  26.2 0.5 collective-permute-done.7.refs_4_.refs_6_
  26.7 0.2 shard_map.83
  26.9 4.3 %collective-permute-done.6.refs_4_.refs_6_ = bf16[2,2,192,128]{3,2,1,0:T(8,128)(2,1)S(1)} collective-permute-done((bf16[2,2,192,128]{3,2,1,0:T(8,128)(2,1)S(1)}, bf16[2,2,192,128]{3,2,1,0:T(8,128)(2,1)S(1)}, u32[]{:S(2)}, u32[]{:S(2)}) %collective-permute-start.6) | collective-permute-done | bytes 196640 | tf_op jit(solution)/shard_map/ppermute | solution.py:234
  31.2 0.2 shard_map.84
  31.4 0.2 shard_map.85
  31.6 0.5 collective-permute-done.3.far_ref
  32.2 0.2 shard_map.87
  32.4 0.2 shard_map.88
  32.7 0.4 shard_map.89
  33.1 0.2 shard_map.90
  33.3 3.6 %collective-permute-start.9 = (bf16[2,2,192,128]{3,2,1,0:T(8,128)(2,1)S(1)}, bf16[2,2,192,128]{3,2,1,0:T(8,128)(2,1)S(1)}, u32[]{:S(2)}, u32[]{:S(2)}) collective-permute-start(bf16[2,2,192,128]{3,2,1,0:T(8,128)(2,1)S(1)} %get-tuple-element.127), channel_id=1, source_target_pairs={{0,2},{2,0},{4,6},{6,4},{8,10},{10,8},{12,14},{14,12},{16,18},{18,... | collective-permute-start | bytes 589832 | tf_op jit(solution)/shard_map/ppermute | solution.py:234
  37.0 2.3 %collective-permute-start.10 = (bf16[2,2,192,128]{3,2,1,0:T(8,128)(2,1)S(1)}, bf16[2,2,192,128]{3,2,1,0:T(8,128)(2,1)S(1)}, u32[]{:S(2)}, u32[]{:S(2)}) collective-permute-start(bf16[2,2,192,128]{3,2,1,0:T(8,128)(2,1)S(1)} %get-tuple-element.128), channel_id=1, source_target_pairs={{0,4},{2,6},{4,0},{6,2},{8,12},{10,14},{12,8},{14,10},{16,20},{18,... | collective-permute-start | bytes 589832 | tf_op jit(solution)/shard_map/ppermute | solution.py:234
  39.3 1.4 %collective-permute-start.11 = (bf16[2,2,192,128]{3,2,1,0:T(8,128)(2,1)S(1)}, bf16[2,2,192,128]{3,2,1,0:T(8,128)(2,1)S(1)}, u32[]{:S(2)}, u32[]{:S(2)}) collective-permute-start(bf16[2,2,192,128]{3,2,1,0:T(8,128)(2,1)S(1)} %get-tuple-element.129), channel_id=1, source_target_pairs={{0,6},{2,4},{4,2},{6,0},{8,14},{10,12},{12,10},{14,8},{16,22},{18,... | collective-permute-start | bytes 589832 | tf_op jit(solution)/shard_map/ppermute | solution.py:234
  40.7 0.2 shard_map.91
  40.9 0.2 shard_map.92
  41.2 0.2 shard_map.93
  41.4 0.6 collective-permute-start.15
  42.0 1.5 %collective-permute-start.14 = (bf16[2,2,192,128]{3,2,1,0:T(8,128)(2,1)S(1)}, bf16[2,2,192,128]{3,2,1,0:T(8,128)(2,1)S(1)}, u32[]{:S(2)}, u32[]{:S(2)}) collective-permute-start(bf16[2,2,192,128]{3,2,1,0:T(8,128)(2,1)S(1)} %get-tuple-element.135), channel_id=1, source_target_pairs={{0,4},{2,6},{4,0},{6,2},{8,12},{10,14},{12,8},{14,10},{16,20},{18,... | collective-permute-start | bytes 589832 | tf_op jit(solution)/shard_map/ppermute | solution.py:234
  43.6 2.9 %collective-permute-start.13 = (bf16[2,2,192,128]{3,2,1,0:T(8,128)(2,1)S(1)}, bf16[2,2,192,128]{3,2,1,0:T(8,128)(2,1)S(1)}, u32[]{:S(2)}, u32[]{:S(2)}) collective-permute-start(bf16[2,2,192,128]{3,2,1,0:T(8,128)(2,1)S(1)} %get-tuple-element.134), channel_id=1, source_target_pairs={{0,6},{2,4},{4,2},{6,0},{8,14},{10,12},{12,10},{14,8},{16,22},{18,... | collective-permute-start | bytes 589832 | tf_op jit(solution)/shard_map/ppermute | solution.py:234
  46.4 3.4 %collective-permute-done.10.refs_1_ = bf16[2,2,192,128]{3,2,1,0:T(8,128)(2,1)S(1)} collective-permute-done((bf16[2,2,192,128]{3,2,1,0:T(8,128)(2,1)S(1)}, bf16[2,2,192,128]{3,2,1,0:T(8,128)(2,1)S(1)}, u32[]{:S(2)}, u32[]{:S(2)}) %collective-permute-start.10) | collective-permute-done | bytes 196640 | tf_op jit(solution)/shard_map/ppermute | solution.py:234
  49.8 0.9 %collective-permute-done.11.refs_2_ = bf16[2,2,192,128]{3,2,1,0:T(8,128)(2,1)S(1)} collective-permute-done((bf16[2,2,192,128]{3,2,1,0:T(8,128)(2,1)S(1)}, bf16[2,2,192,128]{3,2,1,0:T(8,128)(2,1)S(1)}, u32[]{:S(2)}, u32[]{:S(2)}) %collective-permute-start.11) | collective-permute-done | bytes 196640 | tf_op jit(solution)/shard_map/ppermute | solution.py:234
  50.7 0.2 shard_map.95
  50.9 5.4 %collective-permute-start.12 = (bf16[2,2,192,128]{3,2,1,0:T(8,128)(2,1)S(1)}, bf16[2,2,192,128]{3,2,1,0:T(8,128)(2,1)S(1)}, u32[]{:S(2)}, u32[]{:S(2)}) collective-permute-start(bf16[2,2,192,128]{3,2,1,0:T(8,128)(2,1)S(1)} %get-tuple-element.133), channel_id=1, source_target_pairs={{0,24},{2,26},{4,28},{6,30},{8,0},{10,2},{12,4},{14,6},{16,8},{18,... | collective-permute-start | bytes 589832 | tf_op jit(solution)/shard_map/ppermute | solution.py:234
  56.3 1.9 %shard_map.94 = (bf16[2,2,192,128]{3,2,1,0:T(8,128)(2,1)S(1)}, bf16[2,2,192,128]{3,2,1,0:T(8,128)(2,1)S(1)}, bf16[2,1536,128]{2,1,0:T(8,128)(2,1)S(1)}, f32[2,128,1536]{2,1,0:T(8,128)S(1)}) custom-call(s32[1]{0:T(128)} %bitcast.place_ref.refs_0_, s32[1,1536]{1,0:T(1,128)S(1)} %shard_map.76.refs_1_, ...), custom_call_target="tpu_custom_call", output_to_operand_aliasing={{3}: (12, {})} | custom-call | flops 3019898880 | bytes 1048576 | tf_op jit(solution)/shard_map/pallas_call | solution.py:293
  58.2 1.2 %collective-permute-done.12.refs_1_ = bf16[2,2,192,128]{3,2,1,0:T(8,128)(2,1)S(1)} collective-permute-done((bf16[2,2,192,128]{3,2,1,0:T(8,128)(2,1)S(1)}, bf16[2,2,192,128]{3,2,1,0:T(8,128)(2,1)S(1)}, u32[]{:S(2)}, u32[]{:S(2)}) %collective-permute-start.12) | collective-permute-done | bytes 196640 | tf_op jit(solution)/shard_map/ppermute | solution.py:234
  59.5 0.1 shard_map.96
  59.6 4.3 %collective-permute-start.16 = (bf16[2,2,192,128]{3,2,1,0:T(8,128)(2,1)S(1)}, bf16[2,2,192,128]{3,2,1,0:T(8,128)(2,1)S(1)}, u32[]{:S(2)}, u32[]{:S(2)}) collective-permute-start(bf16[2,2,192,128]{3,2,1,0:T(8,128)(2,1)S(1)} %shard_map.96), channel_id=1, source_target_pairs={{0,24},{2,26},{4,28},{6,30},{8,0},{10,2},{12,4},{14,6},{16,8},{18,... | collective-permute-start | bytes 589832 | tf_op jit(solution)/shard_map/ppermute | solution.py:234
  63.9 1.0 %copy_bitcast_fusion = bf16[192,16,128]{2,1,0:T(8,128)(2,1)} fusion(bf16[2,1536,128]{2,1,0:T(8,128)(2,1)S(1)} %get-tuple-element.126), kind=kLoop, calls=%fused_computation | loop fusion | bytes 1572864 | tf_op jit(solution)/shard_map/reshape | solution.py:346
  64.9 2.2 %collective-permute-done.16.down_ref = bf16[2,2,192,128]{3,2,1,0:T(8,128)(2,1)S(1)} collective-permute-done((bf16[2,2,192,128]{3,2,1,0:T(8,128)(2,1)S(1)}, bf16[2,2,192,128]{3,2,1,0:T(8,128)(2,1)S(1)}, u32[]{:S(2)}, u32[]{:S(2)}) %collective-permute-start.16) | collective-permute-done | bytes 196640 | tf_op jit(solution)/shard_map/ppermute | solution.py:234
  67.1 0.7 %shard_map.97 = (bf16[384,128]{1,0:T(8,128)(2,1)}, bf16[384,128]{1,0:T(8,128)(2,1)}) custom-call(f32[2,2,192,128]{3,2,1,0:T(8,128)S(1)} %get-tuple-element.130.mine_ref, bf16[2,2,192,128]{3,2,1,0:T(8,128)(2,1)S(1)} %get-tuple-element.131.own_ref, bf16[2,2,192,128]{3,2,1,0:T(8,128)(2,1)S(1)} %collective-permute-done.16.down_ref), custom_call_target="tpu_custom_call" | custom-call | tf_op jit(solution)/shard_map/pallas_call | solution.py:240
  (14 shorter events, 0.1 us)
Async XLA Ops:
  0.6 4.2 %copy-start = (bf16[192,16,128]{2,1,0:T(8,128)(2,1)S(1)}, bf16[192,16,128]{2,1,0:T(8,128)(2,1)}, u32[]{:S(2)}) copy-start(bf16[192,16,128]{2,1,0:T(8,128)(2,1)} %param.5) | copy-start | bytes 2359300
  1.7 4.5 %copy-start.1 = (s32[8]{0:T(128)S(1)}, s32[8]{0:T(128)}, u32[]{:S(2)}) copy-start(s32[8]{0:T(128)} %lens_ref.1) | copy-start | bytes 100
  1.7 10.0 %collective-permute-start.1 = (bf16[2,2,192,128]{3,2,1,0:T(8,128)(2,1)S(1)}, bf16[2,2,192,128]{3,2,1,0:T(8,128)(2,1)S(1)}, u32[]{:S(2)}, u32[]{:S(2)}) collective-permute-start(bf16[2,2,192,128]{3,2,1,0:T(8,128)(2,1)S(1)} %shard_map.77.refs_4_.own_ref.refs_6_), channel_id=1, source_target_pairs={{0,8},{2,10},{4,12},{6,14},{8,16},{10,18},{12,20},{14,22},{16,24},... | collective-permute-start | bytes 589832 | tf_op jit(solution)/shard_map/ppermute | solution.py:234
  11.8 7.9 %collective-permute-start.4 = (bf16[2,2,192,128]{3,2,1,0:T(8,128)(2,1)S(1)}, bf16[2,2,192,128]{3,2,1,0:T(8,128)(2,1)S(1)}, u32[]{:S(2)}, u32[]{:S(2)}) collective-permute-start(bf16[2,2,192,128]{3,2,1,0:T(8,128)(2,1)S(1)} %collective-permute-done.1.refs_4_.refs_7_), channel_id=1, source_target_pairs={{0,8},{2,10},{4,12},{6,14},{8,16},{10,18},{12,20},{14,22},{16,24},... | collective-permute-start | bytes 589832 | tf_op jit(solution)/shard_map/ppermute | solution.py:234
  11.8 9.4 %collective-permute-start.2 = (bf16[2,2,192,128]{3,2,1,0:T(8,128)(2,1)S(1)}, bf16[2,2,192,128]{3,2,1,0:T(8,128)(2,1)S(1)}, u32[]{:S(2)}, u32[]{:S(2)}) collective-permute-start(bf16[2,2,192,128]{3,2,1,0:T(8,128)(2,1)S(1)} %collective-permute-done.1.refs_4_.refs_7_), channel_id=1, source_target_pairs={{0,6},{2,4},{4,2},{6,0},{8,14},{10,12},{12,10},{14,8},{16,22},{18,... | collective-permute-start | bytes 589832 | tf_op jit(solution)/shard_map/ppermute | solution.py:234
  14.2 10.5 %collective-permute-start.8 = (bf16[2,2,192,128]{3,2,1,0:T(8,128)(2,1)S(1)}, bf16[2,2,192,128]{3,2,1,0:T(8,128)(2,1)S(1)}, u32[]{:S(2)}, u32[]{:S(2)}) collective-permute-start(bf16[2,2,192,128]{3,2,1,0:T(8,128)(2,1)S(1)} %collective-permute-done.1.refs_4_.refs_7_), channel_id=1, source_target_pairs={{0,2},{2,0},{4,6},{6,4},{8,10},{10,8},{12,14},{14,12},{16,18},{18,... | collective-permute-start | bytes 589832 | tf_op jit(solution)/shard_map/ppermute | solution.py:234
  14.7 12.0 %collective-permute-start.7 = (bf16[2,2,192,128]{3,2,1,0:T(8,128)(2,1)S(1)}, bf16[2,2,192,128]{3,2,1,0:T(8,128)(2,1)S(1)}, u32[]{:S(2)}, u32[]{:S(2)}) collective-permute-start(bf16[2,2,192,128]{3,2,1,0:T(8,128)(2,1)S(1)} %collective-permute-done.1.refs_4_.refs_7_), channel_id=1, source_target_pairs={{0,4},{2,6},{4,0},{6,2},{8,12},{10,14},{12,8},{14,10},{16,20},{18,... | collective-permute-start | bytes 589832 | tf_op jit(solution)/shard_map/ppermute | solution.py:234
  15.2 16.9 %collective-permute-start = (bf16[2,2,192,128]{3,2,1,0:T(8,128)(2,1)S(1)}, bf16[2,2,192,128]{3,2,1,0:T(8,128)(2,1)S(1)}, u32[]{:S(2)}, u32[]{:S(2)}) collective-permute-start(bf16[2,2,192,128]{3,2,1,0:T(8,128)(2,1)S(1)} %shard_map.77.refs_4_.own_ref.refs_6_), channel_id=1, source_target_pairs={{0,6},{2,4},{4,2},{6,0},{8,14},{10,12},{12,10},{14,8},{16,22},{18,... | collective-permute-start | bytes 589832 | tf_op jit(solution)/shard_map/ppermute | solution.py:234
  19.7 11.5 %collective-permute-start.6 = (bf16[2,2,192,128]{3,2,1,0:T(8,128)(2,1)S(1)}, bf16[2,2,192,128]{3,2,1,0:T(8,128)(2,1)S(1)}, u32[]{:S(2)}, u32[]{:S(2)}) collective-permute-start(bf16[2,2,192,128]{3,2,1,0:T(8,128)(2,1)S(1)} %get-tuple-element.76), channel_id=1, source_target_pairs={{0,2},{2,0},{4,6},{6,4},{8,10},{10,8},{12,14},{14,12},{16,18},{18,... | collective-permute-start | bytes 589832 | tf_op jit(solution)/shard_map/ppermute | solution.py:234
  21.2 10.2 %collective-permute-start.5 = (bf16[2,2,192,128]{3,2,1,0:T(8,128)(2,1)S(1)}, bf16[2,2,192,128]{3,2,1,0:T(8,128)(2,1)S(1)}, u32[]{:S(2)}, u32[]{:S(2)}) collective-permute-start(bf16[2,2,192,128]{3,2,1,0:T(8,128)(2,1)S(1)} %get-tuple-element.75), channel_id=1, source_target_pairs={{0,4},{2,6},{4,0},{6,2},{8,12},{10,14},{12,8},{14,10},{16,20},{18,... | collective-permute-start | bytes 589832 | tf_op jit(solution)/shard_map/ppermute | solution.py:234
  24.7 7.5 %collective-permute-start.3 = (bf16[2,2,192,128]{3,2,1,0:T(8,128)(2,1)S(1)}, bf16[2,2,192,128]{3,2,1,0:T(8,128)(2,1)S(1)}, u32[]{:S(2)}, u32[]{:S(2)}) collective-permute-start(bf16[2,2,192,128]{3,2,1,0:T(8,128)(2,1)S(1)} %collective-permute-done.2.refs_4_.refs_6_), channel_id=1, source_target_pairs={{0,8},{2,10},{4,12},{6,14},{8,16},{10,18},{12,20},{14,22},{16,24},... | collective-permute-start | bytes 589832 | tf_op jit(solution)/shard_map/ppermute | solution.py:234
  33.3 10.3 %collective-permute-start.9 = (bf16[2,2,192,128]{3,2,1,0:T(8,128)(2,1)S(1)}, bf16[2,2,192,128]{3,2,1,0:T(8,128)(2,1)S(1)}, u32[]{:S(2)}, u32[]{:S(2)}) collective-permute-start(bf16[2,2,192,128]{3,2,1,0:T(8,128)(2,1)S(1)} %get-tuple-element.127), channel_id=1, source_target_pairs={{0,2},{2,0},{4,6},{6,4},{8,10},{10,8},{12,14},{14,12},{16,18},{18,... | collective-permute-start | bytes 589832 | tf_op jit(solution)/shard_map/ppermute | solution.py:234
  37.0 12.8 %collective-permute-start.10 = (bf16[2,2,192,128]{3,2,1,0:T(8,128)(2,1)S(1)}, bf16[2,2,192,128]{3,2,1,0:T(8,128)(2,1)S(1)}, u32[]{:S(2)}, u32[]{:S(2)}) collective-permute-start(bf16[2,2,192,128]{3,2,1,0:T(8,128)(2,1)S(1)} %get-tuple-element.128), channel_id=1, source_target_pairs={{0,4},{2,6},{4,0},{6,2},{8,12},{10,14},{12,8},{14,10},{16,20},{18,... | collective-permute-start | bytes 589832 | tf_op jit(solution)/shard_map/ppermute | solution.py:234
  39.3 11.4 %collective-permute-start.11 = (bf16[2,2,192,128]{3,2,1,0:T(8,128)(2,1)S(1)}, bf16[2,2,192,128]{3,2,1,0:T(8,128)(2,1)S(1)}, u32[]{:S(2)}, u32[]{:S(2)}) collective-permute-start(bf16[2,2,192,128]{3,2,1,0:T(8,128)(2,1)S(1)} %get-tuple-element.129), channel_id=1, source_target_pairs={{0,6},{2,4},{4,2},{6,0},{8,14},{10,12},{12,10},{14,8},{16,22},{18,... | collective-permute-start | bytes 589832 | tf_op jit(solution)/shard_map/ppermute | solution.py:234
  41.4 16.8 %collective-permute-start.15 = (bf16[2,2,192,128]{3,2,1,0:T(8,128)(2,1)S(1)}, bf16[2,2,192,128]{3,2,1,0:T(8,128)(2,1)S(1)}, u32[]{:S(2)}, u32[]{:S(2)}) collective-permute-start(bf16[2,2,192,128]{3,2,1,0:T(8,128)(2,1)S(1)} %get-tuple-element.136), channel_id=1, source_target_pairs={{0,2},{2,0},{4,6},{6,4},{8,10},{10,8},{12,14},{14,12},{16,18},{18,... | collective-permute-start | bytes 589832 | tf_op jit(solution)/shard_map/ppermute | solution.py:234
  42.0 16.2 %collective-permute-start.14 = (bf16[2,2,192,128]{3,2,1,0:T(8,128)(2,1)S(1)}, bf16[2,2,192,128]{3,2,1,0:T(8,128)(2,1)S(1)}, u32[]{:S(2)}, u32[]{:S(2)}) collective-permute-start(bf16[2,2,192,128]{3,2,1,0:T(8,128)(2,1)S(1)} %get-tuple-element.135), channel_id=1, source_target_pairs={{0,4},{2,6},{4,0},{6,2},{8,12},{10,14},{12,8},{14,10},{16,20},{18,... | collective-permute-start | bytes 589832 | tf_op jit(solution)/shard_map/ppermute | solution.py:234
  43.6 14.7 %collective-permute-start.13 = (bf16[2,2,192,128]{3,2,1,0:T(8,128)(2,1)S(1)}, bf16[2,2,192,128]{3,2,1,0:T(8,128)(2,1)S(1)}, u32[]{:S(2)}, u32[]{:S(2)}) collective-permute-start(bf16[2,2,192,128]{3,2,1,0:T(8,128)(2,1)S(1)} %get-tuple-element.134), channel_id=1, source_target_pairs={{0,6},{2,4},{4,2},{6,0},{8,14},{10,12},{12,10},{14,8},{16,22},{18,... | collective-permute-start | bytes 589832 | tf_op jit(solution)/shard_map/ppermute | solution.py:234
  50.9 8.6 %collective-permute-start.12 = (bf16[2,2,192,128]{3,2,1,0:T(8,128)(2,1)S(1)}, bf16[2,2,192,128]{3,2,1,0:T(8,128)(2,1)S(1)}, u32[]{:S(2)}, u32[]{:S(2)}) collective-permute-start(bf16[2,2,192,128]{3,2,1,0:T(8,128)(2,1)S(1)} %get-tuple-element.133), channel_id=1, source_target_pairs={{0,24},{2,26},{4,28},{6,30},{8,0},{10,2},{12,4},{14,6},{16,8},{18,... | collective-permute-start | bytes 589832 | tf_op jit(solution)/shard_map/ppermute | solution.py:234
  59.6 7.5 %collective-permute-start.16 = (bf16[2,2,192,128]{3,2,1,0:T(8,128)(2,1)S(1)}, bf16[2,2,192,128]{3,2,1,0:T(8,128)(2,1)S(1)}, u32[]{:S(2)}, u32[]{:S(2)}) collective-permute-start(bf16[2,2,192,128]{3,2,1,0:T(8,128)(2,1)S(1)} %shard_map.96), channel_id=1, source_target_pairs={{0,24},{2,26},{4,28},{6,30},{8,0},{10,2},{12,4},{14,6},{16,8},{18,... | collective-permute-start | bytes 589832 | tf_op jit(solution)/shard_map/ppermute | solution.py:234

commit v8 on v7

--- a/solution.py
+++ b/solution.py
@@ -11,7 +11,6 @@
 
 PLANE = 4
 FLIPS = (1, 2, 3)
-BACK = (2, 1, 0)
 DIAGONAL = 3
 LOG2E = math.log2(math.e)
 NEG_INIT = -1e30
@@ -190,8 +189,15 @@
         out_ref[...] = near_ref[...]
 
 
+def join_kernel(place_ref, part_ref, above_ref, out_ref):
+    lane = lax.rem(place_ref[0], PLANE)
+    ahead = jnp.bitwise_xor(lane, DIAGONAL) > lane
+    above = jnp.where(ahead, above_ref[...].astype(jnp.float32), 0.0)
+    out_ref[...] = (part_ref[...].astype(jnp.float32) + above).astype(jnp.bfloat16)
+
+
 def far_kernel(place_ref, *refs):
-    mix_refs, (far_ref, mine_ref) = refs[:3], refs[3:]
+    mix_refs, (far_ref, mine_ref) = refs[:2], refs[2:]
     lane = lax.rem(place_ref[0], PLANE)
     mine = jnp.zeros(mine_ref.shape, jnp.float32)
     far = jnp.zeros_like(mine)
@@ -211,12 +217,15 @@
     refs[-1][...] = total.astype(jnp.bfloat16)
 
 
-def total_kernel(mine_ref, own_ref, down_ref, k_ref, v_ref, wide):
+def total_kernel(place_ref, mine_ref, own_ref, down_ref, near_ref, k_ref, v_ref, wide):
+    lane = lax.rem(place_ref[0], PLANE)
+    ahead = jnp.bitwise_xor(lane, DIAGONAL) > lane
     groups, stripe = mine_ref.shape[-3:-1]
     for n, ref in enumerate((k_ref, v_ref)):
         for g in range(groups):
+            near = jnp.where(ahead, near_ref[n, g].astype(jnp.float32), 0.0)
             wide[pl.ds(g, stripe, stride=groups), :] = (
-                mine_ref[n, g] + own_ref[n, g].astype(jnp.float32) + down_ref[n, g].astype(jnp.float32)
+                mine_ref[n, g] + own_ref[n, g].astype(jnp.float32) + down_ref[n, g].astype(jnp.float32) + near
             )
         ref[...] = wide[...].astype(jnp.bfloat16)
 
@@ -282,7 +291,8 @@
             input_output_aliases={} if old is None else {4 + len(kvs) + i: i for i in range(3)},
             **params(2, len(kvs)),
         )(place, start, q, do, *kvs, *(old or ()))
-        kept[name] = outs[3:]
+        for k in range(len(kvs)):
+            kept[f"{name}{k + 1}" if len(kvs) > 1 else name] = outs[3 + k], outs[3 + len(kvs) + k]
         return outs[:3]
 
     def grads(name, slots, kvs, old=None, last=False):
@@ -319,8 +329,8 @@
     seen = stats("up", [up_slot], [up], seen)
     outgoing = small(outgoing_kernel, [place, own, up2], [shaped(jnp.bfloat16)] * 2)
     mix = [swap(x, f) for x, f in zip(outgoing, FLIPS)]
-    for k in (2, 0, 1):
-        seen = stats(f"upx{FLIPS[k]}", [upx_slots[k]], [upx[k]], seen)
+    seen = stats("upx3", upx_slots[2:], upx[2:], seen)
+    seen = stats("upx", upx_slots[:2], upx[:2], seen)
     for k in (0, 1):
         seen = stats(f"mix{FLIPS[k]}", [mix_slots[k]], [mix[k]], seen)
     up3, seen = lax.optimization_barrier((up3, seen))
@@ -328,21 +338,26 @@
     seen = stats("mix3", [mix_slots[2]], [mix[2]], seen, last=True)
     m, _, d = seen
 
-    dq, mixed, level = None, [], []
-    for k, f in zip(BACK, FLIPS[::-1]):
-        (part,), dq = grads(f"mix{f}", [mix_slots[k]], [mix[k]], dq)
-        mixed.append(swap(part, f))
-    for k, f in zip(BACK, FLIPS[::-1]):
-        (part,), dq = grads(f"upx{f}", [upx_slots[k]], [upx[k]], dq)
-        level.append(swap(part, f))
+    mixed, level = {}, []
+    (diagonal,), dq = grads("mix3", [mix_slots[2]], [mix[2]])
+    above = shift(diagonal, -PLANE)
+    for k in (1, 0):
+        (part,), dq = grads(f"mix{FLIPS[k]}", [mix_slots[k]], [mix[k]], dq)
+        mixed[k] = swap(part, FLIPS[k])
+    for k in (1, 2, 0):
+        (part,), dq = grads(f"upx{FLIPS[k]}", [upx_slots[k]], [upx[k]], dq)
+        if FLIPS[k] == DIAGONAL:
+            (part,) = small(join_kernel, [place, part, above], [shaped(jnp.bfloat16)])
+        level.append(swap(part, FLIPS[k]))
     (own_part, up_part), dq = grads("own up", [own_slot, up_slot], [own, up], dq, last=True)
-
-    far, mine = small(far_kernel, [place, *mixed[::-1]], [shaped(jnp.bfloat16), shaped(jnp.float32)])
+    near_back = swap(diagonal, DIAGONAL)
+
+    far, mine = small(far_kernel, [place, mixed[0], mixed[1]], [shaped(jnp.bfloat16), shaped(jnp.float32)])
     down2 = shift(far, -PLANE)
     (below,) = small(level_kernel, [up_part, down2, *level], [shaped(jnp.bfloat16)])
     down = shift(below, -PLANE)
     flat_out = jax.ShapeDtypeStruct(flat, jnp.bfloat16)
-    grad_k, grad_v = small(total_kernel, [mine, own_part, down], [flat_out, flat_out], [wide])
+    grad_k, grad_v = small(total_kernel, [place, mine, own_part, down, near_back], [flat_out, flat_out], [wide])
     dq = dq.reshape(groups, stripe, heads_per, dim).transpose(1, 0, 2, 3).reshape(stripe, heads, dim)
     return dq, grad_k.reshape(key_vectors.shape), grad_v.reshape(value_matrix.shape)
 

time: 68 us -> 67.2 us (0.988)
  starting transfers between devices: 35.3 us -> 32 us
  waiting for transfers between devices: 20.4 us -> 23.1 us
    ppermute x17 -> x18, starting transfers between devices: 35.3 us -> 32 us  [send(): return lax.ppermute(array, 'ctx', [(i, to(i)) for i in range(length)])]
    ppermute x17 -> x18, waiting for transfers between devices: 20.4 us -> 23.1 us  [send(): return lax.ppermute(array, 'ctx', [(i, to(i)) for i in range(length)])]
    pallas_call x8 -> x7, Pallas kernels: 2.58 us -> 2.38 us  [stats(): pl.pallas_call(functools.partial(stats_kernel, slots, heads_per, old is N...]
    pallas_call x6 -> x7, Pallas kernels: 2.17 us -> 2.2 us  [small(): pl.pallas_call(body, out_shape=shapes, in_specs=[SMEM if x is place else...]
  transfers between devices with their start and end apart: 17 -> 18, of which waited for: 10 -> 10; matrix products, arithmetic and copies ran while one was open for 4% -> 4% of each run, Pallas kernels for 9% -> 9%
where the time goes in v8:
time: 67.2 us; the launch traced here: 67 us
  starting transfers between devices  32 us (48%)
  waiting for transfers between devices  23.1 us (34%)
  Pallas kernels  8.65 us (13%)
  local copies, waits for them, and re-layouts  2.43 us (4%)
  between operations  0.85 us (1%)
    ppermute x18, starting transfers between devices, send(): return lax.ppermute(array, 'ctx', [(i, to(i)) for i in range(length)])  32 us
    ppermute x18, waiting for transfers between devices, send(): return lax.ppermute(array, 'ctx', [(i, to(i)) for i in range(length)])  23.1 us
    pallas_call x7, Pallas kernels, grads(): pl.pallas_call(functools.partial(grad_kernel, slots, old is None, last),...  3.49 us
    pallas_call x7, Pallas kernels, stats(): pl.pallas_call(functools.partial(stats_kernel, slots, heads_per, old is N...  2.38 us
    pallas_call x7, Pallas kernels, small(): pl.pallas_call(body, out_shape=shapes, in_specs=[SMEM if x is place else...  2.2 us
    reshape x1, local copies, waits for them, and re-layouts, columns(): array.reshape(stripe, groups, heads_per, dim).transpose(1, 0, 2, 3)  1.4 us
  transfers between devices with their start and end apart: 18, of which 10 were waited for; matrix products, arithmetic and copies ran while one was open for 4% of the time, Pallas kernels for 9%

profile of v8, /device:TPU:0, one launch (start us, length us, event | category | flops | bytes accessed | tf_op | source)
XLA Modules:
  0.0 67.0 jit_solution(8255564775396863878)
XLA Ops:
  0.6 1.1 %shard_map.77.refs_4_.own_ref.refs_6_ = bf16[2,2,192,128]{3,2,1,0:T(8,128)(2,1)S(1)} custom-call(bf16[384,128]{1,0:T(8,128)(2,1)} %bitcast.26, bf16[384,128]{1,0:T(8,128)(2,1)} %bitcast.27), custom_call_target="tpu_custom_call" | custom-call | tf_op jit(solution)/shard_map/pallas_call | solution.py:249
  1.7 3.1 %collective-permute-start.1 = (bf16[2,2,192,128]{3,2,1,0:T(8,128)(2,1)S(1)}, bf16[2,2,192,128]{3,2,1,0:T(8,128)(2,1)S(1)}, u32[]{:S(2)}, u32[]{:S(2)}) collective-permute-start(bf16[2,2,192,128]{3,2,1,0:T(8,128)(2,1)S(1)} %shard_map.77.refs_4_.own_ref.refs_6_), channel_id=1, source_target_pairs={{0,8},{2,10},{4,12},{6,14},{8,16},{10,18},{12,20},{14,22},{16,24},... | collective-permute-start | bytes 589832 | tf_op jit(solution)/shard_map/ppermute | solution.py:243
  4.8 1.4 %copy_bitcast_fusion.1 = (bf16[2,1536,128]{2,1,0:T(8,128)(2,1)S(1)}, bf16[2,1536,128]{2,1,0:T(8,128)(2,1)S(1)}) fusion(bf16[192,16,128]{2,1,0:T(8,128)(2,1)S(1)} %copy-done, bf16[192,16,128]{2,1,0:T(8,128)(2,1)} %param.8), kind=kLoop, calls=%fused_computation.1 | loop fusion | bytes 3145728 | tf_op jit(solution)/shard_map/reshape | solution.py:246
  6.3 0.6 shard_map.76.refs_1_
  6.8 1.1 %shard_map.78 = (f32[2,1,1536]{2,1,0:T(1,128)S(1)}, f32[2,1,1536]{2,1,0:T(1,128)S(1)}, f32[2,1,1536]{2,1,0:T(1,128)S(1)}, bf16[2,192,1536]{2,1,0:T(8,128)(2,1)S(1)}, f32[2,1,1536]{2,1,0:T(1,128)S(1)}) custom-call(s32[1]{0:T(128)} %bitcast.place_ref.refs_0_, s32[1,1536]{1,0:T(1,128)S(1)} %shard_map.76.refs_1_, ...), custom_call_target="tpu_custom_call" | custom-call | flops 603979776 | bytes 1048576 | tf_op jit(solution)/shard_map/pallas_call | solution.py:286
  8.0 3.8 %collective-permute-done.1.refs_4_.refs_7_ = bf16[2,2,192,128]{3,2,1,0:T(8,128)(2,1)S(1)} collective-permute-done((bf16[2,2,192,128]{3,2,1,0:T(8,128)(2,1)S(1)}, bf16[2,2,192,128]{3,2,1,0:T(8,128)(2,1)S(1)}, u32[]{:S(2)}, u32[]{:S(2)}) %collective-permute-start.1) | collective-permute-done | bytes 196640 | tf_op jit(solution)/shard_map/ppermute | solution.py:243
  11.8 2.4 %collective-permute-start.2 = (bf16[2,2,192,128]{3,2,1,0:T(8,128)(2,1)S(1)}, bf16[2,2,192,128]{3,2,1,0:T(8,128)(2,1)S(1)}, u32[]{:S(2)}, u32[]{:S(2)}) collective-permute-start(bf16[2,2,192,128]{3,2,1,0:T(8,128)(2,1)S(1)} %collective-permute-done.1.refs_4_.refs_7_), channel_id=1, source_target_pairs={{0,6},{2,4},{4,2},{6,0},{8,14},{10,12},{12,10},{14,8},{16,22},{18,... | collective-permute-start | bytes 589832 | tf_op jit(solution)/shard_map/ppermute | solution.py:243
  14.2 0.5 collective-permute-start.8
  14.7 0.5 collective-permute-start.7
  15.2 2.4 %collective-permute-start = (bf16[2,2,192,128]{3,2,1,0:T(8,128)(2,1)S(1)}, bf16[2,2,192,128]{3,2,1,0:T(8,128)(2,1)S(1)}, u32[]{:S(2)}, u32[]{:S(2)}) collective-permute-start(bf16[2,2,192,128]{3,2,1,0:T(8,128)(2,1)S(1)} %shard_map.77.refs_4_.own_ref.refs_6_), channel_id=1, source_target_pairs={{0,6},{2,4},{4,2},{6,0},{8,14},{10,12},{12,10},{14,8},{16,22},{18,... | collective-permute-start | bytes 589832 | tf_op jit(solution)/shard_map/ppermute | solution.py:243
  17.7 1.9 %collective-permute-done.4.up2_ref = bf16[2,2,192,128]{3,2,1,0:T(8,128)(2,1)S(1)} collective-permute-done((bf16[2,2,192,128]{3,2,1,0:T(8,128)(2,1)S(1)}, bf16[2,2,192,128]{3,2,1,0:T(8,128)(2,1)S(1)}, u32[]{:S(2)}, u32[]{:S(2)}) %collective-permute-start.4) | collective-permute-done | bytes 196640 | tf_op jit(solution)/shard_map/ppermute | solution.py:243
  19.7 1.3 %collective-permute-start.6 = (bf16[2,2,192,128]{3,2,1,0:T(8,128)(2,1)S(1)}, bf16[2,2,192,128]{3,2,1,0:T(8,128)(2,1)S(1)}, u32[]{:S(2)}, u32[]{:S(2)}) collective-permute-start(bf16[2,2,192,128]{3,2,1,0:T(8,128)(2,1)S(1)} %get-tuple-element.73), channel_id=1, source_target_pairs={{0,2},{2,0},{4,6},{6,4},{8,10},{10,8},{12,14},{14,12},{16,18},{18,... | collective-permute-start | bytes 589832 | tf_op jit(solution)/shard_map/ppermute | solution.py:243
  21.0 0.2 shard_map.80
  21.2 1.6 %collective-permute-start.5 = (bf16[2,2,192,128]{3,2,1,0:T(8,128)(2,1)S(1)}, bf16[2,2,192,128]{3,2,1,0:T(8,128)(2,1)S(1)}, u32[]{:S(2)}, u32[]{:S(2)}) collective-permute-start(bf16[2,2,192,128]{3,2,1,0:T(8,128)(2,1)S(1)} %get-tuple-element.72), channel_id=1, source_target_pairs={{0,4},{2,6},{4,0},{6,2},{8,12},{10,14},{12,8},{14,10},{16,20},{18,... | collective-permute-start | bytes 589832 | tf_op jit(solution)/shard_map/ppermute | solution.py:243
  22.8 0.2 shard_map.81
  23.0 3.2 %collective-permute-done.8.refs_5_.refs_6_ = bf16[2,2,192,128]{3,2,1,0:T(8,128)(2,1)S(1)} collective-permute-done((bf16[2,2,192,128]{3,2,1,0:T(8,128)(2,1)S(1)}, bf16[2,2,192,128]{3,2,1,0:T(8,128)(2,1)S(1)}, u32[]{:S(2)}, u32[]{:S(2)}) %collective-permute-start.8) | collective-permute-done | bytes 196640 | tf_op jit(solution)/shard_map/ppermute | solution.py:243
  26.2 1.3 %collective-permute-start.3 = (bf16[2,2,192,128]{3,2,1,0:T(8,128)(2,1)S(1)}, bf16[2,2,192,128]{3,2,1,0:T(8,128)(2,1)S(1)}, u32[]{:S(2)}, u32[]{:S(2)}) collective-permute-start(bf16[2,2,192,128]{3,2,1,0:T(8,128)(2,1)S(1)} %collective-permute-done.2.refs_4_.refs_6_), channel_id=1, source_target_pairs={{0,8},{2,10},{4,12},{6,14},{8,16},{10,18},{12,20},{14,22},{16,24},... | collective-permute-start | bytes 589832 | tf_op jit(solution)/shard_map/ppermute | solution.py:243
  27.5 0.2 shard_map.82
  27.7 3.5 %collective-permute-done.6.refs_4_.refs_6_ = bf16[2,2,192,128]{3,2,1,0:T(8,128)(2,1)S(1)} collective-permute-done((bf16[2,2,192,128]{3,2,1,0:T(8,128)(2,1)S(1)}, bf16[2,2,192,128]{3,2,1,0:T(8,128)(2,1)S(1)}, u32[]{:S(2)}, u32[]{:S(2)}) %collective-permute-start.6) | collective-permute-done | bytes 196640 | tf_op jit(solution)/shard_map/ppermute | solution.py:243
  31.2 0.2 shard_map.83
  31.5 0.2 shard_map.84
  31.7 2.0 %collective-permute-done.3.far_ref = bf16[2,2,192,128]{3,2,1,0:T(8,128)(2,1)S(1)} collective-permute-done((bf16[2,2,192,128]{3,2,1,0:T(8,128)(2,1)S(1)}, bf16[2,2,192,128]{3,2,1,0:T(8,128)(2,1)S(1)}, u32[]{:S(2)}, u32[]{:S(2)}) %collective-permute-start.3) | collective-permute-done | bytes 196640 | tf_op jit(solution)/shard_map/ppermute | solution.py:243
  33.7 0.2 shard_map.86
  33.9 0.2 shard_map.87
  34.2 1.0 %collective-permute-start.17 = (bf16[2,2,192,128]{3,2,1,0:T(8,128)(2,1)S(1)}, bf16[2,2,192,128]{3,2,1,0:T(8,128)(2,1)S(1)}, u32[]{:S(2)}, u32[]{:S(2)}) collective-permute-start(bf16[2,2,192,128]{3,2,1,0:T(8,128)(2,1)S(1)} %get-tuple-element.129), channel_id=1, source_target_pairs={{0,6},{2,4},{4,2},{6,0},{8,14},{10,12},{12,10},{14,8},{16,22},{18,... | collective-permute-start | bytes 589832 | tf_op jit(solution)/shard_map/ppermute | solution.py:243
  35.2 5.6 %collective-permute-start.13 = (bf16[2,2,192,128]{3,2,1,0:T(8,128)(2,1)S(1)}, bf16[2,2,192,128]{3,2,1,0:T(8,128)(2,1)S(1)}, u32[]{:S(2)}, u32[]{:S(2)}) collective-permute-start(bf16[2,2,192,128]{3,2,1,0:T(8,128)(2,1)S(1)} %get-tuple-element.129), channel_id=1, source_target_pairs={{0,24},{2,26},{4,28},{6,30},{8,0},{10,2},{12,4},{14,6},{16,8},{18,... | collective-permute-start | bytes 589832 | tf_op jit(solution)/shard_map/ppermute | solution.py:243
  40.8 0.4 shard_map.88
  41.2 0.2 shard_map.89
  41.4 1.7 %collective-permute-start.9 = (bf16[2,2,192,128]{3,2,1,0:T(8,128)(2,1)S(1)}, bf16[2,2,192,128]{3,2,1,0:T(8,128)(2,1)S(1)}, u32[]{:S(2)}, u32[]{:S(2)}) collective-permute-start(bf16[2,2,192,128]{3,2,1,0:T(8,128)(2,1)S(1)} %get-tuple-element.121), channel_id=1, source_target_pairs={{0,2},{2,0},{4,6},{6,4},{8,10},{10,8},{12,14},{14,12},{16,18},{18,... | collective-permute-start | bytes 589832 | tf_op jit(solution)/shard_map/ppermute | solution.py:243
  43.1 3.1 %collective-permute-start.10 = (bf16[2,2,192,128]{3,2,1,0:T(8,128)(2,1)S(1)}, bf16[2,2,192,128]{3,2,1,0:T(8,128)(2,1)S(1)}, u32[]{:S(2)}, u32[]{:S(2)}) collective-permute-start(bf16[2,2,192,128]{3,2,1,0:T(8,128)(2,1)S(1)} %get-tuple-element.122), channel_id=1, source_target_pairs={{0,4},{2,6},{4,0},{6,2},{8,12},{10,14},{12,8},{14,10},{16,20},{18,... | collective-permute-start | bytes 589832 | tf_op jit(solution)/shard_map/ppermute | solution.py:243
  46.3 0.2 shard_map.90
  46.5 0.2 shard_map.91
  46.8 0.2 shard_map.92
  47.0 0.1 collective-permute-start.15
  47.2 1.4 %collective-permute-done.9.refs_0_ = bf16[2,2,192,128]{3,2,1,0:T(8,128)(2,1)S(1)} collective-permute-done((bf16[2,2,192,128]{3,2,1,0:T(8,128)(2,1)S(1)}, bf16[2,2,192,128]{3,2,1,0:T(8,128)(2,1)S(1)}, u32[]{:S(2)}, u32[]{:S(2)}) %collective-permute-start.9) | collective-permute-done | bytes 196640 | tf_op jit(solution)/shard_map/ppermute | solution.py:243
  48.5 2.8 %collective-permute-start.12 = (bf16[2,2,192,128]{3,2,1,0:T(8,128)(2,1)S(1)}, bf16[2,2,192,128]{3,2,1,0:T(8,128)(2,1)S(1)}, u32[]{:S(2)}, u32[]{:S(2)}) collective-permute-start(bf16[2,2,192,128]{3,2,1,0:T(8,128)(2,1)S(1)} %get-tuple-element.127), channel_id=1, source_target_pairs={{0,4},{2,6},{4,0},{6,2},{8,12},{10,14},{12,8},{14,10},{16,20},{18,... | collective-permute-start | bytes 589832 | tf_op jit(solution)/shard_map/ppermute | solution.py:243
  51.4 0.1 shard_map.94
  51.5 2.2 %collective-permute-start.11 = (bf16[2,2,192,128]{3,2,1,0:T(8,128)(2,1)S(1)}, bf16[2,2,192,128]{3,2,1,0:T(8,128)(2,1)S(1)}, u32[]{:S(2)}, u32[]{:S(2)}) collective-permute-start(bf16[2,2,192,128]{3,2,1,0:T(8,128)(2,1)S(1)} %get-tuple-element.126), channel_id=1, source_target_pairs={{0,24},{2,26},{4,28},{6,30},{8,0},{10,2},{12,4},{14,6},{16,8},{18,... | collective-permute-start | bytes 589832 | tf_op jit(solution)/shard_map/ppermute | solution.py:243
  53.8 1.3 %collective-permute-start.14 = (bf16[2,2,192,128]{3,2,1,0:T(8,128)(2,1)S(1)}, bf16[2,2,192,128]{3,2,1,0:T(8,128)(2,1)S(1)}, u32[]{:S(2)}, u32[]{:S(2)}) collective-permute-start(bf16[2,2,192,128]{3,2,1,0:T(8,128)(2,1)S(1)} %shard_map.95), channel_id=1, source_target_pairs={{0,6},{2,4},{4,2},{6,0},{8,14},{10,12},{12,10},{14,8},{16,22},{18,... | collective-permute-start | bytes 589832 | tf_op jit(solution)/shard_map/ppermute | solution.py:243
  55.1 1.9 %shard_map.93 = (bf16[2,2,192,128]{3,2,1,0:T(8,128)(2,1)S(1)}, bf16[2,2,192,128]{3,2,1,0:T(8,128)(2,1)S(1)}, bf16[2,1536,128]{2,1,0:T(8,128)(2,1)S(1)}, f32[2,128,1536]{2,1,0:T(8,128)S(1)}) custom-call(s32[1]{0:T(128)} %bitcast.place_ref.refs_0_, s32[1,1536]{1,0:T(1,128)S(1)} %shard_map.76.refs_1_, ...), custom_call_target="tpu_custom_call", output_to_operand_aliasing={{3}: (12, {})} | custom-call | flops 3019898880 | bytes 1048576 | tf_op jit(solution)/shard_map/pallas_call | solution.py:303
  57.0 0.1 collective-permute-done.12.refs_2_
  57.1 0.1 collective-permute-done.11.refs_1_
  57.2 3.1 %collective-permute-done.14.refs_3_ = bf16[2,2,192,128]{3,2,1,0:T(8,128)(2,1)S(1)} collective-permute-done((bf16[2,2,192,128]{3,2,1,0:T(8,128)(2,1)S(1)}, bf16[2,2,192,128]{3,2,1,0:T(8,128)(2,1)S(1)}, u32[]{:S(2)}, u32[]{:S(2)}) %collective-permute-start.14) | collective-permute-done | bytes 196640 | tf_op jit(solution)/shard_map/ppermute | solution.py:243
  60.4 0.1 shard_map.96
  60.5 0.8 %collective-permute-start.16 = (bf16[2,2,192,128]{3,2,1,0:T(8,128)(2,1)S(1)}, bf16[2,2,192,128]{3,2,1,0:T(8,128)(2,1)S(1)}, u32[]{:S(2)}, u32[]{:S(2)}) collective-permute-start(bf16[2,2,192,128]{3,2,1,0:T(8,128)(2,1)S(1)} %shard_map.96), channel_id=1, source_target_pairs={{0,24},{2,26},{4,28},{6,30},{8,0},{10,2},{12,4},{14,6},{16,8},{18,... | collective-permute-start | bytes 589832 | tf_op jit(solution)/shard_map/ppermute | solution.py:243
  61.3 1.0 %copy_bitcast_fusion = bf16[192,16,128]{2,1,0:T(8,128)(2,1)} fusion(bf16[2,1536,128]{2,1,0:T(8,128)(2,1)S(1)} %get-tuple-element.120), kind=kLoop, calls=%fused_computation | loop fusion | bytes 1572864 | tf_op jit(solution)/shard_map/reshape | solution.py:361
  62.4 3.9 %collective-permute-done.16.down_ref = bf16[2,2,192,128]{3,2,1,0:T(8,128)(2,1)S(1)} collective-permute-done((bf16[2,2,192,128]{3,2,1,0:T(8,128)(2,1)S(1)}, bf16[2,2,192,128]{3,2,1,0:T(8,128)(2,1)S(1)}, u32[]{:S(2)}, u32[]{:S(2)}) %collective-permute-start.16) | collective-permute-done | bytes 196640 | tf_op jit(solution)/shard_map/ppermute | solution.py:243
  66.2 0.8 %shard_map.97 = (bf16[384,128]{1,0:T(8,128)(2,1)}, bf16[384,128]{1,0:T(8,128)(2,1)}) custom-call(s32[1]{0:T(128)} %bitcast.place_ref.refs_0_, f32[2,2,192,128]{3,2,1,0:T(8,128)S(1)} %get-tuple-element.123.mine_ref, bf16[2,2,192,128]{3,2,1,0:T(8,128)(2,1)S(1)} %get-tuple-element.124.own_ref, bf16[2,2,192,128]{3,2,1,0:T(8,128)(2,1)S(1)} %collective-permute-done.16.down_ref, ...), custom_call_target="tpu_custom_call" | custom-call | tf_op jit(solution)/shard_map/pallas_call | solution.py:249
  (16 shorter events, 0.2 us)
Async XLA Ops:
  0.6 4.2 %copy-start = (bf16[192,16,128]{2,1,0:T(8,128)(2,1)S(1)}, bf16[192,16,128]{2,1,0:T(8,128)(2,1)}, u32[]{:S(2)}) copy-start(bf16[192,16,128]{2,1,0:T(8,128)(2,1)} %param.5) | copy-start | bytes 2359300
  1.7 4.5 %copy-start.1 = (s32[8]{0:T(128)S(1)}, s32[8]{0:T(128)}, u32[]{:S(2)}) copy-start(s32[8]{0:T(128)} %lens_ref.1) | copy-start | bytes 100
  1.7 10.0 %collective-permute-start.1 = (bf16[2,2,192,128]{3,2,1,0:T(8,128)(2,1)S(1)}, bf16[2,2,192,128]{3,2,1,0:T(8,128)(2,1)S(1)}, u32[]{:S(2)}, u32[]{:S(2)}) collective-permute-start(bf16[2,2,192,128]{3,2,1,0:T(8,128)(2,1)S(1)} %shard_map.77.refs_4_.own_ref.refs_6_), channel_id=1, source_target_pairs={{0,8},{2,10},{4,12},{6,14},{8,16},{10,18},{12,20},{14,22},{16,24},... | collective-permute-start | bytes 589832 | tf_op jit(solution)/shard_map/ppermute | solution.py:243
  11.8 7.9 %collective-permute-start.4 = (bf16[2,2,192,128]{3,2,1,0:T(8,128)(2,1)S(1)}, bf16[2,2,192,128]{3,2,1,0:T(8,128)(2,1)S(1)}, u32[]{:S(2)}, u32[]{:S(2)}) collective-permute-start(bf16[2,2,192,128]{3,2,1,0:T(8,128)(2,1)S(1)} %collective-permute-done.1.refs_4_.refs_7_), channel_id=1, source_target_pairs={{0,8},{2,10},{4,12},{6,14},{8,16},{10,18},{12,20},{14,22},{16,24},... | collective-permute-start | bytes 589832 | tf_op jit(solution)/shard_map/ppermute | solution.py:243
  11.8 9.4 %collective-permute-start.2 = (bf16[2,2,192,128]{3,2,1,0:T(8,128)(2,1)S(1)}, bf16[2,2,192,128]{3,2,1,0:T(8,128)(2,1)S(1)}, u32[]{:S(2)}, u32[]{:S(2)}) collective-permute-start(bf16[2,2,192,128]{3,2,1,0:T(8,128)(2,1)S(1)} %collective-permute-done.1.refs_4_.refs_7_), channel_id=1, source_target_pairs={{0,6},{2,4},{4,2},{6,0},{8,14},{10,12},{12,10},{14,8},{16,22},{18,... | collective-permute-start | bytes 589832 | tf_op jit(solution)/shard_map/ppermute | solution.py:243
  14.2 12.0 %collective-permute-start.8 = (bf16[2,2,192,128]{3,2,1,0:T(8,128)(2,1)S(1)}, bf16[2,2,192,128]{3,2,1,0:T(8,128)(2,1)S(1)}, u32[]{:S(2)}, u32[]{:S(2)}) collective-permute-start(bf16[2,2,192,128]{3,2,1,0:T(8,128)(2,1)S(1)} %collective-permute-done.1.refs_4_.refs_7_), channel_id=1, source_target_pairs={{0,4},{2,6},{4,0},{6,2},{8,12},{10,14},{12,8},{14,10},{16,20},{18,... | collective-permute-start | bytes 589832 | tf_op jit(solution)/shard_map/ppermute | solution.py:243
  14.7 12.8 %collective-permute-start.7 = (bf16[2,2,192,128]{3,2,1,0:T(8,128)(2,1)S(1)}, bf16[2,2,192,128]{3,2,1,0:T(8,128)(2,1)S(1)}, u32[]{:S(2)}, u32[]{:S(2)}) collective-permute-start(bf16[2,2,192,128]{3,2,1,0:T(8,128)(2,1)S(1)} %collective-permute-done.1.refs_4_.refs_7_), channel_id=1, source_target_pairs={{0,2},{2,0},{4,6},{6,4},{8,10},{10,8},{12,14},{14,12},{16,18},{18,... | collective-permute-start | bytes 589832 | tf_op jit(solution)/shard_map/ppermute | solution.py:243
  15.2 18.4 %collective-permute-start = (bf16[2,2,192,128]{3,2,1,0:T(8,128)(2,1)S(1)}, bf16[2,2,192,128]{3,2,1,0:T(8,128)(2,1)S(1)}, u32[]{:S(2)}, u32[]{:S(2)}) collective-permute-start(bf16[2,2,192,128]{3,2,1,0:T(8,128)(2,1)S(1)} %shard_map.77.refs_4_.own_ref.refs_6_), channel_id=1, source_target_pairs={{0,6},{2,4},{4,2},{6,0},{8,14},{10,12},{12,10},{14,8},{16,22},{18,... | collective-permute-start | bytes 589832 | tf_op jit(solution)/shard_map/ppermute | solution.py:243
  19.7 11.6 %collective-permute-start.6 = (bf16[2,2,192,128]{3,2,1,0:T(8,128)(2,1)S(1)}, bf16[2,2,192,128]{3,2,1,0:T(8,128)(2,1)S(1)}, u32[]{:S(2)}, u32[]{:S(2)}) collective-permute-start(bf16[2,2,192,128]{3,2,1,0:T(8,128)(2,1)S(1)} %get-tuple-element.73), channel_id=1, source_target_pairs={{0,2},{2,0},{4,6},{6,4},{8,10},{10,8},{12,14},{14,12},{16,18},{18,... | collective-permute-start | bytes 589832 | tf_op jit(solution)/shard_map/ppermute | solution.py:243
  21.2 10.2 %collective-permute-start.5 = (bf16[2,2,192,128]{3,2,1,0:T(8,128)(2,1)S(1)}, bf16[2,2,192,128]{3,2,1,0:T(8,128)(2,1)S(1)}, u32[]{:S(2)}, u32[]{:S(2)}) collective-permute-start(bf16[2,2,192,128]{3,2,1,0:T(8,128)(2,1)S(1)} %get-tuple-element.72), channel_id=1, source_target_pairs={{0,4},{2,6},{4,0},{6,2},{8,12},{10,14},{12,8},{14,10},{16,20},{18,... | collective-permute-start | bytes 589832 | tf_op jit(solution)/shard_map/ppermute | solution.py:243
  26.2 7.5 %collective-permute-start.3 = (bf16[2,2,192,128]{3,2,1,0:T(8,128)(2,1)S(1)}, bf16[2,2,192,128]{3,2,1,0:T(8,128)(2,1)S(1)}, u32[]{:S(2)}, u32[]{:S(2)}) collective-permute-start(bf16[2,2,192,128]{3,2,1,0:T(8,128)(2,1)S(1)} %collective-permute-done.2.refs_4_.refs_6_), channel_id=1, source_target_pairs={{0,8},{2,10},{4,12},{6,14},{8,16},{10,18},{12,20},{14,22},{16,24},... | collective-permute-start | bytes 589832 | tf_op jit(solution)/shard_map/ppermute | solution.py:243
  34.2 28.2 %collective-permute-start.17 = (bf16[2,2,192,128]{3,2,1,0:T(8,128)(2,1)S(1)}, bf16[2,2,192,128]{3,2,1,0:T(8,128)(2,1)S(1)}, u32[]{:S(2)}, u32[]{:S(2)}) collective-permute-start(bf16[2,2,192,128]{3,2,1,0:T(8,128)(2,1)S(1)} %get-tuple-element.129), channel_id=1, source_target_pairs={{0,6},{2,4},{4,2},{6,0},{8,14},{10,12},{12,10},{14,8},{16,22},{18,... | collective-permute-start | bytes 589832 | tf_op jit(solution)/shard_map/ppermute | solution.py:243
  35.2 18.5 %collective-permute-start.13 = (bf16[2,2,192,128]{3,2,1,0:T(8,128)(2,1)S(1)}, bf16[2,2,192,128]{3,2,1,0:T(8,128)(2,1)S(1)}, u32[]{:S(2)}, u32[]{:S(2)}) collective-permute-start(bf16[2,2,192,128]{3,2,1,0:T(8,128)(2,1)S(1)} %get-tuple-element.129), channel_id=1, source_target_pairs={{0,24},{2,26},{4,28},{6,30},{8,0},{10,2},{12,4},{14,6},{16,8},{18,... | collective-permute-start | bytes 589832 | tf_op jit(solution)/shard_map/ppermute | solution.py:243
  41.4 7.1 %collective-permute-start.9 = (bf16[2,2,192,128]{3,2,1,0:T(8,128)(2,1)S(1)}, bf16[2,2,192,128]{3,2,1,0:T(8,128)(2,1)S(1)}, u32[]{:S(2)}, u32[]{:S(2)}) collective-permute-start(bf16[2,2,192,128]{3,2,1,0:T(8,128)(2,1)S(1)} %get-tuple-element.121), channel_id=1, source_target_pairs={{0,2},{2,0},{4,6},{6,4},{8,10},{10,8},{12,14},{14,12},{16,18},{18,... | collective-permute-start | bytes 589832 | tf_op jit(solution)/shard_map/ppermute | solution.py:243
  43.1 8.2 %collective-permute-start.10 = (bf16[2,2,192,128]{3,2,1,0:T(8,128)(2,1)S(1)}, bf16[2,2,192,128]{3,2,1,0:T(8,128)(2,1)S(1)}, u32[]{:S(2)}, u32[]{:S(2)}) collective-permute-start(bf16[2,2,192,128]{3,2,1,0:T(8,128)(2,1)S(1)} %get-tuple-element.122), channel_id=1, source_target_pairs={{0,4},{2,6},{4,0},{6,2},{8,12},{10,14},{12,8},{14,10},{16,20},{18,... | collective-permute-start | bytes 589832 | tf_op jit(solution)/shard_map/ppermute | solution.py:243
  47.0 10.0 %collective-permute-start.15 = (bf16[2,2,192,128]{3,2,1,0:T(8,128)(2,1)S(1)}, bf16[2,2,192,128]{3,2,1,0:T(8,128)(2,1)S(1)}, u32[]{:S(2)}, u32[]{:S(2)}) collective-permute-start(bf16[2,2,192,128]{3,2,1,0:T(8,128)(2,1)S(1)} %get-tuple-element.130), channel_id=1, source_target_pairs={{0,2},{2,0},{4,6},{6,4},{8,10},{10,8},{12,14},{14,12},{16,18},{18,... | collective-permute-start | bytes 589832 | tf_op jit(solution)/shard_map/ppermute | solution.py:243
  48.5 8.6 %collective-permute-start.12 = (bf16[2,2,192,128]{3,2,1,0:T(8,128)(2,1)S(1)}, bf16[2,2,192,128]{3,2,1,0:T(8,128)(2,1)S(1)}, u32[]{:S(2)}, u32[]{:S(2)}) collective-permute-start(bf16[2,2,192,128]{3,2,1,0:T(8,128)(2,1)S(1)} %get-tuple-element.127), channel_id=1, source_target_pairs={{0,4},{2,6},{4,0},{6,2},{8,12},{10,14},{12,8},{14,10},{16,20},{18,... | collective-permute-start | bytes 589832 | tf_op jit(solution)/shard_map/ppermute | solution.py:243
  51.5 5.7 %collective-permute-start.11 = (bf16[2,2,192,128]{3,2,1,0:T(8,128)(2,1)S(1)}, bf16[2,2,192,128]{3,2,1,0:T(8,128)(2,1)S(1)}, u32[]{:S(2)}, u32[]{:S(2)}) collective-permute-start(bf16[2,2,192,128]{3,2,1,0:T(8,128)(2,1)S(1)} %get-tuple-element.126), channel_id=1, source_target_pairs={{0,24},{2,26},{4,28},{6,30},{8,0},{10,2},{12,4},{14,6},{16,8},{18,... | collective-permute-start | bytes 589832 | tf_op jit(solution)/shard_map/ppermute | solution.py:243
  53.8 6.6 %collective-permute-start.14 = (bf16[2,2,192,128]{3,2,1,0:T(8,128)(2,1)S(1)}, bf16[2,2,192,128]{3,2,1,0:T(8,128)(2,1)S(1)}, u32[]{:S(2)}, u32[]{:S(2)}) collective-permute-start(bf16[2,2,192,128]{3,2,1,0:T(8,128)(2,1)S(1)} %shard_map.95), channel_id=1, source_target_pairs={{0,6},{2,4},{4,2},{6,0},{8,14},{10,12},{12,10},{14,8},{16,22},{18,... | collective-permute-start | bytes 589832 | tf_op jit(solution)/shard_map/ppermute | solution.py:243
  60.5 5.7 %collective-permute-start.16 = (bf16[2,2,192,128]{3,2,1,0:T(8,128)(2,1)S(1)}, bf16[2,2,192,128]{3,2,1,0:T(8,128)(2,1)S(1)}, u32[]{:S(2)}, u32[]{:S(2)}) collective-permute-start(bf16[2,2,192,128]{3,2,1,0:T(8,128)(2,1)S(1)} %shard_map.96), channel_id=1, source_target_pairs={{0,24},{2,26},{4,28},{6,30},{8,0},{10,2},{12,4},{14,6},{16,8},{18,... | collective-permute-start | bytes 589832 | tf_op jit(solution)/shard_map/ppermute | solution.py:243
